TPU v7x, 32 devices: a whole 2x2x4 slice. The times are simulated.
32 devices in a mesh: fsdp: 4 (over y, x), ctx: 2 (over core), tp: 4 (over z).
Axes of the slice: x: 2, y: 2, z: 4, core: 2. Of those that a mesh axis runs over, the one named last changes fastest.
Arguments:
- block_input: float32 [4, 1024, 2048], P('fsdp', 'ctx'), may hold values from -6 to 6
- cotangent: float32 [4, 1024, 2048], P('fsdp', 'ctx'), may hold values from -6 to 6
- w_query: bfloat16 [2048, 2048], P(('fsdp', 'ctx'), 'tp'), may hold values from -0.125 to 0.125
- w_key: bfloat16 [2048, 512], P(('fsdp', 'ctx'), 'tp'), may hold values from -0.125 to 0.125
- w_value: bfloat16 [2048, 512], P(('fsdp', 'ctx'), 'tp'), may hold values from -0.125 to 0.125
- w_output: bfloat16 [2048, 2048], P('tp', ('fsdp', 'ctx')), may hold values from -4 to 4
- w_gate: bfloat16 [2048, 8192], P(('fsdp', 'ctx'), 'tp'), may hold values from -0.125 to 0.125
- w_up: bfloat16 [2048, 8192], P(('fsdp', 'ctx'), 'tp'), may hold values from -0.125 to 0.125
- w_down: bfloat16 [8192, 2048], P('tp', ('fsdp', 'ctx')), may hold values from -0.0625 to 0.0625
- attn_gain: bfloat16 [2048], P(('fsdp', 'ctx')), may hold values from 0.5 to 1.5
- ffn_gain: bfloat16 [2048], P(('fsdp', 'ctx')), may hold values from 0.5 to 1.5
Outputs:
- block_output: float32 [4, 1024, 2048], P('fsdp', 'ctx')
- input_grad: float32 [4, 1024, 2048], P('fsdp', 'ctx')
- grad_query: float32 [2048, 2048], P(('fsdp', 'ctx'), 'tp')
- grad_key: float32 [2048, 512], P(('fsdp', 'ctx'), 'tp')
- grad_value: float32 [2048, 512], P(('fsdp', 'ctx'), 'tp')
- grad_output: float32 [2048, 2048], P('tp', ('fsdp', 'ctx'))
- grad_gate: float32 [2048, 8192], P(('fsdp', 'ctx'), 'tp')
- grad_up: float32 [2048, 8192], P(('fsdp', 'ctx'), 'tp')
- grad_down: float32 [8192, 2048], P('tp', ('fsdp', 'ctx'))
- grad_attn_gain: float32 [2048], P(('fsdp', 'ctx'))
- grad_ffn_gain: float32 [2048], P(('fsdp', 'ctx'))
All inputs are finite; a program needn't handle non-finite values.
Results may differ from a plain program's by a relative error of at most 0.013.
Values may be sent and summed in bfloat16 or wider, within the bound.
No kernel may reach another device: no remote copies, remote signals or barrier semaphores. Data moves between devices by JAX's collectives and lax.ppermute only.
A program may use at most 256 MiB of HBM per device.

v0:
```python
import jax
import jax.numpy as jnp
from jax import lax
from jax.sharding import PartitionSpec as P

HD = 64


EPS = 1e-05
BASE = 500000.0
NEG = -1e30


def shifted(shard, axis, by):
    count = lax.axis_size(axis)
    pairs = [(i, i + by) for i in range(count) if 0 <= i + by < count]
    return lax.ppermute(shard, axis, pairs)


def rotate(values, positions, sign):
    half = values.shape[-1] // 2
    inverse = BASE ** (-(jnp.arange(half, dtype=jnp.float32) * 2.0) / values.shape[-1])
    angle = positions.astype(jnp.float32)[:, None] * inverse[None, :]
    cosine = jnp.cos(angle)[:, None, :]
    sine = sign * jnp.sin(angle)[:, None, :]
    first = values[..., :half]
    second = values[..., half:]
    return jnp.concatenate(
        [first * cosine - second * sine, second * cosine + first * sine], axis=-1
    )


def norm_forward(rows, gain):
    scale = lax.rsqrt(jnp.mean(rows * rows, axis=-1, keepdims=True) + EPS)
    return (rows * scale * gain, scale)


def norm_backward(rows, scale, gain, grad):
    weighted = grad * gain
    d_rows = scale * weighted - rows * scale**3 * jnp.mean(weighted * rows, axis=-1, keepdims=True)
    return (d_rows, jnp.sum(grad * rows * scale, axis=0))


def forward_block(queries, keys, vals, allow, scale):
    scores = jnp.einsum("gbd,kd->gbk", queries, keys, preferred_element_type=jnp.float32) * scale
    scores = jnp.where(allow[None], scores, NEG)
    top = jnp.max(scores, axis=-1, keepdims=True)
    total = top[..., 0] + jnp.log(jnp.sum(jnp.exp(scores - top), axis=-1))
    probs = jnp.exp(scores - total[..., None]).astype(jnp.bfloat16)
    out = jnp.einsum("gbk,kd->gbd", probs, vals, preferred_element_type=jnp.float32)
    return (out.astype(jnp.bfloat16), total)


def backward_block(queries, keys, vals, allow, total, grad_out, out, scale):
    scores = jnp.einsum("gbd,kd->gbk", queries, keys, preferred_element_type=jnp.float32) * scale
    scores = jnp.where(allow[None], scores, NEG)
    probs = jnp.exp(scores - total[..., None])
    rounded = probs.astype(jnp.bfloat16)
    d_vals = jnp.einsum("gbk,gbd->kd", rounded, grad_out, preferred_element_type=jnp.float32)
    d_probs = jnp.einsum("gbd,kd->gbk", grad_out, vals, preferred_element_type=jnp.float32)
    delta = jnp.sum(grad_out.astype(jnp.float32) * out.astype(jnp.float32), axis=-1)
    d_scores = (probs * (d_probs - delta[..., None]) * scale).astype(jnp.bfloat16)
    d_query = jnp.einsum("gbk,kd->gbd", d_scores, keys, preferred_element_type=jnp.float32)
    d_keys = jnp.einsum("gbk,gbd->kd", d_scores, queries, preferred_element_type=jnp.float32)
    return (d_query, d_keys, d_vals)


def split_blocks(tensor, count, block):
    return tensor.reshape((tensor.shape[0], count, block) + tensor.shape[2:]).swapaxes(0, 1)


def attention_forward(grouped, keys, vals, allow, block, scale):

    def per_head(items):
        head_q, head_k, head_v = items
        groups, rows, width = head_q.shape
        count = rows // block
        outs, totals = lax.map(
            lambda piece: forward_block(piece[0], head_k, head_v, piece[1], scale),
            (split_blocks(head_q, count, block), allow.reshape(count, block, allow.shape[1])),
        )
        return (
            outs.swapaxes(0, 1).reshape(groups, rows, width),
            totals.swapaxes(0, 1).reshape(groups, rows),
        )

    return lax.map(per_head, (grouped, keys, vals))


def attention_backward(grouped, keys, vals, allow, totals, grads, outs, block, scale):

    def per_head(items):
        head_q, head_k, head_v, head_t, head_g, head_o = items
        groups, rows, width = head_q.shape
        count = rows // block

        def step(carry, piece):
            d_query, d_keys, d_vals = backward_block(
                piece[0], head_k, head_v, piece[1], piece[2], piece[3], piece[4], scale
            )
            return ((carry[0] + d_keys, carry[1] + d_vals), d_query)

        zeros = jnp.zeros(head_k.shape, jnp.float32)
        pieces = (
            split_blocks(head_q, count, block),
            allow.reshape(count, block, allow.shape[1]),
            split_blocks(head_t, count, block),
            split_blocks(head_g, count, block),
            split_blocks(head_o, count, block),
        )
        (d_keys, d_vals), d_query = lax.scan(step, (zeros, zeros), pieces)
        return (d_query.swapaxes(0, 1).reshape(groups, rows, width), d_keys, d_vals)

    return lax.map(per_head, (grouped, keys, vals, totals, grads, outs))


def dotf(left, right):
    return jnp.dot(left, right, preferred_element_type=jnp.float32)


def body(
    block_input,
    cotangent,
    w_query,
    w_key,
    w_value,
    w_output,
    w_gate,
    w_up,
    w_down,
    attn_gain,
    ffn_gain,
):
    wq, wk, wv, wo, wg, wu, wd, gain_qa, gain_qf = (
        lax.all_gather(w_query, ("fsdp", "ctx"), axis=0, tiled=True),
        lax.all_gather(w_key, ("fsdp", "ctx"), axis=0, tiled=True),
        lax.all_gather(w_value, ("fsdp", "ctx"), axis=0, tiled=True),
        lax.all_gather(w_output, ("fsdp", "ctx"), axis=1, tiled=True),
        lax.all_gather(w_gate, ("fsdp", "ctx"), axis=0, tiled=True),
        lax.all_gather(w_up, ("fsdp", "ctx"), axis=0, tiled=True),
        lax.all_gather(w_down, ("fsdp", "ctx"), axis=1, tiled=True),
        lax.all_gather(attn_gain, ("fsdp", "ctx"), axis=0, tiled=True),
        lax.all_gather(ffn_gain, ("fsdp", "ctx"), axis=0, tiled=True),
    )
    rows = block_input[0]
    cot = cotangent[0]
    local = rows.shape[0]
    block = min(512, local)
    scale = HD ** (-0.5)
    heads = wq.shape[1] // HD
    kv_heads = wk.shape[1] // HD
    groups = heads // kv_heads
    place = lax.axis_index("ctx")
    positions = place * local + jnp.arange(local, dtype=jnp.int32)
    gain_a = gain_qa.astype(jnp.float32)
    gain_f = gain_qf.astype(jnp.float32)
    normed_f, scale_a = norm_forward(rows, gain_a)
    normed = normed_f.astype(jnp.bfloat16)
    query = dotf(normed, wq).reshape(local, heads, HD)
    keys = dotf(normed, wk).reshape(local, kv_heads, HD)
    vals = dotf(normed, wv)
    query_rot = rotate(query, positions, 1.0).astype(jnp.bfloat16)
    keys_rot = rotate(keys, positions, 1.0).astype(jnp.bfloat16).reshape(local, kv_heads * HD)
    vals_b = vals.astype(jnp.bfloat16)
    keys_prev, vals_prev = shifted((keys_rot, vals_b), "ctx", 1)
    all_keys = (
        jnp.concatenate([keys_prev, keys_rot], axis=0)
        .reshape(2 * local, kv_heads, HD)
        .transpose(1, 0, 2)
    )
    all_vals = (
        jnp.concatenate([vals_prev, vals_b], axis=0)
        .reshape(2 * local, kv_heads, HD)
        .transpose(1, 0, 2)
    )
    grouped = query_rot.reshape(local, kv_heads, groups, HD).transpose(1, 2, 0, 3)
    index = jnp.arange(local, dtype=jnp.int32)
    earlier = jnp.broadcast_to(place > 0, (local, local))
    causal = index[None, :] <= index[:, None]
    allow = jnp.concatenate([earlier, causal], axis=1)
    attn, totals = attention_forward(grouped, all_keys, all_vals, allow, block, scale)
    attn_flat = attn.transpose(2, 0, 1, 3).reshape(local, heads * HD)
    hidden = rows + lax.psum(dotf(attn_flat, wo), "tp")
    hnorm_f, scale_f = norm_forward(hidden, gain_f)
    hnorm = hnorm_f.astype(jnp.bfloat16)
    gate = dotf(hnorm, wg)
    up = dotf(hnorm, wu)
    sigma = jax.nn.sigmoid(gate)
    active = gate * sigma
    inner = (active * up).astype(jnp.bfloat16)
    out = hidden + lax.psum(dotf(inner, wd).astype(jnp.bfloat16), "tp").astype(jnp.float32)
    cot_b = cot.astype(jnp.bfloat16)
    d_inner = dotf(cot_b, wd.T)
    d_gate = (d_inner * up * sigma * (1.0 + gate * (1.0 - sigma))).astype(jnp.bfloat16)
    d_up = (d_inner * active).astype(jnp.bfloat16)
    d_hnorm = lax.psum(dotf(d_gate, wg.T) + dotf(d_up, wu.T), "tp")
    d_norm, g_ffn = norm_backward(hidden, scale_f, gain_f, d_hnorm)
    d_hidden = cot + d_norm
    dh_b = d_hidden.astype(jnp.bfloat16)
    d_attn = (
        dotf(dh_b, wo.T)
        .astype(jnp.bfloat16)
        .reshape(local, kv_heads, groups, HD)
        .transpose(1, 2, 0, 3)
    )
    d_query, d_keys, d_vals = attention_backward(
        grouped, all_keys, all_vals, allow, totals, d_attn, attn, block, scale
    )
    keys_grad = d_keys.transpose(1, 0, 2).reshape(2 * local, kv_heads * HD)
    vals_grad = d_vals.transpose(1, 0, 2).reshape(2 * local, kv_heads * HD)
    keys_back, vals_back = shifted((keys_grad[:local], vals_grad[:local]), "ctx", -1)
    keys_own = keys_grad[local:] + keys_back
    vals_own = vals_grad[local:] + vals_back
    d_query = d_query.transpose(2, 0, 1, 3).reshape(local, heads, HD)
    dq_b = rotate(d_query, positions, -1.0).astype(jnp.bfloat16).reshape(local, heads * HD)
    dk_b = (
        rotate(keys_own.reshape(local, kv_heads, HD), positions, -1.0)
        .astype(jnp.bfloat16)
        .reshape(local, kv_heads * HD)
    )
    dv_b = vals_own.astype(jnp.bfloat16)
    d_normed = lax.psum(dotf(dq_b, wq.T) + dotf(dk_b, wk.T) + dotf(dv_b, wv.T), "tp")
    d_rows, g_attn = norm_backward(rows, scale_a, gain_a, d_normed)
    d_input = d_hidden + d_rows
    s_query, s_key, s_value, s_output, s_gate, s_up, s_down, s_attn, s_ffn = (
        lax.psum_scatter(dotf(normed.T, dq_b), ("fsdp", "ctx"), scatter_dimension=0, tiled=True),
        lax.psum_scatter(dotf(normed.T, dk_b), ("fsdp", "ctx"), scatter_dimension=0, tiled=True),
        lax.psum_scatter(dotf(normed.T, dv_b), ("fsdp", "ctx"), scatter_dimension=0, tiled=True),
        lax.psum_scatter(dotf(attn_flat.T, dh_b), ("fsdp", "ctx"), scatter_dimension=1, tiled=True),
        lax.psum_scatter(dotf(hnorm.T, d_gate), ("fsdp", "ctx"), scatter_dimension=0, tiled=True),
        lax.psum_scatter(dotf(hnorm.T, d_up), ("fsdp", "ctx"), scatter_dimension=0, tiled=True),
        lax.psum_scatter(dotf(inner.T, cot_b), ("fsdp", "ctx"), scatter_dimension=1, tiled=True),
        lax.psum_scatter(g_attn, ("fsdp", "ctx"), scatter_dimension=0, tiled=True),
        lax.psum_scatter(g_ffn, ("fsdp", "ctx"), scatter_dimension=0, tiled=True),
    )
    return (
        out[None],
        d_input[None],
        s_query,
        s_key,
        s_value,
        s_output,
        s_gate,
        s_up,
        s_down,
        s_attn,
        s_ffn,
    )


def solution(mesh):
    placed = (
        P("fsdp", "ctx", None),
        P("fsdp", "ctx", None),
        P(("fsdp", "ctx"), "tp"),
        P(("fsdp", "ctx"), "tp"),
        P(("fsdp", "ctx"), "tp"),
        P("tp", ("fsdp", "ctx")),
        P(("fsdp", "ctx"), "tp"),
        P(("fsdp", "ctx"), "tp"),
        P("tp", ("fsdp", "ctx")),
        P(("fsdp", "ctx")),
        P(("fsdp", "ctx")),
    )
    return jax.shard_map(
        body,
        mesh=mesh,
        in_specs=placed,
        out_specs=(
            P("fsdp", "ctx", None),
            P("fsdp", "ctx", None),
            P(("fsdp", "ctx"), "tp"),
            P(("fsdp", "ctx"), "tp"),
            P(("fsdp", "ctx"), "tp"),
            P("tp", ("fsdp", "ctx")),
            P(("fsdp", "ctx"), "tp"),
            P(("fsdp", "ctx"), "tp"),
            P("tp", ("fsdp", "ctx")),
            P(("fsdp", "ctx")),
            P(("fsdp", "ctx")),
        ),
        check_vma=False,
    )
```

profile of v0, /device:TPU:0, one launch (start us, length us, event | category | flops | bytes accessed | tf_op | source)
XLA Modules:
  0.0 1437.5 jit_solution(5688634115593749319)
XLA Ops:
  8.6 10.4 all-gather
  19.0 10.7 all_gather.29
  30.0 3.0 fusion.52
  36.5 2.9 collective-permute-start
  39.4 8.9 all_gather.30
  51.5 2.9 collective-permute-start.1
  59.2 3.9 copy.28
  63.2 2.9 fusion.65
  66.3 12.7 while.10
  79.0 4.0 all-gather.10.cloned.1.call-done
  83.0 4.9 fusion.86
  89.7 9.1 all-gather.1
  98.8 144.2 %all-reduce.9.cloned.1.call-done = f32[512,2048]{1,0:T(8,128)} async-done(((f32[512,2048]{1,0:T(8,128)}), f32[512,2048]{1,0:T(8,128)}) %all-reduce.9.cloned.1.call-update) | async-done | bytes 4194320 | tf_op jit(solution)/shard_map/psum | solution.py:183
  243.0 4.0 multiply_reduce_fusion.2
  250.8 47.2 %all-gather.12.cloned.1.call-done = bf16[2048,2048]{1,0:T(8,128)(2,1)} async-done(((bf16[256,2048]{1,0:T(8,128)(2,1)}), bf16[2048,2048]{1,0:T(8,128)(2,1)}) %all-gather.12.cloned.1.call-update) | async-done | bytes 8388624 | tf_op jit(solution)/shard_map/all_gather | solution.py:139
  298.0 10.5 fusion.87
  308.6 45.5 %all-gather.14.cloned.1.call-done = bf16[2048,2048]{1,0:T(8,128)(2,1)} async-done(((bf16[256,2048]{1,0:T(8,128)(2,1)}), bf16[2048,2048]{1,0:T(8,128)(2,1)}) %all-gather.14.cloned.1.call-update) | async-done | bytes 8388624 | tf_op jit(solution)/shard_map/all_gather | solution.py:140
  354.1 10.5 fusion.88
  364.6 47.1 %all-gather.16.cloned.1.call-done = bf16[2048,2048]{1,0:T(8,128)(2,1)} async-done(((bf16[2048,256]{1,0:T(8,128)(2,1)}), bf16[2048,2048]{1,0:T(8,128)(2,1)}) %all-gather.16.cloned.1.call-update) | async-done | bytes 8388624 | tf_op jit(solution)/shard_map/all_gather | solution.py:141
  411.7 15.3 %multiply_convert_fusion.1 = (bf16[512,2048]{1,0:T(8,128)(2,1)S(1)}, bf16[512,2048]{1,0:T(8,128)(2,1)}, bf16[512,2048]{1,0:T(8,128)(2,1)}) fusion(f32[512,2048]{1,0:T(8,128)} %fusion.87, f32[512,2048]{1,0:T(8,128)} %fusion.88, bf16[2048,2048]{1,0:T(8,128)(2,1)} %all-gather.16.cloned.1.call-done, f32[1,512,2048]{2,1,0:T(8,128)} %param.16), kind=kOutput, calls=%fused_computation.79 | convolution fusion | flops 4310695936 | bytes 27262976 | tf_op jit(solution)/shard_map/dot_general | solution.py:118
  427.0 8.4 fusion.89
  435.4 6.1 convolution_add_fusion
  441.6 9.8 convolution_convert_fusion
  451.7 145.0 %all-reduce.13.cloned.1.call-done = f32[512,2048]{1,0:T(8,128)} async-done(((f32[512,2048]{1,0:T(8,128)}), f32[512,2048]{1,0:T(8,128)}) %all-reduce.13.cloned.1.call-update) | async-done | bytes 4194320 | tf_op jit(solution)/shard_map/psum | solution.py:196
  596.7 4.5 multiply_reduce_fusion
  601.2 83.0 %all-reduce.11.cloned.1.call-done = bf16[512,2048]{1,0:T(8,128)(2,1)} async-done(((bf16[512,2048]{1,0:T(8,128)(2,1)}), bf16[512,2048]{1,0:T(8,128)(2,1)}) %all-reduce.11.cloned.1.call-update) | async-done | bytes 2097168 | tf_op jit(solution)/shard_map/psum | solution.py:191
  684.2 8.1 bitcast_add_fusion
  695.6 20.4 %while.27 = (s32[]{:T(128)}, f32[2,4,512,64]{2,3,1,0:T(8,128)}, f32[2,1024,64]{1,2,0:T(8,128)S(1)}, f32[2,1024,64]{1,2,0:T(8,128)}, pred[512,1024]{1,0:T(8,128)(...) while((s32[]{:T(128)}, f32[2,4,512,64]{2,3,1,0:T(8,128)}, ...), condition=%wide.region_12.13_spmd, body=%wide.region_10.12_spmd.sunk | while | flops 1365768192 | bytes 50255028 | solution.py:114
  697.1 3.3 multiply_convert_fusion.7
  702.8 3.1 fusion.170
  707.3 3.3 multiply_convert_fusion.7
  713.0 3.1 fusion.170
  726.8 3.5 fusion.92
  732.2 5.7 fusion.73
  738.0 3.3 fusion.69
  742.9 9.7 fusion.93
  752.7 9.9 fusion.94
  764.1 10.4 fusion.82
  776.4 105.3 %all-reduce.15.cloned.1.call-done = f32[512,2048]{1,0:T(8,128)} async-done(((f32[512,2048]{1,0:T(8,128)}), f32[512,2048]{1,0:T(8,128)}) %all-reduce.15.cloned.1.call-update) | async-done | bytes 4194320 | tf_op jit(solution)/shard_map/psum | solution.py:222
  881.7 4.5 fusion.61
  886.2 24.1 %all-reduce.3 = (f32[2048]{0:T(1024)S(1)}, f32[2048]{0:T(1024)S(1)}) all-reduce(f32[2048]{0:T(1024)S(1)} %get-tuple-element.169, f32[2048]{0:T(1024)S(1)} %get-tuple-element.167), channel_id=9, replica_groups=mesh['fsdp'=4,'ctx'=2,'tp'=4] {'fsdp','ctx'}, use_global_device_ids=true, to_apply=%region_23.24.clone | all-reduce | flops 4096 | bytes 32768
  911.6 7.8 fusion.58
  920.3 39.8 %reduce-scatter.10.cloned.1.call-done = f32[256,128]{1,0:T(8,128)} async-done(((f32[2048,128]{1,0:T(8,128)}), f32[256,128]{1,0:T(8,128)}) %reduce-scatter.10.cloned.1.call-update) | async-done | bytes 131088 | tf_op jit(solution)/shard_map/reduce_scatter | solution.py:227
  960.1 54.9 %reduce-scatter.14.cloned.1.call-done = f32[512,256]{1,0:T(8,128)} async-done(((f32[512,2048]{1,0:T(8,128)}), f32[512,256]{1,0:T(8,128)}) %reduce-scatter.14.cloned.1.call-update) | async-done | bytes 524304 | tf_op jit(solution)/shard_map/reduce_scatter | solution.py:229
  1015.0 55.1 %reduce-scatter.8.cloned.1.call-done = f32[256,512]{1,0:T(8,128)} async-done(((f32[2048,512]{1,0:T(8,128)}), f32[256,512]{1,0:T(8,128)}) %reduce-scatter.8.cloned.1.call-update) | async-done | bytes 524304 | tf_op jit(solution)/shard_map/reduce_scatter | solution.py:226
  1070.1 120.2 %reduce-scatter.16.cloned.1.call-done = f32[256,2048]{1,0:T(8,128)} async-done(((f32[2048,2048]{1,0:T(8,128)}), f32[256,2048]{1,0:T(8,128)}) %reduce-scatter.16.cloned.1.call-update) | async-done | bytes 2097168 | tf_op jit(solution)/shard_map/reduce_scatter | solution.py:230
  1190.3 120.2 %reduce-scatter.18.cloned.1.call-done = f32[256,2048]{1,0:T(8,128)} async-done(((f32[2048,2048]{1,0:T(8,128)}), f32[256,2048]{1,0:T(8,128)}) %reduce-scatter.18.cloned.1.call-update) | async-done | bytes 2097168 | tf_op jit(solution)/shard_map/reduce_scatter | solution.py:231
  1310.5 120.0 %reduce-scatter.20.cloned.1.call-done = f32[2048,256]{1,0:T(8,128)} async-done(((f32[2048,2048]{1,0:T(8,128)}), f32[2048,256]{1,0:T(8,128)}) %reduce-scatter.20.cloned.1.call-update) | async-done | bytes 2097168 | tf_op jit(solution)/shard_map/reduce_scatter | solution.py:232
  (173 shorter events, 61.7 us)
Async XLA Ops:
  7.2 52.1 %all-gather.8.cloned.1.call-start = ((), (), s32[]{:S(2)}) async-start(), calls=%async_computation.7 | async-start | bytes 2359296 | tf_op jit(solution)/shard_map/all_gather | solution.py:135
  7.9 75.1 %all-gather.10.cloned.1.call-start = ((), (), s32[]{:S(2)}) async-start(), calls=%async_computation.8 | async-start | bytes 2359296 | tf_op jit(solution)/shard_map/all_gather | solution.py:138
  19.0 29.3 %copy-start.20 = (f32[8,1,256]{2,1,0:T(1,128)}, f32[8,1,256]{2,1,0:T(1,128)S(1)}, u32[]{:S(2)}) copy-start(f32[8,1,256]{2,1,0:T(1,128)S(1)} %convert_element_type.149) | copy-start | bytes 24580
  29.7 4.8 copy-start.7
  29.9 4.6 copy-start
  33.5 14.8 %copy-start.23 = (f32[512]{0:T(512)}, f32[512]{0:T(512)S(1)}, u32[]{:S(2)}) copy-start(f32[512]{0:T(512)S(1)} %get-tuple-element.236) | copy-start | bytes 6148
  34.5 31.6 %copy-start.13 = (f32[512,32]{0,1:T(8,128)}, f32[512,32]{0,1:T(8,128)S(1)}, u32[]{:S(2)}) copy-start(f32[512,32]{0,1:T(8,128)S(1)} %get-tuple-element.234) | copy-start | bytes 196612
  34.5 4.9 copy-start.22
  34.9 28.2 %copy-start.2 = (bf16[1,512,2048]{2,1,0:T(8,128)(2,1)}, bf16[1,512,2048]{2,1,0:T(8,128)(2,1)S(1)}, u32[]{:S(2)}) copy-start(bf16[1,512,2048]{2,1,0:T(8,128)(2,1)S(1)} %multiply_convert_fusion.5) | copy-start | bytes 6291460
  36.5 18.2 %collective-permute-start = (bf16[512,128]{0,1:T(8,128)(2,1)}, bf16[512,128]{0,1:T(8,128)(2,1)}, u32[]{:S(2)}, u32[]{:S(2)}) collective-permute-start(bf16[512,128]{0,1:T(8,128)(2,1)} %bitcast.31), channel_id=1, source_target_pairs={{0,4},{1,5},{2,6},{3,7},{8,12},{9,13},{10,14},{11,15},{16,20},{17,... | collective-permute-start | bytes 393224 | tf_op jit(solution)/shard_map/ppermute | solution.py:17
  48.3 3.2 copy-start.9
  51.5 4.2 collective-permute-start.1
  54.5 188.6 %all-reduce.9.cloned.1.call-start = ((), (), s32[]{:S(2)}) async-start(), calls=%async_computation.9 | async-start | bytes 8388608 | tf_op jit(solution)/shard_map/psum | solution.py:183
  67.9 2.4 copy-start.18
  74.3 2.4 copy-start.18
  87.9 1.8 copy-start.27
  87.9 210.1 %all-gather.12.cloned.1.call-start = ((), (), s32[]{:S(2)}) async-start(), calls=%async_computation.10 | async-start | bytes 9437184 | tf_op jit(solution)/shard_map/all_gather | solution.py:139
  88.5 265.6 %all-gather.14.cloned.1.call-start = ((), (), s32[]{:S(2)}) async-start(), calls=%async_computation.11 | async-start | bytes 9437184 | tf_op jit(solution)/shard_map/all_gather | solution.py:140
  89.1 322.6 %all-gather.16.cloned.1.call-start = ((), (), s32[]{:S(2)}) async-start(), calls=%async_computation.12 | async-start | bytes 9437184 | tf_op jit(solution)/shard_map/all_gather | solution.py:141
  89.7 507.0 %all-reduce.13.cloned.1.call-start = ((), (), s32[]{:S(2)}) async-start(), calls=%async_computation.14 | async-start | bytes 8388608 | tf_op jit(solution)/shard_map/psum | solution.py:196
  247.0 2.0 copy-start.1
  426.9 8.4 copy-start.30
  426.9 8.4 copy-start.26
  441.6 242.6 %all-reduce.11.cloned.1.call-start = ((), (), s32[]{:S(2)}) async-start(), calls=%async_computation.13 | async-start | bytes 4194304 | tf_op jit(solution)/shard_map/psum | solution.py:191
  451.4 430.3 %all-reduce.15.cloned.1.call-start = ((), (), s32[]{:S(2)}) async-start(), calls=%async_computation.15 | async-start | bytes 8388608 | tf_op jit(solution)/shard_map/psum | solution.py:222
  684.2 10.1 copy-start.12
  692.3 2.0 copy-start.4
  692.3 3.3 copy-start.19
  695.6 24.5 %copy-start.14 = (f32[512,32]{0,1:T(8,128)S(1)}, f32[512,32]{0,1:T(8,128)}, u32[]{:S(2)}) copy-start(f32[512,32]{0,1:T(8,128)} %copy-done.13) | copy-start | bytes 196612
  695.6 24.5 %copy-start.17 = (f32[512,32]{0,1:T(8,128)S(1)}, f32[512,32]{0,1:T(8,128)}, u32[]{:S(2)}) copy-start(f32[512,32]{0,1:T(8,128)} %get-tuple-element.232) | copy-start | bytes 196612
  697.0 3.3 copy-start.15
  707.3 3.3 copy-start.15
  716.1 5.5 copy-start.6
  717.3 6.5 collective-permute-start.3
  718.6 4.3 collective-permute-start.2
  726.8 3.6 copy-start.3
  726.8 193.6 %reduce-scatter.12.cloned.1.call-start = ((), (), s32[]{:S(2)}) async-start(), calls=%async_computation.18 | async-start | bytes 1179648 | tf_op jit(solution)/shard_map/reduce_scatter | solution.py:228
  730.3 229.8 %reduce-scatter.10.cloned.1.call-start = ((), (), s32[]{:S(2)}) async-start(), calls=%async_computation.17 | async-start | bytes 1179648 | tf_op jit(solution)/shard_map/reduce_scatter | solution.py:227
  732.2 282.8 %reduce-scatter.14.cloned.1.call-start = ((), (), s32[]{:S(2)}) async-start(), calls=%async_computation.19 | async-start | bytes 4718592 | tf_op jit(solution)/shard_map/reduce_scatter | solution.py:229
  737.9 332.2 %reduce-scatter.8.cloned.1.call-start = ((), (), s32[]{:S(2)}) async-start(), calls=%async_computation.16 | async-start | bytes 4718592 | tf_op jit(solution)/shard_map/reduce_scatter | solution.py:226
  741.3 1.6 copy-start.11
  741.3 449.0 %reduce-scatter.16.cloned.1.call-start = ((), (), s32[]{:S(2)}) async-start(), calls=%async_computation.20 | async-start | bytes 18874368 | tf_op jit(solution)/shard_map/reduce_scatter | solution.py:230
  752.6 557.9 %reduce-scatter.18.cloned.1.call-start = ((), (), s32[]{:S(2)}) async-start(), calls=%async_computation.21 | async-start | bytes 18874368 | tf_op jit(solution)/shard_map/reduce_scatter | solution.py:231
  762.6 1.6 copy-start.29
  762.6 668.0 %reduce-scatter.20.cloned.1.call-start = ((), (), s32[]{:S(2)}) async-start(), calls=%async_computation.22 | async-start | bytes 18874368 | tf_op jit(solution)/shard_map/reduce_scatter | solution.py:232
  774.5 107.2 %copy-start.21 = (f32[8,1,256]{2,1,0:T(1,128)S(1)}, f32[8,1,256]{2,1,0:T(1,128)}, u32[]{:S(2)}) copy-start(f32[8,1,256]{2,1,0:T(1,128)} %copy-done.20) | copy-start | bytes 24580
  774.6 107.2 %copy-start.24 = (f32[512]{0:T(512)S(1)}, f32[512]{0:T(512)}, u32[]{:S(2)}) copy-start(f32[512]{0:T(512)} %copy-done.23) | copy-start | bytes 6148
  776.4 135.1 %copy-start.25 = (f32[512]{0:T(512)S(1)}, f32[512]{0:T(512)}, u32[]{:S(2)}) copy-start(f32[512]{0:T(512)} %get-tuple-element.235) | copy-start | bytes 6148
  (6 other events, 6.5 us)
Sparse Core Ops, SparseCore 0:
  9.9 31.1 all-gather.7
  54.6 28.3 all-gather.9
  88.0 154.9 all-reduce.8
  244.8 53.2 all-gather.11
  299.8 54.2 all-gather.13
  355.8 55.8 all-gather.15
  441.7 154.9 all-reduce.12
  599.0 85.0 all-reduce.10
  726.9 154.7 all-reduce.14
  885.3 34.9 reduce-scatter.11
  924.1 35.9 reduce-scatter.9
  963.9 51.0 reduce-scatter.13
  1018.9 51.1 reduce-scatter.7
  1074.1 116.1 reduce-scatter.15
  1194.3 116.1 reduce-scatter.17
  1314.5 115.9 reduce-scatter.19
where the time goes:
time: 1450 us; the launch traced here: 1440 us
  waiting for transfers between devices  1130 us (78%)
  matrix products  149 us (10%)
  blocking collectives  63.1 us (4%)
  other arithmetic  46.2 us (3%)
  local copies, waits for them, and re-layouts  19 us (1%)
  between operations  15.6 us (1%)
    psum x1, waiting for transfers between devices, body(): d_hnorm = lax.psum(dotf(d_gate, wg.T) + dotf(d_up, wu.T), 'tp')  145 us
    psum x1, waiting for transfers between devices, body(): hidden = rows + lax.psum(dotf(attn_flat, wo), 'tp')  144 us
    dot_general x21, matrix products, dotf(): return jnp.dot(left, right, preferred_element_type=jnp.float32)  121 us
    reduce_scatter x1, waiting for transfers between devices, body(): lax.psum_scatter(dotf(hnorm.T, d_gate), ('fsdp', 'ctx'), scatter_dimensio...  120 us
    reduce_scatter x1, waiting for transfers between devices, body(): lax.psum_scatter(dotf(hnorm.T, d_up), ('fsdp', 'ctx'), scatter_dimension=...  120 us
    reduce_scatter x1, waiting for transfers between devices, body(): lax.psum_scatter(dotf(inner.T, cot_b), ('fsdp', 'ctx'), scatter_dimension...  120 us
    psum x1, waiting for transfers between devices, body(): lax.psum(dotf(dq_b, wq.T) + dotf(dk_b, wk.T) + dotf(dv_b, wv.T), 'tp')  105 us
    psum x1, waiting for transfers between devices, body(): lax.psum(dotf(inner, wd).astype(jnp.bfloat16), 'tp').astype(jnp.float32)  83 us
  transfers between devices with their start and end apart: 20, of which 15 were waited for; matrix products, arithmetic and copies ran while one was open for 9% of the time, Pallas kernels for 0%

commit v1 on v0

v1 whole, which is shorter than its diff:
```python
import jax
import jax.numpy as jnp
from jax import lax
from jax.experimental import pallas as pl
from jax.experimental.pallas import tpu as pltpu
from jax.sharding import PartitionSpec as P

HD = 64
EPS = 1e-05
BASE = 500000.0
NEG = -1e30
BF = jnp.bfloat16
F32 = jnp.float32
BLOCK = 256


def dotf(left, right):
    return jnp.dot(left, right, preferred_element_type=F32)


def dot_t(left, right):
    return lax.dot_general(left, right, (((1,), (1,)), ((), ())), preferred_element_type=F32)


def dot_0(left, right):
    return lax.dot_general(left, right, (((0,), (0,)), ((), ())), preferred_element_type=F32)


def after(value, *others):
    return lax.optimization_barrier((value,) + others)[0]


def swap(value):
    return lax.ppermute(value, "ctx", [(0, 1), (1, 0)])


def pair(mine, theirs, core, axis):
    first = jnp.where(core == 0, mine, theirs)
    second = jnp.where(core == 0, theirs, mine)
    return jnp.concatenate([first, second], axis=axis)


def half_of(value, which, axis):
    size = value.shape[axis] // 2
    return lax.dynamic_slice_in_dim(value, which * size, size, axis)


def rotations(count):
    return [[(k, (k + s) % count) for k in range(count)] for s in range(1, count)]


def gather_tokens(piece):
    count = lax.axis_size("tp")
    return [piece] + [lax.ppermute(piece, "tp", pairs) for pairs in rotations(count)]


def scatter_tokens(pieces):
    count = lax.axis_size("tp")
    total = pieces[0].astype(F32)
    got = [
        lax.ppermute(pieces[(count - s) % count].astype(BF), "tp", pairs)
        for s, pairs in enumerate(rotations(count), 1)
    ]
    for item in got:
        total = total + item.astype(F32)
    return total


def to_rotated(rows, place, count):
    size = rows.shape[0] // count
    return [
        lax.dynamic_slice_in_dim(rows, ((place - s) % count) * size, size, 0) for s in range(count)
    ]


def from_rotated(pieces, place):
    count = len(pieces)
    stacked = jnp.concatenate(pieces, axis=0)
    size = pieces[0].shape[0]
    return jnp.concatenate(
        [
            lax.dynamic_slice_in_dim(stacked, ((place - j) % count) * size, size, 0)
            for j in range(count)
        ],
        axis=0,
    )


def gather_fsdp(shard):
    count = lax.axis_size("fsdp")
    if count != 4:
        return lax.all_gather(shard, "fsdp", axis=0, tiled=True)
    me = lax.axis_index("fsdp")
    near = [(k, k ^ 1) for k in range(4)]
    far = [(k, k ^ 2) for k in range(4)]
    size = shard.shape[0]
    cut = size // 32 * 16
    one = lax.ppermute(shard, "fsdp", near)
    two = lax.ppermute(shard, "fsdp", far)
    three_a = lax.ppermute(one[:cut], "fsdp", far)
    three_b = lax.ppermute(two[cut:], "fsdp", near)
    three = jnp.concatenate([three_a, three_b], axis=0)
    low = (me & 1) == 0
    high = (me & 2) == 0
    a, b = jnp.where(low, shard, one), jnp.where(low, one, shard)
    c, d = jnp.where(low, two, three), jnp.where(low, three, two)
    return jnp.concatenate(
        [jnp.where(high, a, c), jnp.where(high, b, d), jnp.where(high, c, a), jnp.where(high, d, b)],
        axis=0,
    )


def sum_everywhere(value):
    for pairs in rotations(lax.axis_size("tp")):
        pass
    got = [lax.ppermute(value, "tp", pairs) for pairs in rotations(lax.axis_size("tp"))]
    for item in got:
        value = value + item
    value = value + swap(value)
    count = lax.axis_size("fsdp")
    step = 1
    while step < count:
        value = value + lax.ppermute(value, "fsdp", [(k, k ^ step) for k in range(count)])
        step *= 2
    return value


def halves_swapped(tile):
    lane = lax.broadcasted_iota(jnp.int32, tile.shape, 1)
    width = tile.shape[1]
    back = pltpu.roll(tile, width - HD // 2, 1)
    ahead = pltpu.roll(tile, HD // 2, 1)
    return jnp.where(lane % HD < HD // 2, back, ahead)


def padded(kv):
    lane = lax.broadcasted_iota(jnp.int32, kv.shape, 1)
    low = lane < HD
    other = pltpu.roll(kv, HD, 1)
    zero = jnp.zeros_like(kv)
    keys = (jnp.where(low, kv, zero), jnp.where(low, zero, other))
    vals = (jnp.where(low, other, zero), jnp.where(low, zero, kv))
    return keys, vals


def attend_kernel(qkv_ref, cos_ref, sin_ref, cos_kv_ref, sin_kv_ref, q_ref, kv_ref, out_ref, lse_ref):
    tokens, width = out_ref.shape
    scale = HD ** (-0.5)
    tiles = width // 128
    for j in range(tiles):
        tile = qkv_ref[:, j * 128 : (j + 1) * 128]
        turned = tile * cos_ref[...] + halves_swapped(tile) * sin_ref[...]
        q_ref[:, j * 128 : (j + 1) * 128] = turned.astype(BF)
    tile = qkv_ref[:, width : width + 128]
    kv = tile * cos_kv_ref[...] + halves_swapped(tile) * sin_kv_ref[...]
    kv_ref[...] = kv.astype(BF)
    keys, vals = padded(kv)
    keys = [k.astype(BF) for k in keys]
    vals = [v.astype(BF) for v in vals]
    row = lax.broadcasted_iota(jnp.int32, (BLOCK, BLOCK), 0)
    col = lax.broadcasted_iota(jnp.int32, (BLOCK, BLOCK), 1)
    causal = col <= row
    for i in range(tokens // BLOCK):
        at = slice(i * BLOCK, (i + 1) * BLOCK)
        for j in range(tiles):
            queries = q_ref[at, j * 128 : (j + 1) * 128]
            result = None
            for side in range(2):
                key, val = keys[side], vals[side]
                diag = dot_t(queries, key[at]) * scale
                diag = jnp.where(causal, diag, NEG)
                top = jnp.max(diag, axis=-1, keepdims=True)
                if i:
                    past = dot_t(queries, key[: i * BLOCK]) * scale
                    top = jnp.maximum(top, jnp.max(past, axis=-1, keepdims=True))
                    weight = jnp.exp(past - top)
                p_diag = jnp.exp(diag - top)
                total = jnp.sum(p_diag, axis=-1, keepdims=True)
                if i:
                    total = total + jnp.sum(weight, axis=-1, keepdims=True)
                inverse = 1.0 / total
                part = dotf((p_diag * inverse).astype(BF), val[at])
                if i:
                    part = part + dotf((weight * inverse).astype(BF), val[: i * BLOCK])
                result = part if result is None else result + part
                head = 2 * j + side
                lse_ref[at, head : head + 1] = top + jnp.log(total)
            out_ref[at, j * 128 : (j + 1) * 128] = result.astype(BF)


def attend(qkv, tables):
    tokens, width = qkv.shape
    width = width - 2 * HD
    return pl.pallas_call(
        attend_kernel,
        out_shape=(
            jax.ShapeDtypeStruct((tokens, width), BF),
            jax.ShapeDtypeStruct((tokens, 2 * HD), BF),
            jax.ShapeDtypeStruct((tokens, width), BF),
            jax.ShapeDtypeStruct((tokens, width // HD), F32),
        ),
        name="attend",
    )(qkv, *tables)


def attend_back_kernel(
    q_ref, kv_ref, out_ref, grad_ref, lse_ref, cos_ref, sin_ref, cos_kv_ref, sin_kv_ref, d_ref, dk_ref, dv_ref
):
    tokens, width = out_ref.shape
    scale = HD ** (-0.5)
    tiles = width // 128
    keys, vals = padded(kv_ref[...].astype(F32))
    keys = [k.astype(BF) for k in keys]
    vals = [v.astype(BF) for v in vals]
    row = lax.broadcasted_iota(jnp.int32, (BLOCK, BLOCK), 0)
    col = lax.broadcasted_iota(jnp.int32, (BLOCK, BLOCK), 1)
    causal = col <= row
    low = lax.broadcasted_iota(jnp.int32, (BLOCK, 128), 1) < HD
    dk_ref[...] = jnp.zeros_like(dk_ref)
    dv_ref[...] = jnp.zeros_like(dv_ref)
    for i in range(tokens // BLOCK):
        at = slice(i * BLOCK, (i + 1) * BLOCK)
        for j in range(tiles):
            lanes = slice(j * 128, (j + 1) * 128)
            queries = q_ref[at, lanes]
            grads = grad_ref[at, lanes]
            product = grads.astype(F32) * out_ref[at, lanes].astype(F32)
            d_query = None
            for side in range(2):
                key, val = keys[side], vals[side]
                head = 2 * j + side
                lse = lse_ref[at, head : head + 1]
                mine = low if side == 0 else jnp.logical_not(low)
                delta = jnp.sum(jnp.where(mine, product, 0.0), axis=-1, keepdims=True)
                spans = [(at, True)]
                if i:
                    spans.append((slice(0, i * BLOCK), False))
                for span, masked in spans:
                    scores = dot_t(queries, key[span]) * scale
                    if masked:
                        scores = jnp.where(causal, scores, NEG)
                    probs = jnp.exp(scores - lse)
                    d_probs = dot_t(grads, val[span])
                    d_scores = (probs * (d_probs - delta) * scale).astype(BF)
                    dv_ref[side, span] += dot_0(probs.astype(BF), grads)
                    dk_ref[side, span] += dot_0(d_scores, queries)
                    part = dotf(d_scores, key[span])
                    d_query = part if d_query is None else d_query + part
            turned = d_query * cos_ref[at] - halves_swapped(d_query) * sin_ref[at]
            d_ref[at, lanes] = turned.astype(BF)
    full = lax.broadcasted_iota(jnp.int32, (tokens, 128), 1) < HD
    d_key = dk_ref[0] + pltpu.roll(dk_ref[1], HD, 1)
    d_val = dv_ref[1] + pltpu.roll(dv_ref[0], HD, 1)
    tile = jnp.where(full, d_key, d_val)
    turned = tile * cos_kv_ref[...] - halves_swapped(tile) * sin_kv_ref[...]
    d_ref[:, width : width + 128] = turned.astype(BF)


def attend_back(queries, kv, out, grads, lse, tables):
    tokens, width = queries.shape
    return pl.pallas_call(
        attend_back_kernel,
        out_shape=jax.ShapeDtypeStruct((tokens, width + 2 * HD), BF),
        scratch_shapes=[pltpu.VMEM((2, tokens, 128), F32), pltpu.VMEM((2, tokens, 128), F32)],
        name="attend_back",
    )(queries, kv, out, grads, lse, *tables)


def rotary_tables(tokens):
    inverse = BASE ** (-(jnp.arange(HD // 2, dtype=F32) * 2.0) / HD)
    angle = jnp.arange(tokens, dtype=jnp.int32).astype(F32)[:, None] * inverse[None, :]
    cosine, sine = jnp.cos(angle), jnp.sin(angle)
    one, zero = jnp.ones((tokens, HD), F32), jnp.zeros((tokens, HD), F32)
    head_cos = jnp.concatenate([cosine, cosine], axis=1)
    head_sin = jnp.concatenate([-sine, sine], axis=1)
    return (
        jnp.concatenate([head_cos, head_cos], axis=1),
        jnp.concatenate([head_sin, head_sin], axis=1),
        jnp.concatenate([head_cos, one], axis=1),
        jnp.concatenate([head_sin, zero], axis=1),
    )


def inverse_rms(rows):
    return lax.rsqrt(jnp.mean(rows * rows, axis=-1, keepdims=True) + EPS)


def norm_backward(rows, scale, gain, grad):
    weighted = grad * gain
    d_rows = scale * weighted - rows * scale**3 * jnp.mean(weighted * rows, axis=-1, keepdims=True)
    return (d_rows, jnp.sum(grad * rows * scale, axis=0))


def body(
    block_input, cotangent, w_query, w_key, w_value, w_output, w_gate, w_up, w_down, attn_gain, ffn_gain
):
    core = lax.axis_index("ctx")
    place = lax.axis_index("tp")
    slot = lax.axis_index("fsdp")
    count = lax.axis_size("tp")
    both = ("fsdp", "ctx")
    rows = block_input[0]
    cot = cotangent[0]
    local, width = rows.shape
    shard = w_query.shape[0]
    other = 1 - core

    gains = jnp.concatenate([attn_gain, ffn_gain])
    narrow = (w_query.shape[1] + 2 * w_key.shape[1]) // 2
    lines = -(-gains.shape[0] // (16 * narrow)) * 16
    gain_rows = jnp.pad(gains, (0, lines * narrow - gains.shape[0])).reshape(lines, narrow)

    def packed(which):
        return jnp.concatenate(
            [
                jnp.concatenate([half_of(w, which, 1) for w in (w_query, w_key, w_value)], axis=1),
                gain_rows,
            ],
            axis=0,
        )

    qkv_mine = packed(core)
    qkv_theirs = swap(packed(other))
    qkv_shard = pair(qkv_mine, qkv_theirs, core, 0)
    qkv_all = gather_fsdp(qkv_shard)
    qkv_all = qkv_all.reshape(-1, shard + lines, narrow)
    w_qkv = qkv_all[:, :shard].reshape(-1, narrow)
    gain_all = qkv_all[:, shard:].reshape(-1, lines * narrow)[:, : 2 * shard]
    gain_a = gain_all[:, :shard].reshape(-1).astype(F32)
    gain_f = gain_all[:, shard:].reshape(-1).astype(F32)

    wo = lax.all_gather(w_output, both, axis=1, tiled=True)

    def split_cols(w):
        return pair(half_of(w, core, 1), swap(half_of(w, other, 1)), core, 0)

    wg = lax.all_gather(split_cols(w_gate), "fsdp", axis=0, tiled=True)
    wu = lax.all_gather(split_cols(w_up), "fsdp", axis=0, tiled=True)
    wd_shard = pair(half_of(w_down, core, 0), swap(half_of(w_down, other, 0)), core, 1)
    wd = lax.all_gather(wd_shard, "fsdp", axis=1, tiled=True)

    rows_full = pair(rows, swap(rows), core, 0)
    normed = (rows_full * inverse_rms(rows_full) * gain_a).astype(BF)
    tables = rotary_tables(2 * local)
    qkv = dotf(normed, w_qkv)
    queries, kv, attn, lse = attend(qkv, tables)
    attn_own = pair(half_of(attn, core, 0), swap(half_of(attn, other, 0)), core, 1)
    attn_rot = jnp.concatenate(to_rotated(attn_own, place, count), axis=0)

    piece = local // count

    def pieces_of(value):
        return [value[s * piece : (s + 1) * piece] for s in range(count)]

    mine = place * piece
    rows_piece = lax.dynamic_slice_in_dim(rows, mine, piece, 0)
    cot_piece = lax.dynamic_slice_in_dim(cot, mine, piece, 0)
    scale_a = inverse_rms(rows_piece)

    hidden = rows_piece + scatter_tokens(pieces_of(dotf(attn_rot, wo)))
    scale_f = inverse_rms(hidden)
    hnorm_piece = (hidden * scale_f * gain_f).astype(BF)
    hnorm_own = jnp.concatenate(gather_tokens(hnorm_piece), axis=0)
    hnorm = jnp.concatenate([hnorm_own, swap(hnorm_own)], axis=0)

    cot_own = jnp.concatenate(to_rotated(cot.astype(BF), place, count), axis=0)
    cot_b = jnp.concatenate([cot_own, swap(cot_own)], axis=0)

    gate = dotf(hnorm, wg)
    up = dotf(hnorm, wu)
    sigma = jax.nn.sigmoid(gate)
    active = gate * sigma
    inner = (active * up).astype(BF)
    d_inner = dot_t(cot_b, wd)
    d_gate = (d_inner * up * sigma * (1.0 + gate * (1.0 - sigma))).astype(BF)
    d_up = (d_inner * active).astype(BF)

    def over_cores(value):
        return value[:local] + swap(value[local:].astype(BF)).astype(F32)

    d_hnorm = scatter_tokens(pieces_of(over_cores(dot_t(d_gate, wg) + dot_t(d_up, wu))))
    d_norm, g_ffn = norm_backward(hidden, scale_f, gain_f, d_hnorm)
    d_hidden = cot_piece + d_norm
    dh_piece = d_hidden.astype(BF)
    dh_own = jnp.concatenate(gather_tokens(dh_piece), axis=0)

    down = over_cores(dotf(inner, wd))
    out_piece = hidden + scatter_tokens(pieces_of(down))
    out = from_rotated(gather_tokens(out_piece.astype(BF)), place).astype(F32)

    def give_cols(grad):
        other_cols = swap(half_of(grad, other, 0))
        return pair(half_of(grad, core, 0), other_cols, core, 1).astype(F32)

    def reduced(grad, axis):
        return lax.psum_scatter(grad.astype(BF), "fsdp", scatter_dimension=axis, tiled=True)

    part = reduced(dot_0(inner, cot_b), 1)
    s_down = pair(half_of(part, core, 1), swap(half_of(part, other, 1)), core, 0).astype(F32)
    s_gate = give_cols(reduced(dot_0(hnorm, d_gate), 0))
    s_up = give_cols(reduced(dot_0(hnorm, d_up), 0))

    s_output = lax.psum_scatter(
        dot_0(attn_rot, dh_own).astype(BF), both, scatter_dimension=1, tiled=True
    ).astype(F32)
    d_attn_own = from_rotated(pieces_of(dot_t(dh_own, wo).astype(BF)), place)
    d_attn = pair(half_of(d_attn_own, core, 1), swap(half_of(d_attn_own, other, 1)), core, 0)
    d_qkv = attend_back(queries, kv, attn, d_attn, lse, tables)

    d_qkv_rot = jnp.concatenate(
        to_rotated(half_of(d_qkv, core, 0), place, count)
        + to_rotated(half_of(d_qkv, other, 0), place, count),
        axis=0,
    )
    d_normed = scatter_tokens(pieces_of(over_cores(dot_t(d_qkv_rot, w_qkv))))
    d_rows, g_attn = norm_backward(rows_piece, scale_a, gain_a, d_normed)
    d_input = from_rotated(gather_tokens((d_hidden + d_rows).astype(BF)), place).astype(F32)

    part = reduced(dot_0(normed, d_qkv), 0)
    got = swap(half_of(part, other, 0))
    kept = half_of(part, core, 0)
    bounds = [0, w_query.shape[1] // 2, (w_query.shape[1] + w_key.shape[1]) // 2, narrow]
    s_query, s_key, s_value = [
        pair(kept[:, a:b], got[:, a:b], core, 1).astype(F32) for a, b in zip(bounds, bounds[1:])
    ]

    g_all = sum_everywhere(jnp.stack([g_attn, g_ffn]))
    start = (slot * 2 + core) * shard
    s_attn = lax.dynamic_slice_in_dim(g_all[0], start, shard, 0)
    s_ffn = lax.dynamic_slice_in_dim(g_all[1], start, shard, 0)
    return (
        out[None],
        d_input[None],
        s_query,
        s_key,
        s_value,
        s_output,
        s_gate,
        s_up,
        s_down,
        s_attn,
        s_ffn,
    )


def solution(mesh):
    placed = (
        P("fsdp", "ctx", None),
        P("fsdp", "ctx", None),
        P(("fsdp", "ctx"), "tp"),
        P(("fsdp", "ctx"), "tp"),
        P(("fsdp", "ctx"), "tp"),
        P("tp", ("fsdp", "ctx")),
        P(("fsdp", "ctx"), "tp"),
        P(("fsdp", "ctx"), "tp"),
        P("tp", ("fsdp", "ctx")),
        P(("fsdp", "ctx")),
        P(("fsdp", "ctx")),
    )
    return jax.shard_map(
        body,
        mesh=mesh,
        in_specs=placed,
        out_specs=(
            P("fsdp", "ctx", None),
            P("fsdp", "ctx", None),
            P(("fsdp", "ctx"), "tp"),
            P(("fsdp", "ctx"), "tp"),
            P(("fsdp", "ctx"), "tp"),
            P("tp", ("fsdp", "ctx")),
            P(("fsdp", "ctx"), "tp"),
            P(("fsdp", "ctx"), "tp"),
            P("tp", ("fsdp", "ctx")),
            P(("fsdp", "ctx")),
            P(("fsdp", "ctx")),
        ),
        check_vma=False,
    )
```

time: 1450 us -> 672 us (0.46)
  waiting for transfers between devices: 1130 us -> 284 us
  starting transfers between devices: 9.73 us -> 120 us
  blocking collectives: 63.1 us -> 0 us
  matrix products: 149 us -> 98 us
  local copies, waits for them, and re-layouts: 19 us -> 54.4 us
  Pallas kernels: 0 us -> 26.5 us
  other arithmetic: 46.2 us -> 65.9 us
    reduce_scatter x7 -> x5, waiting for transfers between devices: 511 us -> 0.01 us  [the longest x4 0.01 us: reduced(): lax.psum_scatter(grad.astype(BF), 'fsdp', scatter_dimension=axis, tiled=T...]
    psum x4 -> x0, waiting for transfers between devices: 477 us -> none  [the longest x1 145 us: body(): d_hnorm = lax.psum(dotf(d_gate, wg.T) + dotf(d_up, wu.T), 'tp')]
    ppermute x4 -> x50, waiting for transfers between devices: 0.01 us -> 283 us  [the longest x12 144 us: scatter_tokens(): lax.ppermute(pieces[(count - s) % count].astype(BF), 'tp', pairs)]
    all_gather x5 -> x4, waiting for transfers between devices: 144 us -> 0.03 us  [the longest x1 0.02 us: body(): wo = lax.all_gather(w_output, both, axis=1, tiled=True)]
    ppermute x4 -> x50, starting transfers between devices: 8.65 us -> 120 us  [the longest x12 47 us: scatter_tokens(): lax.ppermute(pieces[(count - s) % count].astype(BF), 'tp', pairs)]
    dot_general x35 -> x15, matrix products: 149 us -> 98 us  [the longest x5 35 us: dotf(): return jnp.dot(left, right, preferred_element_type=F32)]
    all_gather x4 -> x0, blocking collectives: 39.1 us -> none  [the longest x1 10.7 us: body(): lax.all_gather(w_key, ('fsdp', 'ctx'), axis=0, tiled=True)]
    pallas_call x0 -> x2, Pallas kernels: none -> 26.5 us  [the longest x1 15.6 us: attend_back(): pl.pallas_call(attend_back_kernel, out_shape=jax.ShapeDtypeStruct((tokens...]
  transfers between devices with their start and end apart: 20 -> 59, of which waited for: 15 -> 20; matrix products, arithmetic and copies ran while one was open for 9% -> 26% of each run, Pallas kernels for 0% -> 4%
where the time goes in v1:
time: 672 us; the launch traced here: 665 us
  waiting for transfers between devices  284 us (42%)
  starting transfers between devices  120 us (18%)
  matrix products  98 us (15%)
  other arithmetic  65.9 us (10%)
  local copies, waits for them, and re-layouts  54.4 us (8%)
  Pallas kernels  26.5 us (4%)
  between operations  15.1 us (2%)
    ppermute x12, waiting for transfers between devices, scatter_tokens(): lax.ppermute(pieces[(count - s) % count].astype(BF), 'tp', pairs)  144 us
    ppermute x12, waiting for transfers between devices, gather_tokens(): lax.ppermute(piece, 'tp', pairs)  116 us
    ppermute x12, starting transfers between devices, scatter_tokens(): lax.ppermute(pieces[(count - s) % count].astype(BF), 'tp', pairs)  47 us
    ppermute x3, starting transfers between devices, sum_everywhere(): lax.ppermute(value, 'tp', pairs)  43.5 us
    dot_general x5, matrix products, dotf(): return jnp.dot(left, right, preferred_element_type=F32)  35 us
    dot_general x5, matrix products, dot_0(): lax.dot_general(left, right, (((0,), (0,)), ((), ())), preferred_element_...  33.8 us
    dot_general x5, matrix products, dot_t(): lax.dot_general(left, right, (((1,), (1,)), ((), ())), preferred_element_...  29.2 us
    unnamed x117, local copies, waits for them, and re-layouts  28.7 us
  transfers between devices with their start and end apart: 59, of which 20 were waited for; matrix products, arithmetic and copies ran while one was open for 26% of the time, Pallas kernels for 4%

profile of v1, /device:TPU:0, one launch (start us, length us, event | category | flops | bytes accessed | tf_op | source)
XLA Modules:
  0.0 664.6 jit_solution(6370033337323720761)
XLA Ops:
  19.3 2.6 convert_element_type.215
  29.7 2.9 collective-permute-start.2
  36.6 11.2 %collective-permute-done.2 = bf16[544,384]{1,0:T(8,128)(2,1)S(1)} collective-permute-done((bf16[544,384]{1,0:T(8,128)(2,1)S(1)}, bf16[544,384]{1,0:T(8,128)(2,1)S(1)}, u32[]{:S(2)}, u32[]{:S(2)}) %collective-permute-start.2) | collective-permute-done | bytes 417824 | tf_op jit(solution)/shard_map/ppermute | solution.py:98
  52.4 3.5 collective-permute-done.4
  61.8 3.4 broadcast_select_fusion.1
  67.1 3.5 fusion.47.qkv_ref
  70.6 10.9 %attend.1 = (bf16[1024,256]{1,0:T(8,128)(2,1)}, bf16[1024,128]{1,0:T(8,128)(2,1)}, bf16[1024,256]{1,0:T(8,128)(2,1)}, f32[1024,4]{1,0:T(8,128)}) custom-call(f32[1024,384]{1,0:T(8,128)} %fusion.47.qkv_ref, f32[1024,128]{1,0:T(8,128)} %get-tuple-element.109.cos_ref, f32[1024,128]{1,0:T(8,128)} %get-tuple-element.89.sin_ref, ...), custom_call_target="tpu_custom_call" | custom-call | tf_op jit(solution)/shard_map/attend/pallas_call | solution.py:194
  85.5 4.9 fusion.46
  91.5 3.4 collective-permute-start.9
  97.9 9.8 %collective-permute-done.9 = bf16[128,2048]{1,0:T(8,128)(2,1)} collective-permute-done((bf16[128,2048]{1,0:T(8,128)(2,1)}, bf16[128,2048]{1,0:T(8,128)(2,1)}, u32[]{:S(2)}, u32[]{:S(2)}) %collective-permute-start.9) | collective-permute-done | bytes 524320 | tf_op jit(solution)/shard_map/ppermute | solution.py:61
  107.6 33.2 %collective-permute-done.8 = bf16[128,2048]{1,0:T(8,128)(2,1)} collective-permute-done((bf16[128,2048]{1,0:T(8,128)(2,1)}, bf16[128,2048]{1,0:T(8,128)(2,1)}, u32[]{:S(2)}, u32[]{:S(2)}) %collective-permute-start.8) | collective-permute-done | bytes 524320 | tf_op jit(solution)/shard_map/ppermute | solution.py:61
  140.8 3.0 multiply_reduce_fusion.3
  148.0 3.4 collective-permute-start.12
  151.4 10.6 %collective-permute-done.10 = bf16[128,2048]{1,0:T(8,128)(2,1)S(1)} collective-permute-done((bf16[128,2048]{1,0:T(8,128)(2,1)S(1)}, bf16[128,2048]{1,0:T(8,128)(2,1)S(1)}, u32[]{:S(2)}, u32[]{:S(2)}) %collective-permute-start.10) | collective-permute-done | bytes 524320 | tf_op jit(solution)/shard_map/ppermute | solution.py:54
  162.0 21.2 %collective-permute-done.11 = bf16[128,2048]{1,0:T(8,128)(2,1)S(1)} collective-permute-done((bf16[128,2048]{1,0:T(8,128)(2,1)S(1)}, bf16[128,2048]{1,0:T(8,128)(2,1)S(1)}, u32[]{:S(2)}, u32[]{:S(2)}) %collective-permute-start.11) | collective-permute-done | bytes 524320 | tf_op jit(solution)/shard_map/ppermute | solution.py:54
  184.8 3.5 constant_dynamic-update-slice_fusion.7
  190.9 10.0 %fusion.50 = f32[1024,1024]{1,0:T(8,128)} fusion(bf16[1024,2048]{1,0:T(8,128)(2,1)} %constant_dynamic-update-slice_fusion.7, bf16[1024,2048]{1,0:T(8,128)(2,1)} %all-gather.11.cloned.1.call-done), kind=kOutput, calls=%fused_computation.219 | convolution fusion | flops 4294967296 | bytes 12582912 | tf_op jit(solution)/shard_map/dot_general | solution.py:22
  200.9 3.2 constant_dynamic-update-slice_fusion.2
  204.1 10.0 %fusion.48 = f32[1024,1024]{1,0:T(8,128)} fusion(bf16[1024,2048]{1,0:T(8,128)(2,1)} %constant_dynamic-update-slice_fusion.2, bf16[2048,1024]{1,0:T(8,128)(2,1)} %all-gather.9.cloned.1.call-done), kind=kOutput, calls=%fused_computation.217 | convolution fusion | flops 4294967296 | bytes 12582912 | tf_op jit(solution)/shard_map/dot_general | solution.py:18
  214.1 12.2 %multiply_convert_fusion.2 = (bf16[1024,1024]{1,0:T(8,128)(2,1)S(1)}, bf16[1024,1024]{1,0:T(8,128)(2,1)S(1)}, bf16[1024,1024]{1,0:T(8,128)(2,1)S(1)}) fusion(f32[1024,1024]{1,0:T(8,128)} %fusion.50, f32[1024,1024]{1,0:T(8,128)} %fusion.48, bf16[1024,2048]{1,0:T(8,128)(2,1)} %constant_dynamic-update-slice_fusion.2, ...), kind=kOutput, calls=%fused_computation.10 | convolution fusion | flops 4310695936 | bytes 23068672 | tf_op jit(solution)/shard_map/dot_general | solution.py:18
  226.3 7.0 %fusion.51 = f32[1024,2048]{1,0:T(8,128)} fusion(bf16[1024,1024]{1,0:T(8,128)(2,1)S(1)} %get-tuple-element.46, bf16[2048,1024]{1,0:T(8,128)(2,1)S(1)} %copy-done.38), kind=kOutput, calls=%fused_computation.220 | convolution fusion | flops 4294967296 | bytes 14680064 | tf_op jit(solution)/shard_map/dot_general | solution.py:22
  233.4 7.0 %convolution_add_fusion = f32[1024,2048]{1,0:T(8,128)S(1)} fusion(f32[1024,2048]{1,0:T(8,128)} %fusion.51, bf16[1024,1024]{1,0:T(8,128)(2,1)S(1)} %get-tuple-element.45, bf16[2048,1024]{1,0:T(8,128)(2,1)S(1)} %copy-done.39), kind=kOutput, calls=%fused_computation.14 | convolution fusion | flops 4297064448 | bytes 23068672 | tf_op jit(solution)/shard_map/dot_general | solution.py:22
  242.5 4.5 fusion.49
  247.8 2.7 fusion.38
  250.7 12.4 %collective-permute-start.28 = (bf16[128,2048]{1,0:T(8,128)(2,1)S(1)}, bf16[128,2048]{1,0:T(8,128)(2,1)S(1)}, u32[]{:S(2)}, u32[]{:S(2)}) collective-permute-start(bf16[128,2048]{1,0:T(8,128)(2,1)S(1)} %get-tuple-element.59), channel_id=1, source_target_pairs={{0,3},{1,0},{2,1},{3,2},{4,7},{5,4},{6,5},{7,6},{8,11},{9,8},{10,9... | collective-permute-start | bytes 1572872 | tf_op jit(solution)/shard_map/ppermute | solution.py:61
  265.0 3.2 collective-permute-start.20
  269.4 6.2 collective-permute-done.28
  275.5 23.1 %collective-permute-start.18 = (bf16[128,2048]{1,0:T(8,128)(2,1)S(1)}, bf16[128,2048]{1,0:T(8,128)(2,1)S(1)}, u32[]{:S(2)}, u32[]{:S(2)}) collective-permute-start(bf16[128,2048]{1,0:T(8,128)(2,1)S(1)} %get-tuple-element.65), channel_id=1, source_target_pairs={{0,1},{1,2},{2,3},{3,0},{4,5},{5,6},{6,7},{7,4},{8,9},{9,10},{10,1... | collective-permute-start | bytes 1572872 | tf_op jit(solution)/shard_map/ppermute | solution.py:61
  298.6 33.3 %collective-permute-done.27 = bf16[128,2048]{1,0:T(8,128)(2,1)S(1)} collective-permute-done((bf16[128,2048]{1,0:T(8,128)(2,1)S(1)}, bf16[128,2048]{1,0:T(8,128)(2,1)S(1)}, u32[]{:S(2)}, u32[]{:S(2)}) %collective-permute-start.27) | collective-permute-done | bytes 524320 | tf_op jit(solution)/shard_map/ppermute | solution.py:61
  333.2 20.3 %collective-permute-done.19 = bf16[128,2048]{1,0:T(8,128)(2,1)S(1)} collective-permute-done((bf16[128,2048]{1,0:T(8,128)(2,1)S(1)}, bf16[128,2048]{1,0:T(8,128)(2,1)S(1)}, u32[]{:S(2)}, u32[]{:S(2)}) %collective-permute-start.19) | collective-permute-done | bytes 524320 | tf_op jit(solution)/shard_map/ppermute | solution.py:61
  360.4 9.3 %collective-permute-done.31 = bf16[128,2048]{1,0:T(8,128)(2,1)S(1)} collective-permute-done((bf16[128,2048]{1,0:T(8,128)(2,1)S(1)}, bf16[128,2048]{1,0:T(8,128)(2,1)S(1)}, u32[]{:S(2)}, u32[]{:S(2)}) %collective-permute-start.31) | collective-permute-done | bytes 524320 | tf_op jit(solution)/shard_map/ppermute | solution.py:54
  369.7 33.7 %collective-permute-done.30 = bf16[128,2048]{1,0:T(8,128)(2,1)S(1)} collective-permute-done((bf16[128,2048]{1,0:T(8,128)(2,1)S(1)}, bf16[128,2048]{1,0:T(8,128)(2,1)S(1)}, u32[]{:S(2)}, u32[]{:S(2)}) %collective-permute-start.30) | collective-permute-done | bytes 524320 | tf_op jit(solution)/shard_map/ppermute | solution.py:54
  405.0 2.6 convolution_convert_fusion.3
  407.9 2.8 convolution_convert_fusion.5
  413.5 15.6 %attend_back.1 = bf16[1024,384]{1,0:T(8,128)(2,1)} custom-call(bf16[1024,256]{1,0:T(8,128)(2,1)} %get-tuple-element.16.q_ref, bf16[1024,128]{1,0:T(8,128)(2,1)} %get-tuple-element.17.kv_ref, bf16[1024,256]{1,0:T(8,128)(2,1)} %get-tuple-element.15.out_ref, bf16[1024,256]{1,0:T(8,128)(2,1)} %pad_maximum_fusion.16.grad_ref, ...), custom_call_target="tpu_custom_call" | custom-call | tf_op jit(solution)/shard_map/attend_back/pallas_call | solution.py:261
  429.1 6.1 convolution_convert_fusion.4
  435.3 8.4 %convolution_convert_fusion.1 = bf16[2048,1024]{1,0:T(8,128)(2,1)} fusion(bf16[1024,2048]{1,0:T(8,128)(2,1)} %constant_dynamic-update-slice_fusion.2, bf16[1024,1024]{1,0:T(8,128)(2,1)S(1)} %copy-done.48), kind=kOutput, calls=%fused_computation.16 | convolution fusion | flops 4297064448 | bytes 10485760 | tf_op jit(solution)/shard_map/dot_general | solution.py:26
  445.3 8.4 %convolution_convert_fusion.2 = bf16[2048,1024]{1,0:T(8,128)(2,1)} fusion(bf16[1024,2048]{1,0:T(8,128)(2,1)} %constant_dynamic-update-slice_fusion.2, bf16[1024,1024]{1,0:T(8,128)(2,1)S(1)} %copy-done.46), kind=kOutput, calls=%fused_computation.17 | convolution fusion | flops 4297064448 | bytes 10485760 | tf_op jit(solution)/shard_map/dot_general | solution.py:26
  464.4 3.3 copy-done
  469.3 8.3 %convolution_convert_fusion = bf16[1024,2048]{1,0:T(8,128)(2,1)} fusion(bf16[1024,1024]{1,0:T(8,128)(2,1)S(1)} %copy-done.44, bf16[1024,2048]{1,0:T(8,128)(2,1)} %constant_dynamic-update-slice_fusion.7), kind=kOutput, calls=%fused_computation.15 | convolution fusion | flops 4297064448 | bytes 10485760 | tf_op jit(solution)/shard_map/dot_general | solution.py:26
  477.6 3.7 fusion.35
  486.7 11.0 %collective-permute-done.36 = bf16[128,2048]{1,0:T(8,128)(2,1)S(1)} collective-permute-done((bf16[128,2048]{1,0:T(8,128)(2,1)S(1)}, bf16[128,2048]{1,0:T(8,128)(2,1)S(1)}, u32[]{:S(2)}, u32[]{:S(2)}) %collective-permute-start.36) | collective-permute-done | bytes 524320 | tf_op jit(solution)/shard_map/ppermute | solution.py:61
  497.7 30.0 %collective-permute-done.35 = bf16[128,2048]{1,0:T(8,128)(2,1)S(1)} collective-permute-done((bf16[128,2048]{1,0:T(8,128)(2,1)S(1)}, bf16[128,2048]{1,0:T(8,128)(2,1)S(1)}, u32[]{:S(2)}, u32[]{:S(2)}) %collective-permute-start.35) | collective-permute-done | bytes 524320 | tf_op jit(solution)/shard_map/ppermute | solution.py:61
  530.4 25.6 %collective-permute-start.45 = (f32[2,2048]{1,0:T(2,128)S(1)}, f32[2,2048]{1,0:T(2,128)S(1)}, u32[]{:S(2)}, u32[]{:S(2)}) collective-permute-start(f32[2,2048]{1,0:T(2,128)S(1)} %pad_maximum_fusion.24), channel_id=1, source_target_pairs={{0,2},{1,3},{2,0},{3,1},{4,6},{5,7},{6,4},{7,5},{8,10},{9,11},{10,... | collective-permute-start | bytes 49160 | tf_op jit(solution)/shard_map/ppermute | solution.py:116
  556.0 17.9 %collective-permute-start.44 = (f32[2,2048]{1,0:T(2,128)S(1)}, f32[2,2048]{1,0:T(2,128)S(1)}, u32[]{:S(2)}, u32[]{:S(2)}) collective-permute-start(f32[2,2048]{1,0:T(2,128)S(1)} %pad_maximum_fusion.24), channel_id=1, source_target_pairs={{0,1},{1,2},{2,3},{3,0},{4,5},{5,6},{6,7},{7,4},{8,9},{9,10},{10,1... | collective-permute-start | bytes 49160 | tf_op jit(solution)/shard_map/ppermute | solution.py:116
  579.5 3.5 collective-permute-done.48
  593.5 7.1 %collective-permute-done.39 = bf16[128,2048]{1,0:T(8,128)(2,1)S(1)} collective-permute-done((bf16[128,2048]{1,0:T(8,128)(2,1)}, bf16[128,2048]{1,0:T(8,128)(2,1)S(1)}, u32[]{:S(2)}, u32[]{:S(2)}) %collective-permute-start.39) | collective-permute-done | bytes 524320 | tf_op jit(solution)/shard_map/ppermute | solution.py:54
  600.7 34.2 %collective-permute-done.38 = bf16[128,2048]{1,0:T(8,128)(2,1)S(1)} collective-permute-done((bf16[128,2048]{1,0:T(8,128)(2,1)}, bf16[128,2048]{1,0:T(8,128)(2,1)S(1)}, u32[]{:S(2)}, u32[]{:S(2)}) %collective-permute-start.38) | collective-permute-done | bytes 524320 | tf_op jit(solution)/shard_map/ppermute | solution.py:54
  (310 shorter events, 132.0 us)
Async XLA Ops:
  7.2 78.2 %all-gather.5.cloned.1.call-start = ((), (), s32[]{:S(2)}) async-start(), calls=%async_computation.5 | async-start | bytes 2359296 | tf_op jit(solution)/shard_map/all_gather | solution.py:332
  7.9 182.9 %all-gather.11.cloned.1.call-start = ((), (), s32[]{:S(2)}) async-start(), calls=%async_computation.8 | async-start | bytes 5242880 | tf_op jit(solution)/shard_map/all_gather | solution.py:340
  13.6 190.5 %all-gather.9.cloned.1.call-start = ((), (), s32[]{:S(2)}) async-start(), calls=%async_computation.7 | async-start | bytes 5242880 | tf_op jit(solution)/shard_map/all_gather | solution.py:338
  13.6 46.4 %collective-permute-start = (f32[512,2048]{1,0:T(8,128)}, f32[512,2048]{1,0:T(8,128)}, u32[]{:S(2)}, u32[]{:S(2)}) collective-permute-start(f32[512,2048]{1,0:T(8,128)} %bitcast.98), channel_id=1, source_target_pairs={{0,4},{4,0},{1,5},{5,1},{2,6},{6,2},{3,7},{7,3},{8,12},{12,8},{9,1... | collective-permute-start | bytes 12582920 | tf_op jit(solution)/shard_map/ppermute | solution.py:34
  16.8 12.7 %collective-permute-start.1 = (bf16[272,384]{1,0:T(8,128)(2,1)}, bf16[272,384]{1,0:T(8,128)(2,1)S(1)}, u32[]{:S(2)}, u32[]{:S(2)}) collective-permute-start(bf16[272,384]{1,0:T(8,128)(2,1)} %pad_maximum_fusion.20), channel_id=1, source_target_pairs={{0,4},{4,0},{1,5},{5,1},{2,6},{6,2},{3,7},{7,3},{8,12},{12,8},{9,1... | collective-permute-start | bytes 626696 | tf_op jit(solution)/shard_map/ppermute | solution.py:34
  18.0 64.6 %collective-permute-start.14 = (bf16[256,1024]{1,0:T(8,128)(2,1)}, bf16[256,1024]{1,0:T(8,128)(2,1)}, u32[]{:S(2)}, u32[]{:S(2)}) collective-permute-start(bf16[256,1024]{1,0:T(8,128)(2,1)} %constant_dynamic-slice_fusion.13), channel_id=1, source_target_pairs={{0,4},{4,0},{1,5},{5,1},{2,6},{6,2},{3,7},{7,3},{8,12},{12,8},{9,1... | collective-permute-start | bytes 1572872 | tf_op jit(solution)/shard_map/ppermute | solution.py:34
  24.4 189.7 %all-gather.7.cloned.1.call-start = ((), (), s32[]{:S(2)}) async-start(), calls=%async_computation.6 | async-start | bytes 5242880 | tf_op jit(solution)/shard_map/all_gather | solution.py:337
  29.7 18.1 %collective-permute-start.2 = (bf16[544,384]{1,0:T(8,128)(2,1)S(1)}, bf16[544,384]{1,0:T(8,128)(2,1)S(1)}, u32[]{:S(2)}, u32[]{:S(2)}) collective-permute-start(bf16[544,384]{1,0:T(8,128)(2,1)S(1)} %pad_maximum_fusion.17), channel_id=1, source_target_pairs={{0,8},{8,0},{16,24},{24,16},{1,9},{9,1},{17,25},{25,17},{2,10},{10... | collective-permute-start | bytes 1253384 | tf_op jit(solution)/shard_map/ppermute | solution.py:98
  32.6 17.5 %collective-permute-start.3 = (bf16[544,384]{1,0:T(8,128)(2,1)S(1)}, bf16[544,384]{1,0:T(8,128)(2,1)S(1)}, u32[]{:S(2)}, u32[]{:S(2)}) collective-permute-start(bf16[544,384]{1,0:T(8,128)(2,1)S(1)} %pad_maximum_fusion.17), channel_id=1, source_target_pairs={{0,16},{8,24},{16,0},{24,8},{1,17},{9,25},{17,1},{25,9},{2,18},{10... | collective-permute-start | bytes 1253384 | tf_op jit(solution)/shard_map/ppermute | solution.py:99
  48.5 7.4 %collective-permute-start.4 = (bf16[272,384]{1,0:T(8,128)(2,1)}, bf16[272,384]{1,0:T(8,128)(2,1)}, u32[]{:S(2)}, u32[]{:S(2)}) collective-permute-start(bf16[272,384]{1,0:T(8,128)(2,1)} %slice.167), channel_id=1, source_target_pairs={{0,16},{8,24},{16,0},{24,8},{1,17},{9,25},{17,1},{25,9},{2,18},{10... | collective-permute-start | bytes 626696 | tf_op jit(solution)/shard_map/ppermute | solution.py:100
  85.1 505.6 %reduce-scatter.8.cloned.1.call-start = ((), (), s32[]{:S(2)}) async-start(), calls=%async_computation.10 | async-start | bytes 2359296 | tf_op jit(solution)/shard_map/reduce_scatter | solution.py:403
  91.5 16.1 %collective-permute-start.9 = (bf16[128,2048]{1,0:T(8,128)(2,1)}, bf16[128,2048]{1,0:T(8,128)(2,1)}, u32[]{:S(2)}, u32[]{:S(2)}) collective-permute-start(bf16[128,2048]{1,0:T(8,128)(2,1)} %get-tuple-element.69), channel_id=1, source_target_pairs={{0,3},{1,0},{2,1},{3,2},{4,7},{5,4},{6,5},{7,6},{8,11},{9,8},{10,9... | collective-permute-start | bytes 1572872 | tf_op jit(solution)/shard_map/ppermute | solution.py:61
  94.9 45.9 %collective-permute-start.8 = (bf16[128,2048]{1,0:T(8,128)(2,1)}, bf16[128,2048]{1,0:T(8,128)(2,1)}, u32[]{:S(2)}, u32[]{:S(2)}) collective-permute-start(bf16[128,2048]{1,0:T(8,128)(2,1)} %get-tuple-element.70), channel_id=1, source_target_pairs={{0,2},{1,3},{2,0},{3,1},{4,6},{5,7},{6,4},{7,5},{8,10},{9,11},{10,... | collective-permute-start | bytes 1572872 | tf_op jit(solution)/shard_map/ppermute | solution.py:61
  94.9 45.9 %collective-permute-start.7 = (bf16[128,2048]{1,0:T(8,128)(2,1)}, bf16[128,2048]{1,0:T(8,128)(2,1)}, u32[]{:S(2)}, u32[]{:S(2)}) collective-permute-start(bf16[128,2048]{1,0:T(8,128)(2,1)} %get-tuple-element.68), channel_id=1, source_target_pairs={{0,1},{1,2},{2,3},{3,0},{4,5},{5,6},{6,7},{7,4},{8,9},{9,10},{10,1... | collective-permute-start | bytes 1572872 | tf_op jit(solution)/shard_map/ppermute | solution.py:61
  97.1 87.7 %collective-permute-start.24 = (bf16[512,2048]{1,0:T(8,128)(2,1)S(1)}, bf16[512,2048]{1,0:T(8,128)(2,1)}, u32[]{:S(2)}, u32[]{:S(2)}) collective-permute-start(bf16[512,2048]{1,0:T(8,128)(2,1)S(1)} %pad_maximum_fusion.3), channel_id=1, source_target_pairs={{0,4},{4,0},{1,5},{5,1},{2,6},{6,2},{3,7},{7,3},{8,12},{12,8},{9,1... | collective-permute-start | bytes 6291464 | tf_op jit(solution)/shard_map/ppermute | solution.py:34
  145.3 16.7 %collective-permute-start.10 = (bf16[128,2048]{1,0:T(8,128)(2,1)S(1)}, bf16[128,2048]{1,0:T(8,128)(2,1)S(1)}, u32[]{:S(2)}, u32[]{:S(2)}) collective-permute-start(bf16[128,2048]{1,0:T(8,128)(2,1)S(1)} %get-tuple-element.42), channel_id=1, source_target_pairs={{0,1},{1,2},{2,3},{3,0},{4,5},{5,6},{6,7},{7,4},{8,9},{9,10},{10,1... | collective-permute-start | bytes 1572872 | tf_op jit(solution)/shard_map/ppermute | solution.py:54
  146.1 37.1 %collective-permute-start.11 = (bf16[128,2048]{1,0:T(8,128)(2,1)S(1)}, bf16[128,2048]{1,0:T(8,128)(2,1)S(1)}, u32[]{:S(2)}, u32[]{:S(2)}) collective-permute-start(bf16[128,2048]{1,0:T(8,128)(2,1)S(1)} %get-tuple-element.42), channel_id=1, source_target_pairs={{0,2},{1,3},{2,0},{3,1},{4,6},{5,7},{6,4},{7,5},{8,10},{9,11},{10,... | collective-permute-start | bytes 1572872 | tf_op jit(solution)/shard_map/ppermute | solution.py:54
  148.0 35.2 %collective-permute-start.12 = (bf16[128,2048]{1,0:T(8,128)(2,1)S(1)}, bf16[128,2048]{1,0:T(8,128)(2,1)S(1)}, u32[]{:S(2)}, u32[]{:S(2)}) collective-permute-start(bf16[128,2048]{1,0:T(8,128)(2,1)S(1)} %get-tuple-element.42), channel_id=1, source_target_pairs={{0,3},{1,0},{2,1},{3,2},{4,7},{5,4},{6,5},{7,6},{8,11},{9,8},{10,9... | collective-permute-start | bytes 1572872 | tf_op jit(solution)/shard_map/ppermute | solution.py:54
  184.8 16.1 %collective-permute-start.13 = (bf16[512,2048]{1,0:T(8,128)(2,1)}, bf16[512,2048]{1,0:T(8,128)(2,1)}, u32[]{:S(2)}, u32[]{:S(2)}) collective-permute-start(bf16[512,2048]{1,0:T(8,128)(2,1)} %pad_maximum_fusion.1), channel_id=1, source_target_pairs={{0,4},{4,0},{1,5},{5,1},{2,6},{6,2},{3,7},{7,3},{8,12},{12,8},{9,1... | collective-permute-start | bytes 6291464 | tf_op jit(solution)/shard_map/ppermute | solution.py:34
  247.4 16.4 %collective-permute-start.17 = (bf16[512,2048]{1,0:T(8,128)(2,1)S(1)}, bf16[512,2048]{1,0:T(8,128)(2,1)S(1)}, u32[]{:S(2)}, u32[]{:S(2)}) collective-permute-start(bf16[512,2048]{1,0:T(8,128)(2,1)S(1)} %slice.243), channel_id=1, source_target_pairs={{0,4},{4,0},{1,5},{5,1},{2,6},{6,2},{3,7},{7,3},{8,12},{12,8},{9,1... | collective-permute-start | bytes 6291464 | tf_op jit(solution)/shard_map/ppermute | solution.py:34
  250.7 24.8 %collective-permute-start.28 = (bf16[128,2048]{1,0:T(8,128)(2,1)S(1)}, bf16[128,2048]{1,0:T(8,128)(2,1)S(1)}, u32[]{:S(2)}, u32[]{:S(2)}) collective-permute-start(bf16[128,2048]{1,0:T(8,128)(2,1)S(1)} %get-tuple-element.59), channel_id=1, source_target_pairs={{0,3},{1,0},{2,1},{3,2},{4,7},{5,4},{6,5},{7,6},{8,11},{9,8},{10,9... | collective-permute-start | bytes 1572872 | tf_op jit(solution)/shard_map/ppermute | solution.py:61
  263.1 68.8 %collective-permute-start.27 = (bf16[128,2048]{1,0:T(8,128)(2,1)S(1)}, bf16[128,2048]{1,0:T(8,128)(2,1)S(1)}, u32[]{:S(2)}, u32[]{:S(2)}) collective-permute-start(bf16[128,2048]{1,0:T(8,128)(2,1)S(1)} %get-tuple-element.60), channel_id=1, source_target_pairs={{0,2},{1,3},{2,0},{3,1},{4,6},{5,7},{6,4},{7,5},{8,10},{9,11},{10,... | collective-permute-start | bytes 1572872 | tf_op jit(solution)/shard_map/ppermute | solution.py:61
  263.1 68.8 %collective-permute-start.26 = (bf16[128,2048]{1,0:T(8,128)(2,1)S(1)}, bf16[128,2048]{1,0:T(8,128)(2,1)S(1)}, u32[]{:S(2)}, u32[]{:S(2)}) collective-permute-start(bf16[128,2048]{1,0:T(8,128)(2,1)S(1)} %get-tuple-element.58), channel_id=1, source_target_pairs={{0,1},{1,2},{2,3},{3,0},{4,5},{5,6},{6,7},{7,4},{8,9},{9,10},{10,1... | collective-permute-start | bytes 1572872 | tf_op jit(solution)/shard_map/ppermute | solution.py:61
  265.0 68.1 %collective-permute-start.20 = (bf16[128,2048]{1,0:T(8,128)(2,1)S(1)}, bf16[128,2048]{1,0:T(8,128)(2,1)S(1)}, u32[]{:S(2)}, u32[]{:S(2)}) collective-permute-start(bf16[128,2048]{1,0:T(8,128)(2,1)S(1)} %get-tuple-element.66), channel_id=1, source_target_pairs={{0,3},{1,0},{2,1},{3,2},{4,7},{5,4},{6,5},{7,6},{8,11},{9,8},{10,9... | collective-permute-start | bytes 1572872 | tf_op jit(solution)/shard_map/ppermute | solution.py:61
  268.2 85.2 %collective-permute-start.19 = (bf16[128,2048]{1,0:T(8,128)(2,1)S(1)}, bf16[128,2048]{1,0:T(8,128)(2,1)S(1)}, u32[]{:S(2)}, u32[]{:S(2)}) collective-permute-start(bf16[128,2048]{1,0:T(8,128)(2,1)S(1)} %get-tuple-element.67), channel_id=1, source_target_pairs={{0,2},{1,3},{2,0},{3,1},{4,6},{5,7},{6,4},{7,5},{8,10},{9,11},{10,... | collective-permute-start | bytes 1572872 | tf_op jit(solution)/shard_map/ppermute | solution.py:61
  275.5 77.9 %collective-permute-start.18 = (bf16[128,2048]{1,0:T(8,128)(2,1)S(1)}, bf16[128,2048]{1,0:T(8,128)(2,1)S(1)}, u32[]{:S(2)}, u32[]{:S(2)}) collective-permute-start(bf16[128,2048]{1,0:T(8,128)(2,1)S(1)} %get-tuple-element.65), channel_id=1, source_target_pairs={{0,1},{1,2},{2,3},{3,0},{4,5},{5,6},{6,7},{7,4},{8,9},{9,10},{10,1... | collective-permute-start | bytes 1572872 | tf_op jit(solution)/shard_map/ppermute | solution.py:61
  356.1 13.6 %collective-permute-start.31 = (bf16[128,2048]{1,0:T(8,128)(2,1)S(1)}, bf16[128,2048]{1,0:T(8,128)(2,1)S(1)}, u32[]{:S(2)}, u32[]{:S(2)}) collective-permute-start(bf16[128,2048]{1,0:T(8,128)(2,1)S(1)} %get-tuple-element.26), channel_id=1, source_target_pairs={{0,3},{1,0},{2,1},{3,2},{4,7},{5,4},{6,5},{7,6},{8,11},{9,8},{10,9... | collective-permute-start | bytes 1572872 | tf_op jit(solution)/shard_map/ppermute | solution.py:54
  356.1 47.3 %collective-permute-start.30 = (bf16[128,2048]{1,0:T(8,128)(2,1)S(1)}, bf16[128,2048]{1,0:T(8,128)(2,1)S(1)}, u32[]{:S(2)}, u32[]{:S(2)}) collective-permute-start(bf16[128,2048]{1,0:T(8,128)(2,1)S(1)} %get-tuple-element.26), channel_id=1, source_target_pairs={{0,2},{1,3},{2,0},{3,1},{4,6},{5,7},{6,4},{7,5},{8,10},{9,11},{10,... | collective-permute-start | bytes 1572872 | tf_op jit(solution)/shard_map/ppermute | solution.py:54
  358.4 44.9 %collective-permute-start.29 = (bf16[128,2048]{1,0:T(8,128)(2,1)S(1)}, bf16[128,2048]{1,0:T(8,128)(2,1)S(1)}, u32[]{:S(2)}, u32[]{:S(2)}) collective-permute-start(bf16[128,2048]{1,0:T(8,128)(2,1)S(1)} %get-tuple-element.26), channel_id=1, source_target_pairs={{0,1},{1,2},{2,3},{3,0},{4,5},{5,6},{6,7},{7,4},{8,9},{9,10},{10,1... | collective-permute-start | bytes 1572872 | tf_op jit(solution)/shard_map/ppermute | solution.py:54
  407.6 184.9 %reduce-scatter.6.cloned.1.call-start = ((), (), s32[]{:S(2)}) async-start(), calls=%async_computation.9 | async-start | bytes 1966080 | tf_op jit(solution)/shard_map/reduce_scatter | solution.py:396
  435.3 208.0 %reduce-scatter.12.cloned.1.call-start = ((), (), s32[]{:S(2)}) async-start(), calls=%async_computation.12 | async-start | bytes 5242880 | tf_op jit(solution)/shard_map/reduce_scatter | solution.py:396
  443.7 201.5 %reduce-scatter.10.cloned.1.call-start = ((), (), s32[]{:S(2)}) async-start(), calls=%async_computation.11 | async-start | bytes 5242880 | tf_op jit(solution)/shard_map/reduce_scatter | solution.py:396
  453.8 197.5 %reduce-scatter.14.cloned.1.call-start = ((), (), s32[]{:S(2)}) async-start(), calls=%async_computation.13 | async-start | bytes 5242880 | tf_op jit(solution)/shard_map/reduce_scatter | solution.py:396
  468.0 9.6 %collective-permute-start.33 = (bf16[512,2048]{1,0:T(8,128)(2,1)S(1)}, bf16[512,2048]{1,0:T(8,128)(2,1)}, u32[]{:S(2)}, u32[]{:S(2)}) collective-permute-start(bf16[512,2048]{1,0:T(8,128)(2,1)S(1)} %slice.241), channel_id=1, source_target_pairs={{0,4},{4,0},{1,5},{5,1},{2,6},{6,2},{3,7},{7,3},{8,12},{12,8},{9,1... | collective-permute-start | bytes 6291464 | tf_op jit(solution)/shard_map/ppermute | solution.py:34
  481.6 16.1 %collective-permute-start.36 = (bf16[128,2048]{1,0:T(8,128)(2,1)S(1)}, bf16[128,2048]{1,0:T(8,128)(2,1)S(1)}, u32[]{:S(2)}, u32[]{:S(2)}) collective-permute-start(bf16[128,2048]{1,0:T(8,128)(2,1)S(1)} %get-tuple-element.56), channel_id=1, source_target_pairs={{0,3},{1,0},{2,1},{3,2},{4,7},{5,4},{6,5},{7,6},{8,11},{9,8},{10,9... | collective-permute-start | bytes 1572872 | tf_op jit(solution)/shard_map/ppermute | solution.py:61
  481.6 46.1 %collective-permute-start.35 = (bf16[128,2048]{1,0:T(8,128)(2,1)S(1)}, bf16[128,2048]{1,0:T(8,128)(2,1)S(1)}, u32[]{:S(2)}, u32[]{:S(2)}) collective-permute-start(bf16[128,2048]{1,0:T(8,128)(2,1)S(1)} %get-tuple-element.57), channel_id=1, source_target_pairs={{0,2},{1,3},{2,0},{3,1},{4,6},{5,7},{6,4},{7,5},{8,10},{9,11},{10,... | collective-permute-start | bytes 1572872 | tf_op jit(solution)/shard_map/ppermute | solution.py:61
  481.7 46.0 %collective-permute-start.34 = (bf16[128,2048]{1,0:T(8,128)(2,1)S(1)}, bf16[128,2048]{1,0:T(8,128)(2,1)S(1)}, u32[]{:S(2)}, u32[]{:S(2)}) collective-permute-start(bf16[128,2048]{1,0:T(8,128)(2,1)S(1)} %get-tuple-element.55), channel_id=1, source_target_pairs={{0,1},{1,2},{2,3},{3,0},{4,5},{5,6},{6,7},{7,4},{8,9},{9,10},{10,1... | collective-permute-start | bytes 1572872 | tf_op jit(solution)/shard_map/ppermute | solution.py:61
  483.7 91.8 %collective-permute-start.23 = (bf16[128,2048]{1,0:T(8,128)(2,1)}, bf16[128,2048]{1,0:T(8,128)(2,1)S(1)}, u32[]{:S(2)}, u32[]{:S(2)}) collective-permute-start(bf16[128,2048]{1,0:T(8,128)(2,1)} %get-tuple-element.87), channel_id=1, source_target_pairs={{0,3},{1,0},{2,1},{3,2},{4,7},{5,4},{6,5},{7,6},{8,11},{9,8},{10,9... | collective-permute-start | bytes 1572872 | tf_op jit(solution)/shard_map/ppermute | solution.py:54
  486.1 89.4 %collective-permute-start.22 = (bf16[128,2048]{1,0:T(8,128)(2,1)}, bf16[128,2048]{1,0:T(8,128)(2,1)S(1)}, u32[]{:S(2)}, u32[]{:S(2)}) collective-permute-start(bf16[128,2048]{1,0:T(8,128)(2,1)} %get-tuple-element.87), channel_id=1, source_target_pairs={{0,2},{1,3},{2,0},{3,1},{4,6},{5,7},{6,4},{7,5},{8,10},{9,11},{10,... | collective-permute-start | bytes 1572872 | tf_op jit(solution)/shard_map/ppermute | solution.py:54
  497.7 79.3 %collective-permute-start.21 = (bf16[128,2048]{1,0:T(8,128)(2,1)}, bf16[128,2048]{1,0:T(8,128)(2,1)}, u32[]{:S(2)}, u32[]{:S(2)}) collective-permute-start(bf16[128,2048]{1,0:T(8,128)(2,1)} %get-tuple-element.87), channel_id=1, source_target_pairs={{0,1},{1,2},{2,3},{3,0},{4,5},{5,6},{6,7},{7,4},{8,9},{9,10},{10,1... | collective-permute-start | bytes 1572872 | tf_op jit(solution)/shard_map/ppermute | solution.py:54
  530.3 25.6 %collective-permute-start.46 = (f32[2,2048]{1,0:T(2,128)S(1)}, f32[2,2048]{1,0:T(2,128)S(1)}, u32[]{:S(2)}, u32[]{:S(2)}) collective-permute-start(f32[2,2048]{1,0:T(2,128)S(1)} %pad_maximum_fusion.24), channel_id=1, source_target_pairs={{0,3},{1,0},{2,1},{3,2},{4,7},{5,4},{6,5},{7,6},{8,11},{9,8},{10,9... | collective-permute-start | bytes 49160 | tf_op jit(solution)/shard_map/ppermute | solution.py:116
  530.4 43.5 %collective-permute-start.45 = (f32[2,2048]{1,0:T(2,128)S(1)}, f32[2,2048]{1,0:T(2,128)S(1)}, u32[]{:S(2)}, u32[]{:S(2)}) collective-permute-start(f32[2,2048]{1,0:T(2,128)S(1)} %pad_maximum_fusion.24), channel_id=1, source_target_pairs={{0,2},{1,3},{2,0},{3,1},{4,6},{5,7},{6,4},{7,5},{8,10},{9,11},{10,... | collective-permute-start | bytes 49160 | tf_op jit(solution)/shard_map/ppermute | solution.py:116
  556.0 19.4 %collective-permute-start.44 = (f32[2,2048]{1,0:T(2,128)S(1)}, f32[2,2048]{1,0:T(2,128)S(1)}, u32[]{:S(2)}, u32[]{:S(2)}) collective-permute-start(f32[2,2048]{1,0:T(2,128)S(1)} %pad_maximum_fusion.24), channel_id=1, source_target_pairs={{0,1},{1,2},{2,3},{3,0},{4,5},{5,6},{6,7},{7,4},{8,9},{9,10},{10,1... | collective-permute-start | bytes 49160 | tf_op jit(solution)/shard_map/ppermute | solution.py:116
  586.1 14.6 %collective-permute-start.39 = (bf16[128,2048]{1,0:T(8,128)(2,1)}, bf16[128,2048]{1,0:T(8,128)(2,1)S(1)}, u32[]{:S(2)}, u32[]{:S(2)}) collective-permute-start(bf16[128,2048]{1,0:T(8,128)(2,1)} %fusion.16), channel_id=1, source_target_pairs={{0,3},{1,0},{2,1},{3,2},{4,7},{5,4},{6,5},{7,6},{8,11},{9,8},{10,9... | collective-permute-start | bytes 1572872 | tf_op jit(solution)/shard_map/ppermute | solution.py:54
  588.0 46.9 %collective-permute-start.38 = (bf16[128,2048]{1,0:T(8,128)(2,1)}, bf16[128,2048]{1,0:T(8,128)(2,1)S(1)}, u32[]{:S(2)}, u32[]{:S(2)}) collective-permute-start(bf16[128,2048]{1,0:T(8,128)(2,1)} %fusion.16), channel_id=1, source_target_pairs={{0,2},{1,3},{2,0},{3,1},{4,6},{5,7},{6,4},{7,5},{8,10},{9,11},{10,... | collective-permute-start | bytes 1572872 | tf_op jit(solution)/shard_map/ppermute | solution.py:54
  589.6 45.3 %collective-permute-start.37 = (bf16[128,2048]{1,0:T(8,128)(2,1)}, bf16[128,2048]{1,0:T(8,128)(2,1)}, u32[]{:S(2)}, u32[]{:S(2)}) collective-permute-start(bf16[128,2048]{1,0:T(8,128)(2,1)} %fusion.16), channel_id=1, source_target_pairs={{0,1},{1,2},{2,3},{3,0},{4,5},{5,6},{6,7},{7,4},{8,9},{9,10},{10,1... | collective-permute-start | bytes 1572872 | tf_op jit(solution)/shard_map/ppermute | solution.py:54
  593.5 48.4 %collective-permute-start.40 = (bf16[256,384]{1,0:T(8,128)(2,1)S(1)}, bf16[256,384]{1,0:T(8,128)(2,1)S(1)}, u32[]{:S(2)}, u32[]{:S(2)}) collective-permute-start(bf16[256,384]{1,0:T(8,128)(2,1)S(1)} %constant_dynamic-slice_fusion.5), channel_id=1, source_target_pairs={{0,4},{4,0},{1,5},{5,1},{2,6},{6,2},{3,7},{7,3},{8,12},{12,8},{9,1... | collective-permute-start | bytes 589832 | tf_op jit(solution)/shard_map/ppermute | solution.py:34
  645.3 7.2 %collective-permute-start.42 = (bf16[256,1024]{1,0:T(8,128)(2,1)}, bf16[256,1024]{1,0:T(8,128)(2,1)S(1)}, u32[]{:S(2)}, u32[]{:S(2)}) collective-permute-start(bf16[256,1024]{1,0:T(8,128)(2,1)} %constant_dynamic-slice_fusion.3), channel_id=1, source_target_pairs={{0,4},{4,0},{1,5},{5,1},{2,6},{6,2},{3,7},{7,3},{8,12},{12,8},{9,1... | collective-permute-start | bytes 1572872 | tf_op jit(solution)/shard_map/ppermute | solution.py:34
  (60 other events, 735.5 us)
Sparse Core Ops, SparseCore 0:
  9.9 36.1 all-gather.4
  48.4 51.8 all-gather.10
  102.7 52.5 all-gather.8
  157.0 52.5 all-gather.6
  407.7 37.6 reduce-scatter.7
  448.3 31.1 reduce-scatter.5
  482.4 52.5 reduce-scatter.11
  538.0 52.9 reduce-scatter.9
  594.0 52.5 reduce-scatter.13

commit v2 on v1

v2 whole, which is shorter than its diff:
```python
import jax
import jax.numpy as jnp
from jax import lax
from jax.experimental import pallas as pl
from jax.experimental.pallas import tpu as pltpu
from jax.sharding import PartitionSpec as P

HD = 64
EPS = 1e-05
BASE = 500000.0
NEG = -1e30
BF = jnp.bfloat16
F32 = jnp.float32
BLOCK = 256


def dotf(left, right):
    return jnp.dot(left, right, preferred_element_type=F32)


def dot_t(left, right):
    return lax.dot_general(left, right, (((1,), (1,)), ((), ())), preferred_element_type=F32)


def dot_0(left, right):
    return lax.dot_general(left, right, (((0,), (0,)), ((), ())), preferred_element_type=F32)


def after(value, *others):
    return lax.optimization_barrier((value,) + others)[0]


def swap(value):
    return lax.ppermute(value, "ctx", [(0, 1), (1, 0)])


def pair(mine, theirs, core, axis):
    first = jnp.where(core == 0, mine, theirs)
    second = jnp.where(core == 0, theirs, mine)
    return jnp.concatenate([first, second], axis=axis)


def half_of(value, which, axis):
    size = value.shape[axis] // 2
    return lax.dynamic_slice_in_dim(value, which * size, size, axis)


def xor_pairs(axis, bit):
    return [(k, k ^ bit) for k in range(lax.axis_size(axis))]


def bits_of(axis):
    return [1 << b for b in range(lax.axis_size(axis).bit_length() - 1)]


def gated(value, gate):
    return value if gate is None else after(value, gate)


def near_far():
    return xor_pairs("tp", 1), xor_pairs("tp", 2)


def halved(values, pairs):
    half = values[0].shape[0] // 2
    sent = jnp.concatenate([v[half:].astype(BF) for v in values], axis=0)
    return [v[:half] for v in values], lax.ppermute(sent, "tp", pairs)


def summed(kept, got):
    half = kept[0].shape[0]
    return [
        k.astype(F32) + got[n * half : (n + 1) * half].astype(F32) for n, k in enumerate(kept)
    ]


def position(index, place, count):
    distance = index ^ place
    result = distance & 0
    for bit in range(count.bit_length() - 1):
        result = result * 2 + ((distance >> bit) & 1)
    return result


def arrange(parts, place_at, kind, back):
    count = lax.axis_size("tp")
    rows = parts[0].shape[0]
    size = rows // count
    width = parts[0].shape[1]
    columns = width // 4

    def kernel(place_ref, *refs):
        out_ref = refs[-1]
        for n in range(len(parts)):
            for j in range(count):
                natural = slice(j * size, (j + 1) * size)
                at = pl.multiple_of(position(j, place_ref[0], count) * size, size)
                if back:
                    out_ref[n * rows + j * size : n * rows + (j + 1) * size, :] = refs[n][
                        pl.ds(at, size), :
                    ].astype(kind)
                else:
                    to = pl.ds(pl.multiple_of(n * rows + at, size), size)
                    out_ref[to, :] = refs[n][natural, :].astype(kind)

    return pl.pallas_call(
        kernel,
        grid_spec=pltpu.PrefetchScalarGridSpec(
            num_scalar_prefetch=1,
            grid=(4,),
            in_specs=[pl.BlockSpec((rows, columns), lambda i, at: (0, i)) for _ in parts],
            out_specs=pl.BlockSpec((rows * len(parts), columns), lambda i, at: (0, i)),
        ),
        out_shape=jax.ShapeDtypeStruct((rows * len(parts), width), kind),
        name="arrange",
    )(place_at, *parts)


class Scatter:
    def __init__(self, grad):
        self.plain = grad.shape[0] != 4
        if self.plain:
            self.whole = lax.psum_scatter(grad, "fsdp", scatter_dimension=0, tiled=False)
            return
        me = lax.axis_index("fsdp")
        cut = grad.shape[1] // 32 * 16
        self.near, self.far = xor_pairs("fsdp", 1), xor_pairs("fsdp", 2)
        self.top, self.low = slice(0, cut), slice(cut, None)
        self.blocks = [lax.dynamic_index_in_dim(grad, me ^ k, 0, keepdims=False) for k in range(4)]
        one, two, three = self.blocks[1:]
        self.by_near = lax.ppermute(jnp.stack([one[self.top], three[self.top]]), "fsdp", self.near)
        self.by_far = lax.ppermute(jnp.stack([two[self.low], three[self.low]]), "fsdp", self.far)

    def second(self, *gate):
        if self.plain:
            self.token = self.whole
            return
        by_near, by_far = lax.optimization_barrier((self.by_near, self.by_far) + gate)[:2]
        own, one, two = [b.astype(F32) for b in self.blocks[:3]]
        self.a_own = own[self.top] + by_near[0].astype(F32)
        self.b_own = own[self.low] + by_far[0].astype(F32)
        a_far = (two[self.top] + by_near[1].astype(F32)).astype(BF)
        b_near = (one[self.low] + by_far[1].astype(F32)).astype(BF)
        self.token = b_near
        self.a_got = lax.ppermute(a_far, "fsdp", self.far)
        self.b_got = lax.ppermute(b_near, "fsdp", self.near)

    def third(self, *gate):
        if self.plain:
            return self.whole
        a, b = lax.optimization_barrier((self.a_got, self.b_got) + gate)[:2]
        return jnp.concatenate(
            [(self.a_own + a.astype(F32)).astype(BF), (self.b_own + b.astype(F32)).astype(BF)], axis=0
        )


class Gather:
    def __init__(self, shard, axis=0):
        self.shard, self.axis, self.plain = shard, axis, lax.axis_size("fsdp") != 4

    def first(self, *gate):
        shard = after(self.shard, *gate) if gate else self.shard
        if self.plain:
            self.whole = lax.all_gather(shard, "fsdp", axis=self.axis, tiled=True)
            return self.whole
        self.one = lax.ppermute(shard, "fsdp", xor_pairs("fsdp", 1))
        self.two = lax.ppermute(shard, "fsdp", xor_pairs("fsdp", 2))
        return self.two

    def second(self, *gate):
        if self.plain:
            return self.whole
        one, two = self.one, self.two
        if gate:
            one, two = lax.optimization_barrier((one, two) + gate)[:2]
        cut = self.shard.shape[0] // 32 * 16
        far = lax.ppermute(one[:cut], "fsdp", xor_pairs("fsdp", 2))
        near = lax.ppermute(two[cut:], "fsdp", xor_pairs("fsdp", 1))
        return [self.shard, one, two, jnp.concatenate([far, near], axis=0)]


def in_order(pieces, axis, rows=slice(None)):
    if not isinstance(pieces, list):
        count = lax.axis_size("fsdp")
        size = pieces.shape[axis] // count
        pieces = [lax.slice_in_dim(pieces, k * size, (k + 1) * size, axis=axis)[rows] for k in range(count)]
        return jnp.concatenate(pieces, axis=axis)
    me = lax.axis_index("fsdp")
    low, high = (me & 1) == 0, (me & 2) == 0
    own, one, two, three = [p[rows] for p in pieces]
    a, b = jnp.where(low, own, one), jnp.where(low, one, own)
    c, d = jnp.where(low, two, three), jnp.where(low, three, two)
    return jnp.concatenate(
        [jnp.where(high, a, c), jnp.where(high, b, d), jnp.where(high, c, a), jnp.where(high, d, b)],
        axis=axis,
    )


def sum_steps(value, steps):
    for axis, bit in steps:
        value = value + lax.ppermute(value, axis, xor_pairs(axis, bit))
    return value


def grad_kernel(lefts, rights, column, columns, block):
    rows, wide = lefts[0].shape

    def kernel(*refs):
        total = dot_0(refs[0][...], refs[len(lefts)][...])
        for n in range(1, len(lefts)):
            total = total + dot_0(refs[n][...], refs[len(lefts) + n][...])
        refs[-1][...] = total.astype(BF)

    return pl.pallas_call(
        kernel,
        grid=(wide // block,),
        in_specs=[pl.BlockSpec((rows, block), lambda i: (0, i)) for _ in lefts]
        + [pl.BlockSpec((rows, columns), lambda i: (0, column)) for _ in rights],
        out_specs=pl.BlockSpec((block, columns), lambda i: (i, 0)),
        out_shape=jax.ShapeDtypeStruct((wide, columns), BF),
        name="grad",
    )(*lefts, *rights)


def halves_swapped(tile):
    lane = lax.broadcasted_iota(jnp.int32, tile.shape, 1)
    width = tile.shape[1]
    back = pltpu.roll(tile, width - HD // 2, 1)
    ahead = pltpu.roll(tile, HD // 2, 1)
    return jnp.where(lane % HD < HD // 2, back, ahead)


def padded(kv):
    lane = lax.broadcasted_iota(jnp.int32, kv.shape, 1)
    low = lane < HD
    other = pltpu.roll(kv, HD, 1)
    zero = jnp.zeros_like(kv)
    keys = (jnp.where(low, kv, zero), jnp.where(low, zero, other))
    vals = (jnp.where(low, other, zero), jnp.where(low, zero, kv))
    return [k.astype(BF) for k in keys], [v.astype(BF) for v in vals]


def causal_mask():
    row = lax.broadcasted_iota(jnp.int32, (BLOCK, BLOCK), 0)
    col = lax.broadcasted_iota(jnp.int32, (BLOCK, BLOCK), 1)
    return col <= row


def spread(ref, base, place, count, lanes, value):
    size = value.shape[0] // count
    for j in range(count):
        at = pl.multiple_of(base + position(j, place, count) * size, size)
        ref[pl.ds(at, size), lanes] = value[j * size : (j + 1) * size]


def collect(ref, base, place, count, lanes, rows):
    size = rows // count
    return jnp.concatenate(
        [
            ref[pl.ds(pl.multiple_of(base + position(j, place, count) * size, size), size), lanes]
            for j in range(count)
        ],
        axis=0,
    )


def attend_blocks(at_ref, q_ref, keys, vals, out_ref, lse_ref, blocks, count):
    core, place = at_ref[0], at_ref[1]
    width = out_ref.shape[1]
    scale = HD ** (-0.5)
    causal = causal_mask()
    for n, i in enumerate(blocks):
        at = slice(i * BLOCK, (i + 1) * BLOCK)
        to = slice(n * BLOCK, (n + 1) * BLOCK)
        for j in range(width // 128):
            lanes = slice(j * 128, (j + 1) * 128)
            queries = q_ref[at, lanes]
            result = None
            for side in range(2):
                key, val = keys[side], vals[side]
                diag = dot_t(queries, key[at]) * scale
                diag = jnp.where(causal, diag, NEG)
                top = jnp.max(diag, axis=-1, keepdims=True)
                if i:
                    past = dot_t(queries, key[: i * BLOCK]) * scale
                    top = jnp.maximum(top, jnp.max(past, axis=-1, keepdims=True))
                    weight = jnp.exp(past - top)
                p_diag = jnp.exp(diag - top)
                total = jnp.sum(p_diag, axis=-1, keepdims=True)
                if i:
                    total = total + jnp.sum(weight, axis=-1, keepdims=True)
                inverse = 1.0 / total
                part = dotf(p_diag.astype(BF), val[at])
                if i:
                    part = part + dotf(weight.astype(BF), val[: i * BLOCK])
                part = part * inverse
                result = part if result is None else result + part
                head = 2 * j + side
                lse_ref[to, head : head + 1] = top + jnp.log(total)
            spread(out_ref, (core ^ n) * BLOCK, place, count, lanes, result.astype(BF))


SCALARS = pl.BlockSpec(memory_space=pltpu.SMEM)


def attend_first(at, qkv, tables, blocks, count):
    tokens, width = qkv.shape
    width = width - 2 * HD
    local = tokens // 2

    def kernel(at_ref, qkv_ref, cos_ref, sin_ref, cos_kv_ref, sin_kv_ref, q_ref, kv_ref, out_ref, lse_ref):
        core = at_ref[0]
        for half in range(2):
            to = slice(half * local, (half + 1) * local)
            source = pl.ds(pl.multiple_of((core ^ half) * local, local), local)
            for j in range(width // 128):
                tile = qkv_ref[source, j * 128 : (j + 1) * 128]
                turned = tile * cos_ref[to] + halves_swapped(tile) * sin_ref[to]
                q_ref[to, j * 128 : (j + 1) * 128] = turned.astype(BF)
            tile = qkv_ref[source, width : width + 128]
            turned = tile * cos_kv_ref[to] + halves_swapped(tile) * sin_kv_ref[to]
            kv_ref[to, :] = turned.astype(BF)
        keys, vals = padded(kv_ref[...].astype(F32))
        attend_blocks(at_ref, q_ref, keys, vals, out_ref, lse_ref, blocks, count)

    rows = len(blocks) * BLOCK
    return pl.pallas_call(
        kernel,
        in_specs=[SCALARS] + [pl.BlockSpec()] * 5,
        out_shape=(
            jax.ShapeDtypeStruct((tokens, width), BF),
            jax.ShapeDtypeStruct((tokens, 2 * HD), BF),
            jax.ShapeDtypeStruct((rows, width), BF),
            jax.ShapeDtypeStruct((rows, width // HD), F32),
        ),
        name="attend_first",
    )(at, qkv, *tables)


def attend_next(at, queries, kv, blocks, count):
    width = queries.shape[1]

    def kernel(at_ref, q_ref, kv_ref, out_ref, lse_ref):
        keys, vals = padded(kv_ref[...].astype(F32))
        attend_blocks(at_ref, q_ref, keys, vals, out_ref, lse_ref, blocks, count)

    rows = len(blocks) * BLOCK
    return pl.pallas_call(
        kernel,
        in_specs=[SCALARS] + [pl.BlockSpec()] * 2,
        out_shape=(
            jax.ShapeDtypeStruct((rows, width), BF),
            jax.ShapeDtypeStruct((rows, width // HD), F32),
        ),
        name="attend_next",
    )(at, queries, kv)


def attend_back(at, queries, kv, out, grads, lse, tables, blocks, carried, count):
    tokens, width = queries.shape
    scale = HD ** (-0.5)
    tiles = width // 128
    last = carried is not None

    def kernel(at_ref, q_ref, kv_ref, out_ref, mine_ref, theirs_ref, lse_ref, cos_ref, sin_ref, cos_kv_ref, sin_kv_ref, *refs):
        if last:
            dk_in, dv_in, dq_ref, dq_to_ref, dkv_ref, dkv_to_ref, dk_ref, dv_ref = refs
        else:
            dq_ref, dq_to_ref, dk_ref, dv_ref = refs
        core, place = at_ref[0], at_ref[1]
        keys, vals = padded(kv_ref[...].astype(F32))
        causal = causal_mask()
        low = lax.broadcasted_iota(jnp.int32, (BLOCK, 128), 1) < HD
        if last:
            dk_ref[...] = dk_in[...]
            dv_ref[...] = dv_in[...]
        else:
            dk_ref[...] = jnp.zeros_like(dk_ref)
            dv_ref[...] = jnp.zeros_like(dv_ref)
        for n, i in enumerate(blocks):
            at = slice(i * BLOCK, (i + 1) * BLOCK)
            to = slice(n * BLOCK, (n + 1) * BLOCK)
            for j in range(tiles):
                lanes = slice(j * 128, (j + 1) * 128)
                query = q_ref[at, lanes]
                mine = collect(mine_ref, 0, place, count, lanes, BLOCK).astype(F32)
                theirs = collect(theirs_ref, 0, place, count, lanes, BLOCK).astype(F32)
                grad_f = jnp.where(core == n, mine, theirs)
                grad = grad_f.astype(BF)
                result = collect(out_ref, (core ^ n) * BLOCK, place, count, lanes, BLOCK)
                product = grad_f * result.astype(F32)
                d_query = None
                for side in range(2):
                    key, val = keys[side], vals[side]
                    head = 2 * j + side
                    top = lse_ref[to, head : head + 1]
                    part_of = low if side == 0 else jnp.logical_not(low)
                    delta = jnp.sum(jnp.where(part_of, product, 0.0), axis=-1, keepdims=True)
                    spans = [(at, True)]
                    if i:
                        spans.append((slice(0, i * BLOCK), False))
                    for span, masked in spans:
                        scores = dot_t(query, key[span]) * scale
                        if masked:
                            scores = jnp.where(causal, scores, NEG)
                        probs = jnp.exp(scores - top)
                        d_probs = dot_t(grad, val[span])
                        d_scores = (probs * (d_probs - delta) * scale).astype(BF)
                        dv_ref[side, span] += dot_0(probs.astype(BF), grad)
                        dk_ref[side, span] += dot_0(d_scores, query)
                        part = dotf(d_scores, key[span])
                        d_query = part if d_query is None else d_query + part
                turned = d_query * cos_ref[at] - halves_swapped(d_query) * sin_ref[at]
                turned = turned.astype(BF)
                dq_ref[pl.ds(pl.multiple_of((core ^ n) * BLOCK, BLOCK), BLOCK), lanes] = turned
                spread(dq_to_ref, (core ^ n) * BLOCK, place, count, lanes, turned)
        if last:
            full = lax.broadcasted_iota(jnp.int32, (tokens, 128), 1) < HD
            d_key = dk_ref[0] + pltpu.roll(dk_ref[1], HD, 1)
            d_val = dv_ref[1] + pltpu.roll(dv_ref[0], HD, 1)
            tile = jnp.where(full, d_key, d_val)
            turned = tile * cos_kv_ref[...] - halves_swapped(tile) * sin_kv_ref[...]
            turned = turned.astype(BF)
            half = tokens // 2
            for c in range(2):
                base = (core ^ c) * half
                dkv_ref[pl.ds(pl.multiple_of(base, half), half), :] = turned[c * half : (c + 1) * half]
                for i in range(half // BLOCK):
                    rows = turned[c * half + i * BLOCK : c * half + (i + 1) * BLOCK]
                    spread(dkv_to_ref, base + i * BLOCK, place, count, slice(0, 128), rows)

    sums = [((2, tokens, 128), F32)] * 2
    rows = len(blocks) * BLOCK
    shapes = [jax.ShapeDtypeStruct((rows, width), BF)] * 2
    if last:
        shapes += [jax.ShapeDtypeStruct((tokens, 2 * HD), BF)] * 2
    else:
        shapes += [jax.ShapeDtypeStruct(*s) for s in sums]
    return pl.pallas_call(
        kernel,
        in_specs=[SCALARS] + [pl.BlockSpec()] * (10 + 2 * last),
        out_shape=tuple(shapes),
        scratch_shapes=[pltpu.VMEM(*s) for s in sums] if last else [],
        name="attend_back",
    )(at, queries, kv, out, *grads, lse, *tables, *(carried or ()))


def rotary_tables(tokens):
    lane = lax.broadcasted_iota(jnp.int32, (1, 2 * HD), 1)
    inverse = BASE ** (-((lane % (HD // 2)).astype(F32) * 2.0) / HD)
    angle = lax.broadcasted_iota(jnp.int32, (tokens, 2 * HD), 0).astype(F32) * inverse
    cosine, sine = jnp.cos(angle), jnp.sin(angle) * jnp.where(lane % HD < HD // 2, -1.0, 1.0)
    keyed = lane < HD
    return (cosine, sine, jnp.where(keyed, cosine, 1.0), jnp.where(keyed, sine, 0.0))


def inverse_rms(rows):
    return lax.rsqrt(jnp.mean(rows * rows, axis=-1, keepdims=True) + EPS)


def norm_backward(rows, scale, gain, grad):
    weighted = grad * gain
    d_rows = scale * weighted - rows * scale**3 * jnp.mean(weighted * rows, axis=-1, keepdims=True)
    return (d_rows, jnp.sum(grad * rows * scale, axis=0))


def stack(*parts):
    return jnp.concatenate(parts, axis=0)


CHUNKS = 2


def body(
    block_input, cotangent, w_query, w_key, w_value, w_output, w_gate, w_up, w_down, attn_gain, ffn_gain
):
    core = lax.axis_index("ctx")
    place = lax.axis_index("tp")
    slot = lax.axis_index("fsdp")
    count = lax.axis_size("tp")
    fsdp = lax.axis_size("fsdp")
    near, far = near_far()
    rows = block_input[0]
    cot = cotangent[0]
    local, width = rows.shape
    shard = w_query.shape[0]
    other = 1 - core
    span = local // CHUNKS
    piece = span // count
    units = w_gate.shape[1] // 2
    where = jnp.stack([core, place]).astype(jnp.int32)
    place_at = place.astype(jnp.int32).reshape(1)

    gains = jnp.concatenate([attn_gain, ffn_gain])
    narrow = (w_query.shape[1] + 2 * w_key.shape[1]) // 2
    lines = -(-gains.shape[0] // (16 * narrow)) * 16
    gain_rows = jnp.pad(gains, (0, lines * narrow - gains.shape[0])).reshape(lines, narrow)

    def packed(which):
        halves = [half_of(w, which, 1) for w in (w_query, w_key, w_value)]
        return stack(jnp.concatenate(halves, axis=1), gain_rows)

    def packed_gu(which):
        return jnp.concatenate([half_of(w_gate, which, 1), half_of(w_up, which, 1)], axis=1)

    qkv_mine, qkv_got = packed(core), swap(packed(other))
    gu_got = swap(after(packed_gu(other), qkv_got))
    rows_theirs = swap(after(rows, qkv_got))
    wd_got = swap(after(half_of(w_down, other, 0), rows_theirs))
    get_qkv = Gather(
        stack(
            pair(qkv_mine[:shard], qkv_got[:shard], core, 0), pair(qkv_mine[shard:], qkv_got[shard:], core, 0)
        )
    )
    get_wo = Gather(w_output, 1)
    t_qkv = get_qkv.first()
    w_gu = lax.all_gather(pair(packed_gu(core), gu_got, core, 0), "fsdp", axis=0, tiled=True)
    wd = lax.all_gather(
        pair(half_of(w_down, core, 0), wd_got, core, 1), "fsdp", axis=1, tiled=True
    )
    scale_own, scale_theirs = inverse_rms(rows), inverse_rms(rows_theirs)
    tables = rotary_tables(2 * local)
    qkv_pieces = get_qkv.second(scale_own)
    t_wo = get_wo.first(t_qkv)
    w_qkv = in_order(qkv_pieces, 0, slice(0, 2 * shard))
    gain_all = in_order(qkv_pieces, 0, slice(2 * shard, None)).reshape(-1, lines * narrow)
    w_qkv, gain_all = lax.optimization_barrier((w_qkv, gain_all, scale_theirs) + tuple(tables))[:2]
    gain_a = gain_all[:, :shard].reshape(-1).astype(F32)
    gain_f = gain_all[:, shard : 2 * shard].reshape(-1).astype(F32)

    normed = stack(
        (rows * scale_own * gain_a).astype(BF), (rows_theirs * scale_theirs * gain_a).astype(BF)
    )
    qkv = dotf(normed, w_qkv)
    blocks = [[h * span // BLOCK, h * span // BLOCK + local // BLOCK] for h in range(CHUNKS)]
    queries, kv, attn_0, lse_0 = attend_first(where, qkv, tables, blocks[0], count)

    wo_mine = in_order(get_wo.second(qkv), 1)
    wo_theirs = swap(wo_mine)
    wo_halves = [w.reshape(w.shape[0], -1, shard) for w in (wo_mine, wo_theirs)]
    first = jnp.where(core == 0, wo_halves[0], wo_halves[1])
    second = jnp.where(core == 0, wo_halves[1], wo_halves[0])
    wo = jnp.stack([first, second], axis=2).reshape(w_output.shape[0], width)
    wo_a, wo_b = lax.optimization_barrier((half_of(wo, core, 0), half_of(wo, other, 0)))

    def slice_of(value, h):
        return lax.dynamic_slice_in_dim(value, h * span + place * piece, piece, 0)

    attn_1, lse_1 = attend_next(where, queries, kv, blocks[1], count)
    attn, lse = [attn_0, attn_1], [lse_0, lse_1]
    attn_own = [(a[:span], swap(a[span:])) for a in attn]
    partial = [dotf(mine, wo_a) + dotf(theirs, wo_b) for mine, theirs in attn_own]

    def hidden_of(h, total):
        hidden = slice_of(rows, h) + total
        scale = inverse_rms(hidden)
        return hidden, scale, (hidden * scale * gain_f).astype(BF)

    k0, g0 = halved([partial[0]], near)
    k1, g1 = halved([partial[1]], near)
    v0 = summed(k0, after(g0, partial[1]))
    k0, g0 = halved(v0, far)
    v1 = summed(k1, after(g1, v0[0]))
    k1, g1 = halved(v1, far)
    hidden_0, scale_0, c0 = hidden_of(0, summed(k0, after(g0, v1[0]))[0])
    a0 = lax.ppermute(c0, "tp", far)
    hidden_1, scale_1, c1 = hidden_of(1, summed(k1, after(g1, c0))[0])
    a1 = lax.ppermute(c1, "tp", far)
    cur0 = stack(c0, after(a0, c1))
    b0, s0 = lax.ppermute(cur0, "tp", near), swap(cur0)
    cur1 = stack(c1, after(a1, cur0))
    b1, s1 = lax.ppermute(cur1, "tp", near), swap(cur1)

    cot_gated = after(cot.astype(BF), v1[0])
    cot_own = arrange([cot_gated[h * span : (h + 1) * span] for h in range(CHUNKS)], place_at, BF, False)
    cot_theirs = swap(cot_own)
    cots = [
        stack(cot_own[h * span : (h + 1) * span], cot_theirs[h * span : (h + 1) * span])
        for h in range(CHUNKS)
    ]

    def backward_of(gu, d_inner):
        gate, up = gu[:, :units], gu[:, units:]
        sigma = jax.nn.sigmoid(gate)
        active = gate * sigma
        d_gate = (d_inner * up * sigma * (1.0 + gate * (1.0 - sigma))).astype(BF)
        d_up = (d_inner * active).astype(BF)
        return (active * up).astype(BF), jnp.concatenate([d_gate, d_up], axis=1)

    b0 = after(b0, cur1, *cots)
    hnorm_0 = stack(cur0, b0, s0, swap(b0))
    gu_0 = dotf(hnorm_0, w_gu)
    b1 = after(b1, gu_0)
    s_b1 = swap(b1)
    inner_0, d_gu_0 = backward_of(gu_0, dot_t(cots[0], wd))
    d_full_0 = dot_t(d_gu_0, w_gu)
    s0 = swap(d_full_0[span:].astype(BF))
    cur1, b1, s1, s_b1 = lax.optimization_barrier((cur1, b1, s1, s_b1, d_full_0))[:4]
    hnorm_1 = stack(cur1, b1, s1, s_b1)
    gu_1 = dotf(hnorm_1, w_gu)
    d0 = d_full_0[:span] + after(s0, gu_1).astype(F32)
    k0, g0 = halved([d0], near)
    inner_1, d_gu_1 = backward_of(gu_1, dot_t(after(cots[1], d0), wd))
    d_full_1 = dot_t(d_gu_1, w_gu)
    s1 = swap(d_full_1[span:].astype(BF))
    v0 = summed(k0, after(g0, d_full_1))
    k0, g0 = halved(v0, far)
    d1 = d_full_1[:span] + after(s1, v0[0]).astype(F32)
    k1, g1 = halved([d1], near)

    def reduced(grad, axis):
        return lax.psum_scatter(grad, "fsdp", scatter_dimension=axis, tiled=True)

    def gradient(lefts, rights, column, *gate):
        n = len(rights)
        rights = lax.optimization_barrier(tuple(rights) + gate)[:n]
        return grad_kernel(lefts, rights, column, units if column is not None else width, 512)

    d_gu, inner, hnorm = [d_gu_0, d_gu_1], [inner_0, inner_1], [hnorm_0, hnorm_1]
    g_gate = gradient(hnorm, d_gu, 0, v0[0], d1)

    def back_of(h, hidden, scale, total):
        d_norm, gain = norm_backward(hidden, scale, gain_f, total)
        d_hidden = slice_of(cot, h) + d_norm
        return d_hidden, gain, d_hidden.astype(BF)

    dh_0, gain_0, c0 = back_of(0, hidden_0, scale_0, summed(k0, after(g0, g_gate))[0])
    a0 = lax.ppermute(c0, "tp", far)
    v1 = summed(k1, after(g1, c0))
    k1, g1 = halved(v1, far)
    g_up = gradient(hnorm, d_gu, 1, c0, v1[0])
    cur0 = stack(c0, after(a0, g_up))
    b0 = lax.ppermute(cur0, "tp", near)
    dh_1, gain_1, c1 = back_of(1, hidden_1, scale_1, summed(k1, after(g1, cur0))[0])
    a1 = lax.ppermute(c1, "tp", far)
    g_ffn = gain_0 + gain_1
    g_down = grad_kernel(inner, lax.optimization_barrier(tuple(cots) + (cur0, c1))[:2], 0, width, 512)
    down = [dotf(after(i, g_down), wd) for i in inner]
    s_down = swap(stack(*[d[span:].astype(BF) for d in down]))
    r_gate, r_up, r_down = reduced(g_gate, 0), reduced(g_up, 0), reduced(g_down, 1)
    full_0 = stack(cur0, after(b0, *down))
    cur1 = stack(c1, after(a1, full_0))
    b1 = lax.ppermute(cur1, "tp", near)
    down = [
        d[:span] + after(s_down, cur1)[n * span : (n + 1) * span].astype(F32) for n, d in enumerate(down)
    ]
    k_out, g_out = halved(down, near)

    def grads_of(full):
        send = swap(dot_t(full, wo_b).astype(BF))
        return dot_t(full, wo_a).astype(BF), send

    dq_0, dq_to_0, *carried = attend_back(
        where, queries, kv, attn_0, grads_of(after(full_0, *down)), lse_0, tables, blocks[0], None, count
    )
    v_out = summed(k_out, after(g_out, dq_0))
    k_out, g_out = halved(v_out, far)
    full_1 = stack(cur1, after(b1, *v_out))
    dq_1, dq_to_1, d_kv, d_kv_to = attend_back(
        where, queries, kv, attn_1, grads_of(full_1), lse_1, tables, blocks[1], carried, count
    )

    def joined(query, kv_of, h, side):
        at = side * local + h * span
        return jnp.concatenate([query[side * span : (side + 1) * span], kv_of[at : at + span]], axis=1)

    parts = [
        dot_t(stack(*[joined(q, d_kv_to, h, s) for s in range(2)]), w_qkv)
        for h, q in enumerate((dq_to_0, dq_to_1))
    ]
    sent = [swap(p[span:].astype(BF)) for p in parts]
    d_qkv = stack(*[joined(q, d_kv, h, s) for s in range(2) for h, q in enumerate((dq_0, dq_1))])
    g_qkv = dot_0(normed, after(d_qkv, *parts)).astype(BF)
    d0 = parts[0][:span] + after(sent[0], g_qkv).astype(F32)
    d1 = parts[1][:span] + after(sent[1], g_qkv).astype(F32)
    k0, g0 = halved([d0], near)
    k1, g1 = halved([d1], near)
    totals = summed(k_out, after(g_out, d0, d1))
    c_out = stack(hidden_0 + totals[0], hidden_1 + totals[1]).astype(BF)
    a_out = lax.ppermute(c_out, "tp", far)

    dh_all = after(stack(full_0, full_1), c_out)
    g_mine = dot_0(stack(*[a[0] for a in attn_own]), dh_all).astype(BF)
    g_theirs = dot_0(stack(*[a[1] for a in attn_own]), dh_all).astype(BF)

    def columns(grad, which):
        grad = grad.reshape(grad.shape[0], fsdp, 2, shard)
        return lax.dynamic_index_in_dim(grad, which, 2, keepdims=False)

    got = swap(stack(columns(g_theirs, other), columns(g_mine, other)))
    g_output = stack(columns(g_mine, core), columns(g_theirs, core)).astype(F32) + got.astype(F32)
    g_output = g_output.astype(BF).swapaxes(0, 1)
    g_qkv = g_qkv.reshape(fsdp, -1, narrow)
    joint = g_qkv.shape[1] == g_output.shape[1]
    if joint:
        reduce = [Scatter(jnp.concatenate([g_qkv, g_output], axis=2))]
    else:
        reduce = [Scatter(g_qkv), Scatter(g_output)]

    v0 = summed(k0, after(g0, g_output))
    k0, g0 = halved(v0, far)
    v1 = summed(k1, after(g1, v0[0]))
    k1, g1 = halved(v1, far)
    cur_out = stack(*[stack(c_out[h * piece : (h + 1) * piece], after(a_out, v1[0])[h * piece : (h + 1) * piece]) for h in range(CHUNKS)])
    b_out = lax.ppermute(cur_out, "tp", near)
    for item in reduce:
        item.second(cur_out)

    def input_of(h, d_hidden, total):
        d_rows, gain = norm_backward(slice_of(rows, h), slice_of(scale_own, h), gain_a, total)
        return gain, (d_hidden + d_rows).astype(BF)

    gain_0, c0 = input_of(0, dh_0, summed(k0, after(g0, *[r.token for r in reduce]))[0])
    a0 = lax.ppermute(c0, "tp", far)
    gain_1, c1 = input_of(1, dh_1, summed(k1, after(g1, c0))[0])
    a1 = lax.ppermute(c1, "tp", far)
    g_all = sum_steps(jnp.stack([gain_0 + gain_1, g_ffn]), [("ctx", 1)])
    cur0 = stack(c0, after(a0, c1, g_all))
    b0 = lax.ppermute(cur0, "tp", near)
    cur1 = stack(c1, after(a1, cur0))
    b1 = lax.ppermute(cur1, "tp", near)

    r_down, r_gate, r_up = lax.optimization_barrier((r_down, r_gate, r_up, cur1))[:3]
    s_down = pair(half_of(r_down, core, 1), swap(half_of(r_down, other, 1)), core, 0).astype(F32)
    s_gate = pair(half_of(r_gate, core, 0), swap(half_of(r_gate, other, 0)), core, 1).astype(F32)
    s_up = pair(half_of(r_up, core, 0), swap(half_of(r_up, other, 0)), core, 1).astype(F32)

    half = span
    cur_half, got_half = cur_out.shape[0] // CHUNKS, b_out.shape[0] // CHUNKS
    b_out = after(b_out, cur1)
    out = arrange(
        [
            stack(cur_out[h * cur_half : (h + 1) * cur_half], b_out[h * got_half : (h + 1) * got_half])
            for h in range(CHUNKS)
        ],
        place_at,
        F32,
        True,
    )
    g_all = sum_steps(after(g_all, cur1), [("tp", 1), ("tp", 2)] + [("fsdp", b) for b in bits_of("fsdp")])

    results = [item.third(out) for item in reduce]
    if joint:
        r_qkv, r_output = results[0][:, :narrow], results[0][:, narrow:]
    else:
        r_qkv, r_output = results
    half = r_output.shape[0] // 2
    s_output = pair(r_output[:half], r_output[half:], core, 0).astype(F32)
    mine, theirs = half_of(r_qkv, core, 0), swap(half_of(r_qkv, other, 0))
    bounds = [0, w_query.shape[1] // 2, (w_query.shape[1] + w_key.shape[1]) // 2, narrow]
    s_query, s_key, s_value = [
        pair(mine[:, a:b], theirs[:, a:b], core, 1).astype(F32) for a, b in zip(bounds, bounds[1:])
    ]
    d_input = arrange([stack(cur0, b0), stack(cur1, b1)], place_at, F32, True)

    start = (slot * 2 + core) * shard
    s_attn = lax.dynamic_slice_in_dim(g_all[0], start, shard, 0)
    s_ffn = lax.dynamic_slice_in_dim(g_all[1], start, shard, 0)
    return (
        out[None],
        d_input[None],
        s_query,
        s_key,
        s_value,
        s_output,
        s_gate,
        s_up,
        s_down,
        s_attn,
        s_ffn,
    )


def solution(mesh):
    placed = (
        P("fsdp", "ctx", None),
        P("fsdp", "ctx", None),
        P(("fsdp", "ctx"), "tp"),
        P(("fsdp", "ctx"), "tp"),
        P(("fsdp", "ctx"), "tp"),
        P("tp", ("fsdp", "ctx")),
        P(("fsdp", "ctx"), "tp"),
        P(("fsdp", "ctx"), "tp"),
        P("tp", ("fsdp", "ctx")),
        P(("fsdp", "ctx")),
        P(("fsdp", "ctx")),
    )
    return jax.shard_map(
        body,
        mesh=mesh,
        in_specs=placed,
        out_specs=(
            P("fsdp", "ctx", None),
            P("fsdp", "ctx", None),
            P(("fsdp", "ctx"), "tp"),
            P(("fsdp", "ctx"), "tp"),
            P(("fsdp", "ctx"), "tp"),
            P("tp", ("fsdp", "ctx")),
            P(("fsdp", "ctx"), "tp"),
            P(("fsdp", "ctx"), "tp"),
            P("tp", ("fsdp", "ctx")),
            P(("fsdp", "ctx")),
            P(("fsdp", "ctx")),
        ),
        check_vma=False,
    )
```

time: 672 us -> 616 us (0.917)
  waiting for transfers between devices: 284 us -> 214 us
  starting transfers between devices: 120 us -> 73.5 us
  Pallas kernels: 26.5 us -> 70.6 us
  other arithmetic: 65.9 us -> 99.4 us
  matrix products: 98 us -> 68 us
  local copies, waits for them, and re-layouts: 54.4 us -> 69.3 us
    ppermute x33 -> x45, waiting for transfers between devices: 280 us -> 210 us  [the longest x14 91.3 us: halved(): return ([v[:half] for v in values], lax.ppermute(sent, 'tp', pairs))]
    ppermute x33 -> x45, starting transfers between devices: 116 us -> 66.9 us  [the longest x14 24.2 us: halved(): return ([v[:half] for v in values], lax.ppermute(sent, 'tp', pairs))]
    pallas_call x2 -> x10, Pallas kernels: 26.5 us -> 70.6 us  [the longest x3 25.8 us: grad_kernel(): pl.pallas_call(kernel, grid=(wide // block,), in_specs=[pl.BlockSpec((row...]
    dot_general x5 -> x3, matrix products: 33.8 us -> 8.16 us  [dot_0(): lax.dot_general(left, right, (((0,), (0,)), ((), ())), preferred_element_...]
    concatenate x9 -> x29, other arithmetic: 9.22 us -> 31.3 us  [the longest x20 23.9 us: stack(): return jnp.concatenate(parts, axis=0)]
    slice x10 -> x42, local copies, waits for them, and re-layouts: 4.13 us -> 19.3 us  [the longest x16 7.48 us: halved(): sent = jnp.concatenate([v[half:].astype(BF) for v in values], axis=0)]
    add x4 -> x19, other arithmetic: 0.06 us -> 14.3 us  [the longest x7 6.17 us: summed(): k.astype(F32) + got[n * half:(n + 1) * half].astype(F32)]
    dynamic_slice x1 -> x7, local copies, waits for them, and re-layouts: 0.05 us -> 8.53 us  [the longest x6 7.96 us: columns(): return lax.dynamic_index_in_dim(grad, which, 2, keepdims=False)]
  transfers between devices with their start and end apart: 59 -> 74, of which waited for: 20 -> 31; matrix products, arithmetic and copies ran while one was open for 26% -> 34% of each run, Pallas kernels for 4% -> 10%
where the time goes in v2:
time: 616 us; the launch traced here: 610 us
  waiting for transfers between devices  214 us (35%)
  other arithmetic  99.4 us (16%)
  starting transfers between devices  73.5 us (12%)
  Pallas kernels  70.6 us (11%)
  local copies, waits for them, and re-layouts  69.3 us (11%)
  matrix products  68 us (11%)
  between operations  15.9 us (3%)
    ppermute x14, waiting for transfers between devices, halved(): return ([v[:half] for v in values], lax.ppermute(sent, 'tp', pairs))  91.3 us
    dot_general x10, matrix products, dot_t(): lax.dot_general(left, right, (((1,), (1,)), ((), ())), preferred_element_...  31.7 us
    unnamed x181, local copies, waits for them, and re-layouts  28.6 us
    dot_general x9, matrix products, dotf(): return jnp.dot(left, right, preferred_element_type=F32)  28.1 us
    pallas_call x3, Pallas kernels, grad_kernel(): pl.pallas_call(kernel, grid=(wide // block,), in_specs=[pl.BlockSpec((row...  25.8 us
    ppermute x14, starting transfers between devices, halved(): return ([v[:half] for v in values], lax.ppermute(sent, 'tp', pairs))  24.2 us
    ppermute x3, waiting for transfers between devices, body(): a0 = lax.ppermute(c0, 'tp', far)  24 us
    concatenate x20, other arithmetic, stack(): return jnp.concatenate(parts, axis=0)  23.9 us
  transfers between devices with their start and end apart: 74, of which 31 were waited for; matrix products, arithmetic and copies ran while one was open for 34% of the time, Pallas kernels for 10%

profile of v2, /device:TPU:0, one launch (start us, length us, event | category | flops | bytes accessed | tf_op | source)
XLA Modules:
  0.0 610.4 jit_solution(8652013046236630675)
XLA Ops:
  26.8 3.4 broadcast_select_fusion.20
  30.2 9.3 %collective-permute-done.2 = bf16[544,384]{1,0:T(8,128)(2,1)S(1)} collective-permute-done((bf16[544,384]{1,0:T(8,128)(2,1)S(1)}, bf16[544,384]{1,0:T(8,128)(2,1)S(1)}, u32[]{:S(2)}, u32[]{:S(2)}) %collective-permute-start.2) | collective-permute-done | bytes 417824 | tf_op jit(solution)/shard_map/ppermute | solution.py:167
  39.5 3.3 collective-permute-done.1
  47.6 8.2 %collective-permute-done.4 = bf16[272,384]{1,0:T(8,128)(2,1)S(1)} collective-permute-done((bf16[272,384]{1,0:T(8,128)(2,1)S(1)}, bf16[272,384]{1,0:T(8,128)(2,1)S(1)}, u32[]{:S(2)}, u32[]{:S(2)}) %collective-permute-start.4) | collective-permute-done | bytes 208928 | tf_op jit(solution)/shard_map/ppermute | solution.py:178
  56.0 11.9 %collective-permute-done.3 = bf16[272,384]{1,0:T(8,128)(2,1)S(1)} collective-permute-done((bf16[272,384]{1,0:T(8,128)(2,1)S(1)}, bf16[272,384]{1,0:T(8,128)(2,1)S(1)}, u32[]{:S(2)}, u32[]{:S(2)}) %collective-permute-start.3) | collective-permute-done | bytes 208928 | tf_op jit(solution)/shard_map/ppermute | solution.py:177
  68.7 3.1 multiply_reduce_fusion
  75.7 3.5 fusion.qkv_ref
  81.4 5.8 collective-permute-done.8
  92.7 7.6 %attend_first.1 = (bf16[1024,256]{1,0:T(8,128)(2,1)}, bf16[1024,128]{1,0:T(8,128)(2,1)}, bf16[512,256]{1,0:T(8,128)(2,1)}, f32[512,4]{1,0:T(8,128)}) custom-call(s32[2]{0:T(128)} %pad_add_fusion.at_ref, f32[1024,384]{1,0:T(8,128)} %fusion.qkv_ref, f32[1024,128]{1,0:T(8,128)} %get-tuple-element.310.cos_ref, f32[1024,128]{1,0:T(8,128)} %get-tuple-element.308.sin_ref, ...), custom_call_target="tpu_custom_call" | custom-call | tf_op jit(solution)/shard_map/attend_first/pallas_call | solution.py:327
  102.5 5.4 attend_next.1
  124.8 8.5 %collective-permute-done.12 = bf16[128,2048]{1,0:T(8,128)(2,1)S(1)} collective-permute-done((bf16[128,2048]{1,0:T(8,128)(2,1)}, bf16[128,2048]{1,0:T(8,128)(2,1)S(1)}, u32[]{:S(2)}, u32[]{:S(2)}) %collective-permute-start.12) | collective-permute-done | bytes 524320 | tf_op jit(solution)/shard_map/ppermute | solution.py:67
  137.4 12.3 %collective-permute-done.15 = bf16[128,2048]{1,0:T(8,128)(2,1)S(1)} collective-permute-done((bf16[128,2048]{1,0:T(8,128)(2,1)}, bf16[128,2048]{1,0:T(8,128)(2,1)S(1)}, u32[]{:S(2)}, u32[]{:S(2)}) %collective-permute-start.15) | collective-permute-done | bytes 524320 | tf_op jit(solution)/shard_map/ppermute | solution.py:67
  154.2 3.8 arrange.3
  161.6 4.7 collective-permute-done.17
  167.9 9.6 %collective-permute-done.16 = bf16[64,2048]{1,0:T(8,128)(2,1)S(1)} collective-permute-done((bf16[64,2048]{1,0:T(8,128)(2,1)S(1)}, bf16[64,2048]{1,0:T(8,128)(2,1)S(1)}, u32[]{:S(2)}, u32[]{:S(2)}) %collective-permute-start.16) | collective-permute-done | bytes 262176 | tf_op jit(solution)/shard_map/ppermute | solution.py:566
  177.5 4.6 collective-permute-start.18
  182.2 5.5 collective-permute-done.19
  198.8 10.6 %fusion.106 = f32[512,2048]{1,0:T(8,128)} fusion(bf16[512,2048]{1,0:T(8,128)(2,1)} %constant_dynamic-update-slice_fusion.2.refs_0_, bf16[2048,2048]{1,0:T(8,128)(2,1)} %all-gather.3.cloned.1.call-done), kind=kOutput, calls=%fused_computation.368 | convolution fusion | flops 4294967296 | bytes 14680064 | tf_op jit(solution)/shard_map/dot_general | solution.py:18
  209.9 8.2 %multiply_convert_fusion.6 = (bf16[512,1024]{1,0:T(8,128)(2,1)S(1)}, bf16[512,1024]{1,0:T(8,128)(2,1)S(1)}, bf16[512,1024]{1,0:T(8,128)(2,1)}) fusion(f32[512,2048]{1,0:T(8,128)} %fusion.106, bf16[1024,2048]{1,0:T(8,128)(2,1)} %all-gather.5.cloned.1.call-done, bf16[256,2048]{1,0:T(8,128)(2,1)} %copy-done.21, bf16[256,2048]{1,0:T(8,128)(2,1)} %copy-done.20), kind=kOutput, calls=%fused_computation.45 | convolution fusion | flops 2159542272 | bytes 13631488 | tf_op jit(solution)/shard_map/dot_general | solution.py:22
  218.2 4.5 fusion.86
  227.3 4.8 fusion.107
  234.9 4.2 multiply_convert_fusion.3
  239.1 6.9 %fusion.85 = f32[512,2048]{1,0:T(8,128)S(1)} fusion(bf16[2048,2048]{1,0:T(8,128)(2,1)} %all-gather.3.cloned.1.call-done, bf16[512,1024]{1,0:T(8,128)(2,1)S(1)} %get-tuple-element.199, bf16[512,1024]{1,0:T(8,128)(2,1)S(1)} %get-tuple-element.198), kind=kOutput, calls=%fused_computation.349 | convolution fusion | flops 4299161600 | bytes 14680064 | tf_op jit(solution)/shard_map/dot_general | solution.py:22
  252.5 8.4 %grad.3 = bf16[2048,1024]{1,0:T(8,128)(2,1)} custom-call(bf16[512,2048]{1,0:T(8,128)(2,1)} %constant_dynamic-update-slice_fusion.2.refs_0_, bf16[512,2048]{1,0:T(8,128)(2,1)} %copy-done.4, bf16[512,2048]{1,0:T(8,128)(2,1)} %pad_maximum_fusion.7.refs_2_, bf16[512,2048]{1,0:T(8,128)(2,1)} %pad_maximum_fusion.8.refs_3_), custom_call_target="tpu_custom_call" | custom-call | tf_op jit(solution)/shard_map/grad/pallas_call | solution.py:214
  262.1 4.3 collective-permute-start.30
  267.8 11.0 %collective-permute-done.30 = bf16[64,2048]{1,0:T(8,128)(2,1)S(1)} collective-permute-done((bf16[64,2048]{1,0:T(8,128)(2,1)S(1)}, bf16[64,2048]{1,0:T(8,128)(2,1)S(1)}, u32[]{:S(2)}, u32[]{:S(2)}) %collective-permute-start.30) | collective-permute-done | bytes 262176 | tf_op jit(solution)/shard_map/ppermute | solution.py:67
  283.1 3.3 collective-permute-start.32
  286.4 11.5 %collective-permute-done.33 = bf16[128,2048]{1,0:T(8,128)(2,1)S(1)} collective-permute-done((bf16[128,2048]{1,0:T(8,128)(2,1)S(1)}, bf16[128,2048]{1,0:T(8,128)(2,1)S(1)}, u32[]{:S(2)}, u32[]{:S(2)}) %collective-permute-start.33) | collective-permute-done | bytes 524320 | tf_op jit(solution)/shard_map/ppermute | solution.py:67
  301.7 8.7 %grad.4 = bf16[2048,1024]{1,0:T(8,128)(2,1)} custom-call(bf16[512,2048]{1,0:T(8,128)(2,1)} %constant_dynamic-update-slice_fusion.2.refs_0_, bf16[512,2048]{1,0:T(8,128)(2,1)} %copy-done.4, bf16[512,2048]{1,0:T(8,128)(2,1)} %pad_maximum_fusion.7.refs_2_, bf16[512,2048]{1,0:T(8,128)(2,1)} %pad_maximum_fusion.8.refs_3_), custom_call_target="tpu_custom_call" | custom-call | tf_op jit(solution)/shard_map/grad/pallas_call | solution.py:214
  317.3 8.7 %grad.5 = bf16[1024,2048]{1,0:T(8,128)(2,1)} custom-call(bf16[512,1024]{1,0:T(8,128)(2,1)} %get-tuple-element.136.refs_0_, bf16[512,1024]{1,0:T(8,128)(2,1)} %get-tuple-element.137.refs_1_, bf16[512,2048]{1,0:T(8,128)(2,1)} %pad_maximum_fusion.4.refs_2_, bf16[512,2048]{1,0:T(8,128)(2,1)} %pad_maximum_fusion.5.refs_3_), custom_call_target="tpu_custom_call" | custom-call | tf_op jit(solution)/shard_map/grad/pallas_call | solution.py:214
  325.9 5.0 fusion.109
  343.9 14.4 %collective-permute-done.37 = bf16[128,2048]{1,0:T(8,128)(2,1)} collective-permute-done((bf16[128,2048]{1,0:T(8,128)(2,1)}, bf16[128,2048]{1,0:T(8,128)(2,1)}, u32[]{:S(2)}, u32[]{:S(2)}) %collective-permute-start.37) | collective-permute-done | bytes 524320 | tf_op jit(solution)/shard_map/ppermute | solution.py:633
  375.5 8.2 %attend_back.2 = (bf16[512,256]{1,0:T(8,128)(2,1)}, bf16[512,256]{1,0:T(8,128)(2,1)}, f32[2,1024,128]{2,1,0:T(8,128)}, f32[2,1024,128]{2,1,0:T(8,128)}) custom-call(s32[2]{0:T(128)} %pad_add_fusion.at_ref, bf16[1024,256]{1,0:T(8,128)(2,1)} %get-tuple-element.104.q_ref, bf16[1024,128]{1,0:T(8,128)(2,1)} %get-tuple-element.105.kv_ref, ...), custom_call_target="tpu_custom_call" | custom-call | tf_op jit(solution)/shard_map/attend_back/pallas_call | solution.py:439
  387.0 10.6 %collective-permute-done.38 = bf16[256,2048]{1,0:T(8,128)(2,1)} collective-permute-done((bf16[256,2048]{1,0:T(8,128)(2,1)}, bf16[256,2048]{1,0:T(8,128)(2,1)}, u32[]{:S(2)}, u32[]{:S(2)}) %collective-permute-start.38) | collective-permute-done | bytes 1048608 | tf_op jit(solution)/shard_map/ppermute | solution.py:67
  409.4 11.1 %attend_back.3 = (bf16[512,256]{1,0:T(8,128)(2,1)}, bf16[512,256]{1,0:T(8,128)(2,1)}, bf16[1024,128]{1,0:T(8,128)(2,1)}, bf16[1024,128]{1,0:T(8,128)(2,1)}) custom-call(s32[2]{0:T(128)} %pad_add_fusion.at_ref, bf16[1024,256]{1,0:T(8,128)(2,1)} %get-tuple-element.104.q_ref, bf16[1024,128]{1,0:T(8,128)(2,1)} %get-tuple-element.105.kv_ref, ...), custom_call_target="tpu_custom_call" | custom-call | tf_op jit(solution)/shard_map/attend_back/pallas_call | solution.py:439
  427.2 3.5 convolution_convert_fusion
  446.4 3.1 constant_dynamic-slice_fusion.7
  460.3 17.1 %collective-permute-done.47 = bf16[128,2048]{1,0:T(8,128)(2,1)} collective-permute-done((bf16[128,2048]{1,0:T(8,128)(2,1)}, bf16[128,2048]{1,0:T(8,128)(2,1)}, u32[]{:S(2)}, u32[]{:S(2)}) %collective-permute-start.47) | collective-permute-done | bytes 524320 | tf_op jit(solution)/shard_map/ppermute | solution.py:67
  478.7 11.1 %collective-permute-done.46 = bf16[128,2048]{1,0:T(8,128)(2,1)S(1)} collective-permute-done((bf16[128,2048]{1,0:T(8,128)(2,1)S(1)}, bf16[128,2048]{1,0:T(8,128)(2,1)S(1)}, u32[]{:S(2)}, u32[]{:S(2)}) %collective-permute-start.46) | collective-permute-done | bytes 524320 | tf_op jit(solution)/shard_map/ppermute | solution.py:67
  500.2 18.1 %collective-permute-done.52 = bf16[2,256,640]{2,1,0:T(8,128)(2,1)S(1)} collective-permute-done((bf16[2,256,640]{2,1,0:T(8,128)(2,1)S(1)}, bf16[2,256,640]{2,1,0:T(8,128)(2,1)S(1)}, u32[]{:S(2)}, u32[]{:S(2)}) %collective-permute-start.52) | collective-permute-done | bytes 655392 | tf_op jit(solution)/shard_map/ppermute | solution.py:131
  523.1 3.0 collective-permute-done.50
  526.7 3.5 collective-permute-start.54
  530.2 14.4 %collective-permute-done.55 = bf16[64,2048]{1,0:T(8,128)(2,1)S(1)} collective-permute-done((bf16[64,2048]{1,0:T(8,128)(2,1)S(1)}, bf16[64,2048]{1,0:T(8,128)(2,1)S(1)}, u32[]{:S(2)}, u32[]{:S(2)}) %collective-permute-start.55) | collective-permute-done | bytes 262176 | tf_op jit(solution)/shard_map/ppermute | solution.py:714
  545.5 4.3 collective-permute-done.54
  550.7 3.7 collective-permute-done.65
  554.6 4.6 collective-permute-done.66
  574.6 4.5 arrange.4
  591.6 4.3 arrange.5
  (502 shorter events, 244.1 us)
Async XLA Ops:
  7.2 191.6 %all-gather.3.cloned.1.call-start = ((), (), s32[]{:S(2)}) async-start(), calls=%async_computation.3 | async-start | bytes 10485760 | tf_op jit(solution)/shard_map/all_gather | solution.py:517
  17.7 192.2 %all-gather.5.cloned.1.call-start = ((), (), s32[]{:S(2)}) async-start(), calls=%async_computation.4 | async-start | bytes 5242880 | tf_op jit(solution)/shard_map/all_gather | solution.py:518
  17.7 51.0 %collective-permute-start.5 = (f32[512,2048]{1,0:T(8,128)}, f32[512,2048]{1,0:T(8,128)}, u32[]{:S(2)}, u32[]{:S(2)}) collective-permute-start(f32[512,2048]{1,0:T(8,128)} %bitcast.138), channel_id=1, source_target_pairs={{0,4},{4,0},{1,5},{5,1},{2,6},{6,2},{3,7},{7,3},{8,12},{12,8},{9,1... | collective-permute-start | bytes 12582920 | tf_op jit(solution)/shard_map/ppermute | solution.py:34
  22.4 17.1 %collective-permute-start.2 = (bf16[544,384]{1,0:T(8,128)(2,1)S(1)}, bf16[544,384]{1,0:T(8,128)(2,1)S(1)}, u32[]{:S(2)}, u32[]{:S(2)}) collective-permute-start(bf16[544,384]{1,0:T(8,128)(2,1)S(1)} %pad_maximum_fusion.37), channel_id=1, source_target_pairs={{0,16},{8,24},{16,0},{24,8},{1,17},{9,25},{17,1},{25,9},{2,18},{10... | collective-permute-start | bytes 1253384 | tf_op jit(solution)/shard_map/ppermute | solution.py:167
  25.3 17.5 %collective-permute-start.1 = (bf16[544,384]{1,0:T(8,128)(2,1)S(1)}, bf16[544,384]{1,0:T(8,128)(2,1)S(1)}, u32[]{:S(2)}, u32[]{:S(2)}) collective-permute-start(bf16[544,384]{1,0:T(8,128)(2,1)S(1)} %pad_maximum_fusion.37), channel_id=1, source_target_pairs={{0,8},{8,0},{16,24},{24,16},{1,9},{9,1},{17,25},{25,17},{2,10},{10... | collective-permute-start | bytes 1253384 | tf_op jit(solution)/shard_map/ppermute | solution.py:166
  45.4 33.8 %collective-permute-start.6 = (bf16[512,256]{1,0:T(8,128)(2,1)S(1)}, bf16[512,256]{1,0:T(8,128)(2,1)S(1)}, u32[]{:S(2)}, u32[]{:S(2)}) collective-permute-start(bf16[512,256]{1,0:T(8,128)(2,1)S(1)} %copy-done.75), channel_id=1, source_target_pairs={{0,8},{8,0},{16,24},{24,16},{1,9},{9,1},{17,25},{25,17},{2,10},{10... | collective-permute-start | bytes 786440 | tf_op jit(solution)/shard_map/ppermute | solution.py:166
  45.5 33.7 %collective-permute-start.7 = (bf16[512,256]{1,0:T(8,128)(2,1)S(1)}, bf16[512,256]{1,0:T(8,128)(2,1)S(1)}, u32[]{:S(2)}, u32[]{:S(2)}) collective-permute-start(bf16[512,256]{1,0:T(8,128)(2,1)S(1)} %copy-done.75), channel_id=1, source_target_pairs={{0,16},{8,24},{16,0},{24,8},{1,17},{9,25},{17,1},{25,9},{2,18},{10... | collective-permute-start | bytes 786440 | tf_op jit(solution)/shard_map/ppermute | solution.py:167
  45.6 22.3 %collective-permute-start.3 = (bf16[272,384]{1,0:T(8,128)(2,1)S(1)}, bf16[272,384]{1,0:T(8,128)(2,1)S(1)}, u32[]{:S(2)}, u32[]{:S(2)}) collective-permute-start(bf16[272,384]{1,0:T(8,128)(2,1)S(1)} %slice.414), channel_id=1, source_target_pairs={{0,16},{8,24},{16,0},{24,8},{1,17},{9,25},{17,1},{25,9},{2,18},{10... | collective-permute-start | bytes 626696 | tf_op jit(solution)/shard_map/ppermute | solution.py:177
  87.7 24.6 %collective-permute-start.10 = (bf16[512,1024]{1,0:T(8,128)(2,1)S(1)}, bf16[512,1024]{1,0:T(8,128)(2,1)}, u32[]{:S(2)}, u32[]{:S(2)}) collective-permute-start(bf16[512,1024]{1,0:T(8,128)(2,1)S(1)} %pad_maximum_fusion.11), channel_id=1, source_target_pairs={{0,4},{4,0},{1,5},{5,1},{2,6},{6,2},{3,7},{7,3},{8,12},{12,8},{9,1... | collective-permute-start | bytes 3145736 | tf_op jit(solution)/shard_map/ppermute | solution.py:34
  92.1 17.9 %collective-permute-start.27 = (bf16[1024,256]{1,0:T(8,128)(2,1)}, bf16[1024,256]{1,0:T(8,128)(2,1)}, u32[]{:S(2)}, u32[]{:S(2)}) collective-permute-start(bf16[1024,256]{1,0:T(8,128)(2,1)} %constant_dynamic-slice_fusion.9), channel_id=1, source_target_pairs={{0,4},{4,0},{1,5},{5,1},{2,6},{6,2},{3,7},{7,3},{8,12},{12,8},{9,1... | collective-permute-start | bytes 1572872 | tf_op jit(solution)/shard_map/ppermute | solution.py:34
  101.9 14.8 %collective-permute-start.11 = (bf16[256,256]{1,0:T(8,128)(2,1)}, bf16[256,256]{1,0:T(8,128)(2,1)S(1)}, u32[]{:S(2)}, u32[]{:S(2)}) collective-permute-start(bf16[256,256]{1,0:T(8,128)(2,1)} %get-tuple-element.274), channel_id=1, source_target_pairs={{0,4},{4,0},{1,5},{5,1},{2,6},{6,2},{3,7},{7,3},{8,12},{12,8},{9,1... | collective-permute-start | bytes 393224 | tf_op jit(solution)/shard_map/ppermute | solution.py:34
  118.3 15.0 %collective-permute-start.12 = (bf16[128,2048]{1,0:T(8,128)(2,1)}, bf16[128,2048]{1,0:T(8,128)(2,1)S(1)}, u32[]{:S(2)}, u32[]{:S(2)}) collective-permute-start(bf16[128,2048]{1,0:T(8,128)(2,1)} %slice.827), channel_id=1, source_target_pairs={{0,1},{1,0},{2,3},{3,2},{4,5},{5,4},{6,7},{7,6},{8,9},{9,8},{10,11... | collective-permute-start | bytes 1572872 | tf_op jit(solution)/shard_map/ppermute | solution.py:67
  123.0 26.6 %collective-permute-start.15 = (bf16[128,2048]{1,0:T(8,128)(2,1)}, bf16[128,2048]{1,0:T(8,128)(2,1)S(1)}, u32[]{:S(2)}, u32[]{:S(2)}) collective-permute-start(bf16[128,2048]{1,0:T(8,128)(2,1)} %slice.826), channel_id=1, source_target_pairs={{0,1},{1,0},{2,3},{3,2},{4,5},{5,4},{6,7},{7,6},{8,9},{9,8},{10,11... | collective-permute-start | bytes 1572872 | tf_op jit(solution)/shard_map/ppermute | solution.py:67
  124.7 461.4 %reduce-scatter.6.cloned.1.call-start = ((), (), s32[]{:S(2)}) async-start(), calls=%async_computation.6 | async-start | bytes 5242880 | tf_op jit(solution)/shard_map/reduce_scatter | solution.py:612
  134.8 23.2 %collective-permute-start.14 = (bf16[64,2048]{1,0:T(8,128)(2,1)S(1)}, bf16[64,2048]{1,0:T(8,128)(2,1)}, u32[]{:S(2)}, u32[]{:S(2)}) collective-permute-start(bf16[64,2048]{1,0:T(8,128)(2,1)S(1)} %slice.835), channel_id=1, source_target_pairs={{0,2},{1,3},{2,0},{3,1},{4,6},{5,7},{6,4},{7,5},{8,10},{9,11},{10,... | collective-permute-start | bytes 786440 | tf_op jit(solution)/shard_map/ppermute | solution.py:67
  150.8 15.5 %collective-permute-start.17 = (bf16[64,2048]{1,0:T(8,128)(2,1)S(1)}, bf16[64,2048]{1,0:T(8,128)(2,1)S(1)}, u32[]{:S(2)}, u32[]{:S(2)}) collective-permute-start(bf16[64,2048]{1,0:T(8,128)(2,1)S(1)} %slice.834), channel_id=1, source_target_pairs={{0,2},{1,3},{2,0},{3,1},{4,6},{5,7},{6,4},{7,5},{8,10},{9,11},{10,... | collective-permute-start | bytes 786440 | tf_op jit(solution)/shard_map/ppermute | solution.py:67
  158.0 31.3 %collective-permute-start.20 = (bf16[512,2048]{1,0:T(8,128)(2,1)}, bf16[512,2048]{1,0:T(8,128)(2,1)S(1)}, u32[]{:S(2)}, u32[]{:S(2)}) collective-permute-start(bf16[512,2048]{1,0:T(8,128)(2,1)} %arrange.3), channel_id=1, source_target_pairs={{0,4},{4,0},{1,5},{5,1},{2,6},{6,2},{3,7},{7,3},{8,12},{12,8},{9,1... | collective-permute-start | bytes 6291464 | tf_op jit(solution)/shard_map/ppermute | solution.py:34
  160.5 17.0 %collective-permute-start.16 = (bf16[64,2048]{1,0:T(8,128)(2,1)S(1)}, bf16[64,2048]{1,0:T(8,128)(2,1)S(1)}, u32[]{:S(2)}, u32[]{:S(2)}) collective-permute-start(bf16[64,2048]{1,0:T(8,128)(2,1)S(1)} %get-tuple-element.193), channel_id=1, source_target_pairs={{0,2},{1,3},{2,0},{3,1},{4,6},{5,7},{6,4},{7,5},{8,10},{9,11},{10,... | collective-permute-start | bytes 786440 | tf_op jit(solution)/shard_map/ppermute | solution.py:566
  167.7 20.0 %collective-permute-start.19 = (bf16[64,2048]{1,0:T(8,128)(2,1)S(1)}, bf16[64,2048]{1,0:T(8,128)(2,1)S(1)}, u32[]{:S(2)}, u32[]{:S(2)}) collective-permute-start(bf16[64,2048]{1,0:T(8,128)(2,1)S(1)} %multiply_convert_fusion.8), channel_id=1, source_target_pairs={{0,2},{1,3},{2,0},{3,1},{4,6},{5,7},{6,4},{7,5},{8,10},{9,11},{10,... | collective-permute-start | bytes 786440 | tf_op jit(solution)/shard_map/ppermute | solution.py:568
  177.5 18.0 %collective-permute-start.18 = (bf16[128,2048]{1,0:T(8,128)(2,1)S(1)}, bf16[128,2048]{1,0:T(8,128)(2,1)S(1)}, u32[]{:S(2)}, u32[]{:S(2)}) collective-permute-start(bf16[128,2048]{1,0:T(8,128)(2,1)S(1)} %pad_maximum_fusion.27), channel_id=1, source_target_pairs={{0,1},{1,0},{2,3},{3,2},{4,5},{5,4},{6,7},{7,6},{8,9},{9,8},{10,11... | collective-permute-start | bytes 1572872 | tf_op jit(solution)/shard_map/ppermute | solution.py:570
  182.2 14.9 %collective-permute-start.21 = (bf16[128,2048]{1,0:T(8,128)(2,1)S(1)}, bf16[128,2048]{1,0:T(8,128)(2,1)S(1)}, u32[]{:S(2)}, u32[]{:S(2)}) collective-permute-start(bf16[128,2048]{1,0:T(8,128)(2,1)S(1)} %pad_maximum_fusion.27), channel_id=1, source_target_pairs={{0,4},{4,0},{1,5},{5,1},{2,6},{6,2},{3,7},{7,3},{8,12},{12,8},{9,1... | collective-permute-start | bytes 1572872 | tf_op jit(solution)/shard_map/ppermute | solution.py:34
  188.5 20.9 %collective-permute-start.24 = (bf16[128,2048]{1,0:T(8,128)(2,1)}, bf16[128,2048]{1,0:T(8,128)(2,1)}, u32[]{:S(2)}, u32[]{:S(2)}) collective-permute-start(bf16[128,2048]{1,0:T(8,128)(2,1)} %pad_maximum_fusion.28), channel_id=1, source_target_pairs={{0,1},{1,0},{2,3},{3,2},{4,5},{5,4},{6,7},{7,6},{8,9},{9,8},{10,11... | collective-permute-start | bytes 1572872 | tf_op jit(solution)/shard_map/ppermute | solution.py:572
  189.3 33.6 %collective-permute-start.25 = (bf16[128,2048]{1,0:T(8,128)(2,1)}, bf16[128,2048]{1,0:T(8,128)(2,1)}, u32[]{:S(2)}, u32[]{:S(2)}) collective-permute-start(bf16[128,2048]{1,0:T(8,128)(2,1)} %pad_maximum_fusion.28), channel_id=1, source_target_pairs={{0,4},{4,0},{1,5},{5,1},{2,6},{6,2},{3,7},{7,3},{8,12},{12,8},{9,1... | collective-permute-start | bytes 1572872 | tf_op jit(solution)/shard_map/ppermute | solution.py:34
  232.5 17.2 %collective-permute-start.29 = (bf16[128,2048]{1,0:T(8,128)(2,1)S(1)}, bf16[128,2048]{1,0:T(8,128)(2,1)S(1)}, u32[]{:S(2)}, u32[]{:S(2)}) collective-permute-start(bf16[128,2048]{1,0:T(8,128)(2,1)S(1)} %slice.825), channel_id=1, source_target_pairs={{0,1},{1,0},{2,3},{3,2},{4,5},{5,4},{6,7},{7,6},{8,9},{9,8},{10,11... | collective-permute-start | bytes 1572872 | tf_op jit(solution)/shard_map/ppermute | solution.py:67
  260.9 325.2 %reduce-scatter.8.cloned.1.call-start = ((), (), s32[]{:S(2)}) async-start(), calls=%async_computation.7 | async-start | bytes 5242880 | tf_op jit(solution)/shard_map/reduce_scatter | solution.py:612
  262.1 16.7 %collective-permute-start.30 = (bf16[64,2048]{1,0:T(8,128)(2,1)S(1)}, bf16[64,2048]{1,0:T(8,128)(2,1)S(1)}, u32[]{:S(2)}, u32[]{:S(2)}) collective-permute-start(bf16[64,2048]{1,0:T(8,128)(2,1)S(1)} %slice.833), channel_id=1, source_target_pairs={{0,2},{1,3},{2,0},{3,1},{4,6},{5,7},{6,4},{7,5},{8,10},{9,11},{10,... | collective-permute-start | bytes 786440 | tf_op jit(solution)/shard_map/ppermute | solution.py:67
  278.8 19.1 %collective-permute-start.33 = (bf16[128,2048]{1,0:T(8,128)(2,1)S(1)}, bf16[128,2048]{1,0:T(8,128)(2,1)S(1)}, u32[]{:S(2)}, u32[]{:S(2)}) collective-permute-start(bf16[128,2048]{1,0:T(8,128)(2,1)S(1)} %slice.824), channel_id=1, source_target_pairs={{0,1},{1,0},{2,3},{3,2},{4,5},{5,4},{6,7},{7,6},{8,9},{9,8},{10,11... | collective-permute-start | bytes 1572872 | tf_op jit(solution)/shard_map/ppermute | solution.py:67
  283.1 27.3 %collective-permute-start.32 = (bf16[64,2048]{1,0:T(8,128)(2,1)S(1)}, bf16[64,2048]{1,0:T(8,128)(2,1)}, u32[]{:S(2)}, u32[]{:S(2)}) collective-permute-start(bf16[64,2048]{1,0:T(8,128)(2,1)S(1)} %get-tuple-element.188), channel_id=1, source_target_pairs={{0,2},{1,3},{2,0},{3,1},{4,6},{5,7},{6,4},{7,5},{8,10},{9,11},{10,... | collective-permute-start | bytes 786440 | tf_op jit(solution)/shard_map/ppermute | solution.py:628
  338.0 26.7 %collective-permute-start.35 = (bf16[512,2048]{1,0:T(8,128)(2,1)}, bf16[512,2048]{1,0:T(8,128)(2,1)}, u32[]{:S(2)}, u32[]{:S(2)}) collective-permute-start(bf16[512,2048]{1,0:T(8,128)(2,1)} %pad_maximum_fusion.9), channel_id=1, source_target_pairs={{0,4},{4,0},{1,5},{5,1},{2,6},{6,2},{3,7},{7,3},{8,12},{12,8},{9,1... | collective-permute-start | bytes 6291464 | tf_op jit(solution)/shard_map/ppermute | solution.py:34
  338.0 20.3 %collective-permute-start.37 = (bf16[128,2048]{1,0:T(8,128)(2,1)}, bf16[128,2048]{1,0:T(8,128)(2,1)}, u32[]{:S(2)}, u32[]{:S(2)}) collective-permute-start(bf16[128,2048]{1,0:T(8,128)(2,1)} %pad_maximum_fusion.29), channel_id=1, source_target_pairs={{0,1},{1,0},{2,3},{3,2},{4,5},{5,4},{6,7},{7,6},{8,9},{9,8},{10,11... | collective-permute-start | bytes 1572872 | tf_op jit(solution)/shard_map/ppermute | solution.py:633
  339.5 20.1 %collective-permute-start.36 = (bf16[64,2048]{1,0:T(8,128)(2,1)S(1)}, bf16[64,2048]{1,0:T(8,128)(2,1)}, u32[]{:S(2)}, u32[]{:S(2)}) collective-permute-start(bf16[64,2048]{1,0:T(8,128)(2,1)S(1)} %get-tuple-element.190), channel_id=1, source_target_pairs={{0,2},{1,3},{2,0},{3,1},{4,6},{5,7},{6,4},{7,5},{8,10},{9,11},{10,... | collective-permute-start | bytes 786440 | tf_op jit(solution)/shard_map/ppermute | solution.py:635
  343.4 242.7 %reduce-scatter.4.cloned.1.call-start = ((), (), s32[]{:S(2)}) async-start(), calls=%async_computation.5 | async-start | bytes 5242880 | tf_op jit(solution)/shard_map/reduce_scatter | solution.py:612
  361.4 41.6 %collective-permute-start.41 = (bf16[128,2048]{1,0:T(8,128)(2,1)}, bf16[128,2048]{1,0:T(8,128)(2,1)}, u32[]{:S(2)}, u32[]{:S(2)}) collective-permute-start(bf16[128,2048]{1,0:T(8,128)(2,1)} %pad_maximum_fusion.30), channel_id=1, source_target_pairs={{0,1},{1,0},{2,3},{3,2},{4,5},{5,4},{6,7},{7,6},{8,9},{9,8},{10,11... | collective-permute-start | bytes 1572872 | tf_op jit(solution)/shard_map/ppermute | solution.py:643
  370.0 27.6 %collective-permute-start.38 = (bf16[256,2048]{1,0:T(8,128)(2,1)}, bf16[256,2048]{1,0:T(8,128)(2,1)}, u32[]{:S(2)}, u32[]{:S(2)}) collective-permute-start(bf16[256,2048]{1,0:T(8,128)(2,1)} %pad_maximum_fusion.16), channel_id=1, source_target_pairs={{0,1},{1,0},{2,3},{3,2},{4,5},{5,4},{6,7},{7,6},{8,9},{9,8},{10,11... | collective-permute-start | bytes 3145736 | tf_op jit(solution)/shard_map/ppermute | solution.py:67
  400.9 33.0 %collective-permute-start.40 = (bf16[128,2048]{1,0:T(8,128)(2,1)}, bf16[128,2048]{1,0:T(8,128)(2,1)}, u32[]{:S(2)}, u32[]{:S(2)}) collective-permute-start(bf16[128,2048]{1,0:T(8,128)(2,1)} %pad_maximum_fusion.31), channel_id=1, source_target_pairs={{0,2},{1,3},{2,0},{3,1},{4,6},{5,7},{6,4},{7,5},{8,10},{9,11},{10,... | collective-permute-start | bytes 1572872 | tf_op jit(solution)/shard_map/ppermute | solution.py:67
  453.3 24.2 %collective-permute-start.47 = (bf16[128,2048]{1,0:T(8,128)(2,1)}, bf16[128,2048]{1,0:T(8,128)(2,1)}, u32[]{:S(2)}, u32[]{:S(2)}) collective-permute-start(bf16[128,2048]{1,0:T(8,128)(2,1)} %slice.820), channel_id=1, source_target_pairs={{0,1},{1,0},{2,3},{3,2},{4,5},{5,4},{6,7},{7,6},{8,9},{9,8},{10,11... | collective-permute-start | bytes 1572872 | tf_op jit(solution)/shard_map/ppermute | solution.py:67
  455.2 34.8 %collective-permute-start.45 = (bf16[128,2048]{1,0:T(8,128)(2,1)}, bf16[128,2048]{1,0:T(8,128)(2,1)S(1)}, u32[]{:S(2)}, u32[]{:S(2)}) collective-permute-start(bf16[128,2048]{1,0:T(8,128)(2,1)} %pad_maximum_fusion.32), channel_id=1, source_target_pairs={{0,2},{1,3},{2,0},{3,1},{4,6},{5,7},{6,4},{7,5},{8,10},{9,11},{10,... | collective-permute-start | bytes 1572872 | tf_op jit(solution)/shard_map/ppermute | solution.py:680
  456.8 33.0 %collective-permute-start.46 = (bf16[128,2048]{1,0:T(8,128)(2,1)S(1)}, bf16[128,2048]{1,0:T(8,128)(2,1)S(1)}, u32[]{:S(2)}, u32[]{:S(2)}) collective-permute-start(bf16[128,2048]{1,0:T(8,128)(2,1)S(1)} %slice.821), channel_id=1, source_target_pairs={{0,1},{1,0},{2,3},{3,2},{4,5},{5,4},{6,7},{7,6},{8,9},{9,8},{10,11... | collective-permute-start | bytes 1572872 | tf_op jit(solution)/shard_map/ppermute | solution.py:67
  490.0 30.1 %collective-permute-start.51 = (bf16[64,2048]{1,0:T(8,128)(2,1)S(1)}, bf16[64,2048]{1,0:T(8,128)(2,1)S(1)}, u32[]{:S(2)}, u32[]{:S(2)}) collective-permute-start(bf16[64,2048]{1,0:T(8,128)(2,1)S(1)} %slice.828), channel_id=1, source_target_pairs={{0,2},{1,3},{2,0},{3,1},{4,6},{5,7},{6,4},{7,5},{8,10},{9,11},{10,... | collective-permute-start | bytes 786440 | tf_op jit(solution)/shard_map/ppermute | solution.py:67
  491.5 26.8 %collective-permute-start.52 = (bf16[2,256,640]{2,1,0:T(8,128)(2,1)S(1)}, bf16[2,256,640]{2,1,0:T(8,128)(2,1)S(1)}, u32[]{:S(2)}, u32[]{:S(2)}) collective-permute-start(bf16[2,256,640]{2,1,0:T(8,128)(2,1)S(1)} %pad_maximum_fusion.25), channel_id=1, source_target_pairs={{0,8},{8,0},{16,24},{24,16},{1,9},{9,1},{17,25},{25,17},{2,10},{10... | collective-permute-start | bytes 1966088 | tf_op jit(solution)/shard_map/ppermute | solution.py:131
  493.4 25.8 %collective-permute-start.53 = (bf16[2,256,640]{2,1,0:T(8,128)(2,1)S(1)}, bf16[2,256,640]{2,1,0:T(8,128)(2,1)S(1)}, u32[]{:S(2)}, u32[]{:S(2)}) collective-permute-start(bf16[2,256,640]{2,1,0:T(8,128)(2,1)S(1)} %pad_maximum_fusion.26), channel_id=1, source_target_pairs={{0,16},{8,24},{16,0},{24,8},{1,17},{9,25},{17,1},{25,9},{2,18},{10... | collective-permute-start | bytes 1966088 | tf_op jit(solution)/shard_map/ppermute | solution.py:132
  496.4 73.8 %collective-permute-start.49 = (bf16[256,2048]{1,0:T(8,128)(2,1)}, bf16[256,2048]{1,0:T(8,128)(2,1)}, u32[]{:S(2)}, u32[]{:S(2)}) collective-permute-start(bf16[256,2048]{1,0:T(8,128)(2,1)} %pad_maximum_fusion.19), channel_id=1, source_target_pairs={{0,1},{1,0},{2,3},{3,2},{4,5},{5,4},{6,7},{7,6},{8,9},{9,8},{10,11... | collective-permute-start | bytes 3145736 | tf_op jit(solution)/shard_map/ppermute | solution.py:705
  497.5 28.6 %collective-permute-start.50 = (bf16[64,2048]{1,0:T(8,128)(2,1)S(1)}, bf16[64,2048]{1,0:T(8,128)(2,1)S(1)}, u32[]{:S(2)}, u32[]{:S(2)}) collective-permute-start(bf16[64,2048]{1,0:T(8,128)(2,1)S(1)} %slice.829), channel_id=1, source_target_pairs={{0,2},{1,3},{2,0},{3,1},{4,6},{5,7},{6,4},{7,5},{8,10},{9,11},{10,... | collective-permute-start | bytes 786440 | tf_op jit(solution)/shard_map/ppermute | solution.py:67
  520.6 24.0 %collective-permute-start.55 = (bf16[64,2048]{1,0:T(8,128)(2,1)S(1)}, bf16[64,2048]{1,0:T(8,128)(2,1)S(1)}, u32[]{:S(2)}, u32[]{:S(2)}) collective-permute-start(bf16[64,2048]{1,0:T(8,128)(2,1)S(1)} %fusion.32), channel_id=1, source_target_pairs={{0,2},{1,3},{2,0},{3,1},{4,6},{5,7},{6,4},{7,5},{8,10},{9,11},{10,... | collective-permute-start | bytes 786440 | tf_op jit(solution)/shard_map/ppermute | solution.py:714
  526.7 23.2 %collective-permute-start.54 = (bf16[64,2048]{1,0:T(8,128)(2,1)S(1)}, bf16[64,2048]{1,0:T(8,128)(2,1)S(1)}, u32[]{:S(2)}, u32[]{:S(2)}) collective-permute-start(bf16[64,2048]{1,0:T(8,128)(2,1)S(1)} %fusion.25), channel_id=1, source_target_pairs={{0,2},{1,3},{2,0},{3,1},{4,6},{5,7},{6,4},{7,5},{8,10},{9,11},{10,... | collective-permute-start | bytes 786440 | tf_op jit(solution)/shard_map/ppermute | solution.py:716
  560.8 18.3 %collective-permute-start.60 = (bf16[256,640]{1,0:T(8,128)(2,1)}, bf16[256,640]{1,0:T(8,128)(2,1)}, u32[]{:S(2)}, u32[]{:S(2)}) collective-permute-start(bf16[256,640]{1,0:T(8,128)(2,1)} %fusion.52), channel_id=1, source_target_pairs={{0,8},{8,0},{16,24},{24,16},{1,9},{9,1},{17,25},{25,17},{2,10},{10... | collective-permute-start | bytes 983048 | tf_op jit(solution)/shard_map/ppermute | solution.py:146
  567.0 20.4 %collective-permute-start.57 = (bf16[128,2048]{1,0:T(8,128)(2,1)}, bf16[128,2048]{1,0:T(8,128)(2,1)}, u32[]{:S(2)}, u32[]{:S(2)}) collective-permute-start(bf16[128,2048]{1,0:T(8,128)(2,1)} %pad_maximum_fusion.33), channel_id=1, source_target_pairs={{0,1},{1,0},{2,3},{3,2},{4,5},{5,4},{6,7},{7,6},{8,9},{9,8},{10,11... | collective-permute-start | bytes 1572872 | tf_op jit(solution)/shard_map/ppermute | solution.py:719
  567.2 22.4 %collective-permute-start.58 = (bf16[128,2048]{1,0:T(8,128)(2,1)}, bf16[128,2048]{1,0:T(8,128)(2,1)}, u32[]{:S(2)}, u32[]{:S(2)}) collective-permute-start(bf16[128,2048]{1,0:T(8,128)(2,1)} %pad_maximum_fusion.34), channel_id=1, source_target_pairs={{0,1},{1,0},{2,3},{3,2},{4,5},{5,4},{6,7},{7,6},{8,9},{9,8},{10,11... | collective-permute-start | bytes 1572872 | tf_op jit(solution)/shard_map/ppermute | solution.py:721
  (110 other events, 759.3 us)
Sparse Core Ops, SparseCore 0:
  17.8 107.4 all-gather.2
  127.7 52.4 all-gather.4
  261.0 56.9 reduce-scatter.5
  343.6 51.3 reduce-scatter.7
  455.3 62.3 reduce-scatter.3

commit v3 on v2

--- a/solution.py
+++ b/solution.py
@@ -12,6 +12,7 @@
 BF = jnp.bfloat16
 F32 = jnp.float32
 BLOCK = 256
+SLOW = 2
 
 
 def dotf(left, right):
@@ -24,6 +25,11 @@
 
 def dot_0(left, right):
     return lax.dot_general(left, right, (((0,), (0,)), ((), ())), preferred_element_type=F32)
+
+
+def cost(flops, *arrays):
+    size = sum(a.size * jnp.dtype(a.dtype).itemsize for a in arrays)
+    return pl.CostEstimate(flops=int(flops), bytes_accessed=int(size), transcendentals=0)
 
 
 def after(value, *others):
@@ -64,7 +70,7 @@
 def halved(values, pairs):
     half = values[0].shape[0] // 2
     sent = jnp.concatenate([v[half:].astype(BF) for v in values], axis=0)
-    return [v[:half] for v in values], lax.ppermute(sent, "tp", pairs)
+    return [v[:half] for v in values], lax.ppermute(sent, "tp", pairs), sent
 
 
 def summed(kept, got):
@@ -72,6 +78,13 @@
     return [
         k.astype(F32) + got[n * half : (n + 1) * half].astype(F32) for n, k in enumerate(kept)
     ]
+
+
+def across(value, *gate):
+    near, far = near_far()
+    value = after(value, *gate) if gate else value
+    both = jnp.concatenate([value, lax.ppermute(value, "tp", far)], axis=0)
+    return jnp.concatenate([both, lax.ppermute(both, "tp", near)], axis=0)
 
 
 def position(index, place, count):
@@ -112,6 +125,7 @@
             out_specs=pl.BlockSpec((rows * len(parts), columns), lambda i, at: (0, i)),
         ),
         out_shape=jax.ShapeDtypeStruct((rows * len(parts), width), kind),
+        cost_estimate=cost(0, *parts, *parts),
         name="arrange",
     )(place_at, *parts)
 
@@ -121,6 +135,7 @@
         self.plain = grad.shape[0] != 4
         if self.plain:
             self.whole = lax.psum_scatter(grad, "fsdp", scatter_dimension=0, tiled=False)
+            self.first_sent = grad
             return
         me = lax.axis_index("fsdp")
         cut = grad.shape[1] // 32 * 16
@@ -128,8 +143,11 @@
         self.top, self.low = slice(0, cut), slice(cut, None)
         self.blocks = [lax.dynamic_index_in_dim(grad, me ^ k, 0, keepdims=False) for k in range(4)]
         one, two, three = self.blocks[1:]
-        self.by_near = lax.ppermute(jnp.stack([one[self.top], three[self.top]]), "fsdp", self.near)
-        self.by_far = lax.ppermute(jnp.stack([two[self.low], three[self.low]]), "fsdp", self.far)
+        to_near = jnp.stack([one[self.top], three[self.top]])
+        to_far = jnp.stack([two[self.low], three[self.low]])
+        self.first_sent = to_far + to_near
+        self.by_near = lax.ppermute(to_near, "fsdp", self.near)
+        self.by_far = lax.ppermute(to_far, "fsdp", self.far)
 
     def second(self, *gate):
         if self.plain:
@@ -196,9 +214,13 @@
     )
 
 
-def sum_steps(value, steps):
-    for axis, bit in steps:
-        value = value + lax.ppermute(value, axis, xor_pairs(axis, bit))
+def sum_direct(value, axis, gate):
+    if lax.axis_size(axis) > 4:
+        return lax.psum(value, axis)
+    got = [lax.ppermute(value, axis, xor_pairs(axis, d)) for d in range(1, lax.axis_size(axis))]
+    got = lax.optimization_barrier((*got, gate))[:-1]
+    for item in got:
+        value = value + item
     return value
 
 
@@ -218,8 +240,55 @@
         + [pl.BlockSpec((rows, columns), lambda i: (0, column)) for _ in rights],
         out_specs=pl.BlockSpec((block, columns), lambda i: (i, 0)),
         out_shape=jax.ShapeDtypeStruct((wide, columns), BF),
+        cost_estimate=cost(SLOW * 2 * len(lefts) * rows * wide * columns, *lefts, *rights),
         name="grad",
     )(*lefts, *rights)
+
+
+def output_grad(core_at, mine, theirs, dh, shard, fsdp):
+    span, wide = mine[0].shape
+    if shard % 128:
+        grads = []
+        for side in (mine, theirs):
+            grad = dot_0(jnp.concatenate(side, axis=0), dh).astype(BF).reshape(wide, fsdp, 2, shard)
+            grads.append(grad.transpose(1, 0, 2, 3))
+
+        def columns(grad, which):
+            return lax.dynamic_index_in_dim(grad, which, 2, keepdims=False)
+
+        return (
+            jnp.concatenate([columns(g, core_at[0]) for g in grads], axis=1),
+            jnp.concatenate([columns(g, 1 - core_at[0]) for g in grads[::-1]], axis=1),
+        )
+
+    def kernel(core_ref, *refs):
+        chunks = len(mine)
+        keep, send = refs[2 * chunks : 2 * chunks + 2]
+        for dh_ref, out_ref, order in ((keep, refs[-2], (0, 1)), (send, refs[-1], (1, 0))):
+            for n, side in enumerate(order):
+                lefts = refs[side * chunks : (side + 1) * chunks]
+                total = dot_0(lefts[0][...], dh_ref[:span])
+                for h in range(1, chunks):
+                    total = total + dot_0(lefts[h][...], dh_ref[h * span : (h + 1) * span])
+                out_ref[0, n * wide : (n + 1) * wide, :] = total.astype(BF)
+
+    part = pl.BlockSpec((1, 2 * wide, shard), lambda f, core: (f, 0, 0))
+    return pl.pallas_call(
+        kernel,
+        grid_spec=pltpu.PrefetchScalarGridSpec(
+            num_scalar_prefetch=1,
+            grid=(fsdp,),
+            in_specs=[pl.BlockSpec((span, wide), lambda f, core: (0, 0))] * (2 * len(mine))
+            + [
+                pl.BlockSpec((dh.shape[0], shard), lambda f, core: (0, 2 * f + core[0])),
+                pl.BlockSpec((dh.shape[0], shard), lambda f, core: (0, 2 * f + 1 - core[0])),
+            ],
+            out_specs=(part, part),
+        ),
+        out_shape=(jax.ShapeDtypeStruct((fsdp, 2 * wide, shard), BF),) * 2,
+        cost_estimate=cost(SLOW * 4 * dh.size * wide, dh, dh, dh),
+        name="output_grad",
+    )(core_at, *mine, *theirs, dh, dh)
 
 
 def halves_swapped(tile):
@@ -333,6 +402,7 @@
             jax.ShapeDtypeStruct((rows, width), BF),
             jax.ShapeDtypeStruct((rows, width // HD), F32),
         ),
+        cost_estimate=cost(SLOW * 4e9, qkv),
         name="attend_first",
     )(at, qkv, *tables)
 
@@ -352,6 +422,7 @@
             jax.ShapeDtypeStruct((rows, width), BF),
             jax.ShapeDtypeStruct((rows, width // HD), F32),
         ),
+        cost_estimate=cost(SLOW * 2.5e9, queries),
         name="attend_next",
     )(at, queries, kv)
 
@@ -441,6 +512,7 @@
         in_specs=[SCALARS] + [pl.BlockSpec()] * (10 + 2 * last),
         out_shape=tuple(shapes),
         scratch_shapes=[pltpu.VMEM(*s) for s in sums] if last else [],
+        cost_estimate=cost(SLOW * 4e9, queries, queries),
         name="attend_back",
     )(at, queries, kv, out, *grads, lse, *tables, *(carried or ()))
 
@@ -504,27 +576,30 @@
         return jnp.concatenate([half_of(w_gate, which, 1), half_of(w_up, which, 1)], axis=1)
 
     qkv_mine, qkv_got = packed(core), swap(packed(other))
-    gu_got = swap(after(packed_gu(other), qkv_got))
-    rows_theirs = swap(after(rows, qkv_got))
-    wd_got = swap(after(half_of(w_down, other, 0), rows_theirs))
-    get_qkv = Gather(
-        stack(
-            pair(qkv_mine[:shard], qkv_got[:shard], core, 0), pair(qkv_mine[shard:], qkv_got[shard:], core, 0)
-        )
-    )
+    qkv_shard = stack(
+        pair(qkv_mine[:shard], qkv_got[:shard], core, 0), pair(qkv_mine[shard:], qkv_got[shard:], core, 0)
+    )
+    get_qkv = Gather(qkv_shard)
     get_wo = Gather(w_output, 1)
     t_qkv = get_qkv.first()
-    w_gu = lax.all_gather(pair(packed_gu(core), gu_got, core, 0), "fsdp", axis=0, tiled=True)
-    wd = lax.all_gather(
-        pair(half_of(w_down, core, 0), wd_got, core, 1), "fsdp", axis=1, tiled=True
-    )
+    gu_got = swap(after(packed_gu(other), qkv_shard))
+    gu_shard = pair(packed_gu(core), gu_got, core, 0)
+    rows_theirs = swap(after(rows, gu_shard))
+    wd_got = swap(after(half_of(w_down, other, 0), rows_theirs))
+    wd_shard = pair(half_of(w_down, core, 0), wd_got, core, 1)
+    w_gu = lax.all_gather(gu_shard, "fsdp", axis=0, tiled=True)
+    wd = lax.all_gather(wd_shard, "fsdp", axis=1, tiled=True)
     scale_own, scale_theirs = inverse_rms(rows), inverse_rms(rows_theirs)
     tables = rotary_tables(2 * local)
-    qkv_pieces = get_qkv.second(scale_own)
-    t_wo = get_wo.first(t_qkv)
+    cot_gated = after(cot.astype(BF), rows_theirs)
+    cot_own = arrange([cot_gated[h * span : (h + 1) * span] for h in range(CHUNKS)], place_at, BF, False)
+    cot_theirs = swap(cot_own)
+    qkv_pieces = get_qkv.second(scale_own, scale_theirs, cot_own)
     w_qkv = in_order(qkv_pieces, 0, slice(0, 2 * shard))
     gain_all = in_order(qkv_pieces, 0, slice(2 * shard, None)).reshape(-1, lines * narrow)
-    w_qkv, gain_all = lax.optimization_barrier((w_qkv, gain_all, scale_theirs) + tuple(tables))[:2]
+    w_qkv, gain_all = lax.optimization_barrier((w_qkv, gain_all, wd_shard) + tuple(tables))[:2]
+    get_wo.first(gain_all)
+    wo_column = across(w_output, gain_all)
     gain_a = gain_all[:, :shard].reshape(-1).astype(F32)
     gain_f = gain_all[:, shard : 2 * shard].reshape(-1).astype(F32)
 
@@ -534,6 +609,8 @@
     qkv = dotf(normed, w_qkv)
     blocks = [[h * span // BLOCK, h * span // BLOCK + local // BLOCK] for h in range(CHUNKS)]
     queries, kv, attn_0, lse_0 = attend_first(where, qkv, tables, blocks[0], count)
+    kv = after(kv, wo_column)
+    wo_all = lax.all_gather(after(wo_column, wd), ("fsdp", "ctx"), axis=1, tiled=True)
 
     wo_mine = in_order(get_wo.second(qkv), 1)
     wo_theirs = swap(wo_mine)
@@ -549,20 +626,21 @@
     attn_1, lse_1 = attend_next(where, queries, kv, blocks[1], count)
     attn, lse = [attn_0, attn_1], [lse_0, lse_1]
     attn_own = [(a[:span], swap(a[span:])) for a in attn]
-    partial = [dotf(mine, wo_a) + dotf(theirs, wo_b) for mine, theirs in attn_own]
+    partial = [dotf(attn_own[0][0], wo_a) + dotf(attn_own[0][1], wo_b)]
 
     def hidden_of(h, total):
         hidden = slice_of(rows, h) + total
         scale = inverse_rms(hidden)
         return hidden, scale, (hidden * scale * gain_f).astype(BF)
 
-    k0, g0 = halved([partial[0]], near)
-    k1, g1 = halved([partial[1]], near)
-    v0 = summed(k0, after(g0, partial[1]))
-    k0, g0 = halved(v0, far)
-    v1 = summed(k1, after(g1, v0[0]))
-    k1, g1 = halved(v1, far)
-    hidden_0, scale_0, c0 = hidden_of(0, summed(k0, after(g0, v1[0]))[0])
+    k0, g0, t0 = halved([partial[0]], near)
+    partial.append(dotf(after(attn_own[1][0], t0), wo_a) + dotf(attn_own[1][1], wo_b))
+    k1, g1, t1 = halved([partial[1]], near)
+    v0 = summed(k0, after(g0, t1))
+    k0, g0, t0 = halved(v0, far)
+    v1 = summed(k1, after(g1, t0))
+    k1, g1, t1 = halved(v1, far)
+    hidden_0, scale_0, c0 = hidden_of(0, summed(k0, after(g0, t1))[0])
     a0 = lax.ppermute(c0, "tp", far)
     hidden_1, scale_1, c1 = hidden_of(1, summed(k1, after(g1, c0))[0])
     a1 = lax.ppermute(c1, "tp", far)
@@ -571,9 +649,6 @@
     cur1 = stack(c1, after(a1, cur0))
     b1, s1 = lax.ppermute(cur1, "tp", near), swap(cur1)
 
-    cot_gated = after(cot.astype(BF), v1[0])
-    cot_own = arrange([cot_gated[h * span : (h + 1) * span] for h in range(CHUNKS)], place_at, BF, False)
-    cot_theirs = swap(cot_own)
     cots = [
         stack(cot_own[h * span : (h + 1) * span], cot_theirs[h * span : (h + 1) * span])
         for h in range(CHUNKS)
@@ -599,14 +674,14 @@
     hnorm_1 = stack(cur1, b1, s1, s_b1)
     gu_1 = dotf(hnorm_1, w_gu)
     d0 = d_full_0[:span] + after(s0, gu_1).astype(F32)
-    k0, g0 = halved([d0], near)
-    inner_1, d_gu_1 = backward_of(gu_1, dot_t(after(cots[1], d0), wd))
-    d_full_1 = dot_t(d_gu_1, w_gu)
+    k0, g0, t0 = halved([d0], near)
+    inner_1, d_gu_1 = backward_of(gu_1, dot_t(after(cots[1], t0), wd))
+    v0 = summed(k0, after(g0, d_gu_1))
+    k0, g0, t0 = halved(v0, far)
+    d_full_1 = dot_t(after(d_gu_1, t0), w_gu)
     s1 = swap(d_full_1[span:].astype(BF))
-    v0 = summed(k0, after(g0, d_full_1))
-    k0, g0 = halved(v0, far)
-    d1 = d_full_1[:span] + after(s1, v0[0]).astype(F32)
-    k1, g1 = halved([d1], near)
+    d1 = d_full_1[:span] + s1.astype(F32)
+    k1, g1, t1 = halved([d1], near)
 
     def reduced(grad, axis):
         return lax.psum_scatter(grad, "fsdp", scatter_dimension=axis, tiled=True)
@@ -617,48 +692,49 @@
         return grad_kernel(lefts, rights, column, units if column is not None else width, 512)
 
     d_gu, inner, hnorm = [d_gu_0, d_gu_1], [inner_0, inner_1], [hnorm_0, hnorm_1]
-    g_gate = gradient(hnorm, d_gu, 0, v0[0], d1)
-
     def back_of(h, hidden, scale, total):
         d_norm, gain = norm_backward(hidden, scale, gain_f, total)
         d_hidden = slice_of(cot, h) + d_norm
         return d_hidden, gain, d_hidden.astype(BF)
 
-    dh_0, gain_0, c0 = back_of(0, hidden_0, scale_0, summed(k0, after(g0, g_gate))[0])
-    a0 = lax.ppermute(c0, "tp", far)
-    v1 = summed(k1, after(g1, c0))
-    k1, g1 = halved(v1, far)
-    g_up = gradient(hnorm, d_gu, 1, c0, v1[0])
-    cur0 = stack(c0, after(a0, g_up))
-    b0 = lax.ppermute(cur0, "tp", near)
-    dh_1, gain_1, c1 = back_of(1, hidden_1, scale_1, summed(k1, after(g1, cur0))[0])
-    a1 = lax.ppermute(c1, "tp", far)
+    heads = w_output.shape[0]
+
+    def to_heads(piece):
+        blocks = [piece[:, n * heads : (n + 1) * heads] for n in range(count)]
+        distances = [0, 2, 1, 3]
+        return blocks[:1] + [
+            lax.ppermute(b, "tp", xor_pairs("tp", d)) for b, d in zip(blocks[1:], distances[1:])
+        ]
+
+    def grads_of(pieces, *gate):
+        pieces = lax.optimization_barrier(tuple(pieces) + gate)[: len(pieces)]
+        full = stack(*pieces)
+        return half_of(full, core, 1), swap(half_of(full, other, 1))
+
+    dh_0, gain_0, c0 = back_of(0, hidden_0, scale_0, summed(k0, after(g0, t1))[0])
+    p0 = dot_t(c0, wo_all).astype(BF)
+    x0 = to_heads(p0)
+    g_gate = gradient(hnorm, d_gu, 0, *x0[:1], p0)
+    v1 = summed(k1, after(g1, g_gate))
+    k1, g1, t1 = halved(v1, far)
+    g_up = gradient(hnorm, d_gu, 1, t1)
+    dh_1, gain_1, c1 = back_of(1, hidden_1, scale_1, summed(k1, after(g1, g_up))[0])
+    p1 = dot_t(c1, wo_all).astype(BF)
+    x1 = to_heads(p1)
     g_ffn = gain_0 + gain_1
-    g_down = grad_kernel(inner, lax.optimization_barrier(tuple(cots) + (cur0, c1))[:2], 0, width, 512)
-    down = [dotf(after(i, g_down), wd) for i in inner]
-    s_down = swap(stack(*[d[span:].astype(BF) for d in down]))
-    r_gate, r_up, r_down = reduced(g_gate, 0), reduced(g_up, 0), reduced(g_down, 1)
-    full_0 = stack(cur0, after(b0, *down))
-    cur1 = stack(c1, after(a1, full_0))
-    b1 = lax.ppermute(cur1, "tp", near)
-    down = [
-        d[:span] + after(s_down, cur1)[n * span : (n + 1) * span].astype(F32) for n, d in enumerate(down)
-    ]
-    k_out, g_out = halved(down, near)
-
-    def grads_of(full):
-        send = swap(dot_t(full, wo_b).astype(BF))
-        return dot_t(full, wo_a).astype(BF), send
-
+    c_dh = after(stack(c0, c1), p1)
+    a_dh = lax.ppermute(c_dh, "tp", far)
     dq_0, dq_to_0, *carried = attend_back(
-        where, queries, kv, attn_0, grads_of(after(full_0, *down)), lse_0, tables, blocks[0], None, count
-    )
-    v_out = summed(k_out, after(g_out, dq_0))
-    k_out, g_out = halved(v_out, far)
-    full_1 = stack(cur1, after(b1, *v_out))
+        where, queries, kv, attn_0, grads_of(x0, g_up, p1), lse_0, tables, blocks[0], None, count
+    )
+    grads_1 = grads_of(x1, dq_0)
     dq_1, dq_to_1, d_kv, d_kv_to = attend_back(
-        where, queries, kv, attn_1, grads_of(full_1), lse_1, tables, blocks[1], carried, count
-    )
+        where, queries, kv, attn_1, grads_1, lse_1, tables, blocks[1], carried, count
+    )
+
+    cur_dh = stack(c_dh, after(a_dh, dq_1))
+    b_dh = lax.ppermute(cur_dh, "tp", near)
+    dq_to_0, dq_to_1 = lax.optimization_barrier((dq_to_0, dq_to_1, cur_dh))[:2]
 
     def joined(query, kv_of, h, side):
         at = side * local + h * span
@@ -669,77 +745,69 @@
         for h, q in enumerate((dq_to_0, dq_to_1))
     ]
     sent = [swap(p[span:].astype(BF)) for p in parts]
+    d0 = parts[0][:span] + sent[0].astype(F32)
+    d1 = parts[1][:span] + sent[1].astype(F32)
+    k0, g0, t0 = halved([d0], near)
+    k1, g1, t1 = halved([d1], near)
+    down = [dotf(i, wd) for i in lax.optimization_barrier(tuple(inner) + (t0, t1))[:2]]
+    s_down = swap(stack(*[d[span:].astype(BF) for d in down]))
+    g_down = grad_kernel(inner, lax.optimization_barrier(tuple(cots) + (*down, b_dh))[:2], 0, width, 512)
+    r_gate, r_up, r_down = reduced(g_gate, 0), reduced(g_up, 0), reduced(g_down, 1)
+    down = [
+        d[:span] + after(s_down, g_down)[n * span : (n + 1) * span].astype(F32) for n, d in enumerate(down)
+    ]
+    v0 = summed(k0, after(g0, g_down))
+    k0, g0, t0 = halved(v0, far)
+    r_gate, r_up = lax.optimization_barrier((r_gate, r_up, t0))[:2]
+    s_gate = pair(half_of(r_gate, core, 0), swap(half_of(r_gate, other, 0)), core, 1).astype(F32)
+    s_up = pair(half_of(r_up, core, 0), swap(half_of(r_up, other, 0)), core, 1).astype(F32)
+    v1 = summed(k1, after(g1, t0, s_gate, s_up))
+    k1, g1, t1 = halved(v1, far)
+    k_out, g_out, t_out = halved(down, near)
     d_qkv = stack(*[joined(q, d_kv, h, s) for s in range(2) for h, q in enumerate((dq_0, dq_1))])
-    g_qkv = dot_0(normed, after(d_qkv, *parts)).astype(BF)
-    d0 = parts[0][:span] + after(sent[0], g_qkv).astype(F32)
-    d1 = parts[1][:span] + after(sent[1], g_qkv).astype(F32)
-    k0, g0 = halved([d0], near)
-    k1, g1 = halved([d1], near)
-    totals = summed(k_out, after(g_out, d0, d1))
-    c_out = stack(hidden_0 + totals[0], hidden_1 + totals[1]).astype(BF)
-    a_out = lax.ppermute(c_out, "tp", far)
-
-    dh_all = after(stack(full_0, full_1), c_out)
-    g_mine = dot_0(stack(*[a[0] for a in attn_own]), dh_all).astype(BF)
-    g_theirs = dot_0(stack(*[a[1] for a in attn_own]), dh_all).astype(BF)
-
-    def columns(grad, which):
-        grad = grad.reshape(grad.shape[0], fsdp, 2, shard)
-        return lax.dynamic_index_in_dim(grad, which, 2, keepdims=False)
-
-    got = swap(stack(columns(g_theirs, other), columns(g_mine, other)))
-    g_output = stack(columns(g_mine, core), columns(g_theirs, core)).astype(F32) + got.astype(F32)
-    g_output = g_output.astype(BF).swapaxes(0, 1)
+    g_qkv = dot_0(normed, after(d_qkv, t0, t1, t_out)).astype(BF)
+
+    def input_of(h, d_hidden, total):
+        d_rows, gain = norm_backward(slice_of(rows, h), slice_of(scale_own, h), gain_a, total)
+        return gain, (d_hidden + d_rows).astype(BF)
+
+    by_distance = stack(cur_dh, after(b_dh, t1, t_out)).reshape(count, CHUNKS, piece, width)
+    dh_all = by_distance.swapaxes(0, 1).reshape(-1, width)
+    keep, send = output_grad(
+        core.astype(jnp.int32).reshape(1), [a[0] for a in attn_own], [a[1] for a in attn_own], dh_all, shard, fsdp
+    )
+    g_output = (keep.astype(F32) + swap(send).astype(F32)).astype(BF)
     g_qkv = g_qkv.reshape(fsdp, -1, narrow)
     joint = g_qkv.shape[1] == g_output.shape[1]
     if joint:
         reduce = [Scatter(jnp.concatenate([g_qkv, g_output], axis=2))]
     else:
         reduce = [Scatter(g_qkv), Scatter(g_output)]
-
-    v0 = summed(k0, after(g0, g_output))
-    k0, g0 = halved(v0, far)
-    v1 = summed(k1, after(g1, v0[0]))
-    k1, g1 = halved(v1, far)
-    cur_out = stack(*[stack(c_out[h * piece : (h + 1) * piece], after(a_out, v1[0])[h * piece : (h + 1) * piece]) for h in range(CHUNKS)])
-    b_out = lax.ppermute(cur_out, "tp", near)
-    for item in reduce:
-        item.second(cur_out)
-
-    def input_of(h, d_hidden, total):
-        d_rows, gain = norm_backward(slice_of(rows, h), slice_of(scale_own, h), gain_a, total)
-        return gain, (d_hidden + d_rows).astype(BF)
-
-    gain_0, c0 = input_of(0, dh_0, summed(k0, after(g0, *[r.token for r in reduce]))[0])
+    firsts = [item.first_sent for item in reduce]
+
+    gain_0, c0 = input_of(0, dh_0, summed(k0, after(g0, g_qkv, g_output, *firsts))[0])
     a0 = lax.ppermute(c0, "tp", far)
     gain_1, c1 = input_of(1, dh_1, summed(k1, after(g1, c0))[0])
     a1 = lax.ppermute(c1, "tp", far)
-    g_all = sum_steps(jnp.stack([gain_0 + gain_1, g_ffn]), [("ctx", 1)])
-    cur0 = stack(c0, after(a0, c1, g_all))
+    for item in reduce:
+        item.second(c1)
+    tokens = [r.token for r in reduce]
+    cur0 = stack(c0, after(a0, *tokens))
     b0 = lax.ppermute(cur0, "tp", near)
-    cur1 = stack(c1, after(a1, cur0))
+    v_out = summed(k_out, after(g_out, cur0))
+    k_out, g_out, t_out = halved(v_out, far)
+    b0 = after(b0, t_out)
+    cur1 = stack(c1, after(a1, b0))
     b1 = lax.ppermute(cur1, "tp", near)
-
-    r_down, r_gate, r_up = lax.optimization_barrier((r_down, r_gate, r_up, cur1))[:3]
+    totals = summed(k_out, after(g_out, cur1))
+    c_out = stack(hidden_0 + totals[0], hidden_1 + totals[1]).astype(BF)
+    a_out = lax.ppermute(c_out, "tp", far)
+    g_all = sum_direct(jnp.stack([gain_0 + gain_1, g_ffn]), "ctx", cur0)
+    g_all = sum_direct(g_all, "fsdp", c_out)
+
+    r_down = after(r_down, c_out)
     s_down = pair(half_of(r_down, core, 1), swap(half_of(r_down, other, 1)), core, 0).astype(F32)
-    s_gate = pair(half_of(r_gate, core, 0), swap(half_of(r_gate, other, 0)), core, 1).astype(F32)
-    s_up = pair(half_of(r_up, core, 0), swap(half_of(r_up, other, 0)), core, 1).astype(F32)
-
-    half = span
-    cur_half, got_half = cur_out.shape[0] // CHUNKS, b_out.shape[0] // CHUNKS
-    b_out = after(b_out, cur1)
-    out = arrange(
-        [
-            stack(cur_out[h * cur_half : (h + 1) * cur_half], b_out[h * got_half : (h + 1) * got_half])
-            for h in range(CHUNKS)
-        ],
-        place_at,
-        F32,
-        True,
-    )
-    g_all = sum_steps(after(g_all, cur1), [("tp", 1), ("tp", 2)] + [("fsdp", b) for b in bits_of("fsdp")])
-
-    results = [item.third(out) for item in reduce]
+    results = [item.third(c_out) for item in reduce]
     if joint:
         r_qkv, r_output = results[0][:, :narrow], results[0][:, narrow:]
     else:
@@ -751,7 +819,23 @@
     s_query, s_key, s_value = [
         pair(mine[:, a:b], theirs[:, a:b], core, 1).astype(F32) for a, b in zip(bounds, bounds[1:])
     ]
+    a_out = after(a_out, b1, s_down, s_query, s_key, s_value, s_output, g_all)
+    cur_out = stack(*[stack(c_out[h * piece : (h + 1) * piece], a_out[h * piece : (h + 1) * piece]) for h in range(CHUNKS)])
+    b_out = lax.ppermute(cur_out, "tp", near)
+    b0, b1 = lax.optimization_barrier((b0, b1, cur_out))[:2]
     d_input = arrange([stack(cur0, b0), stack(cur1, b1)], place_at, F32, True)
+    b_out = after(b_out, d_input)
+    g_all = sum_direct(g_all, "tp", d_input)
+    cur_half, got_half = cur_out.shape[0] // CHUNKS, b_out.shape[0] // CHUNKS
+    out = arrange(
+        [
+            stack(cur_out[h * cur_half : (h + 1) * cur_half], b_out[h * got_half : (h + 1) * got_half])
+            for h in range(CHUNKS)
+        ],
+        place_at,
+        F32,
+        True,
+    )
 
     start = (slot * 2 + core) * shard
     s_attn = lax.dynamic_slice_in_dim(g_all[0], start, shard, 0)

time: 616 us -> 589 us (0.956)
  other arithmetic: 99.4 us -> 74.7 us
    ppermute x3 -> x2, waiting for transfers between devices: 24 us -> 3.99 us  [body(): a0 = lax.ppermute(c0, 'tp', far)]
    ppermute x2, waiting for transfers between devices: 17.7 us -> 3.49 us  [second(): far = lax.ppermute(one[:cut], 'fsdp', xor_pairs('fsdp', 2))]
    ppermute x1, waiting for transfers between devices: 0.01 us -> 13.2 us  [body(): b_out = lax.ppermute(cur_out, 'tp', near)]
    ppermute x24, waiting for transfers between devices: 3.26 us -> 13.4 us  [swap(): return lax.ppermute(value, 'ctx', [(0, 1), (1, 0)])]
    concatenate x20 -> x18, other arithmetic: 23.9 us -> 14.2 us  [stack(): return jnp.concatenate(parts, axis=0)]
    ppermute x1, waiting for transfers between devices: 0.01 us -> 8.97 us  [body(): a_out = lax.ppermute(c_out, 'tp', far)]
    ppermute x2, waiting for transfers between devices: 3.25 us -> 12.1 us  [first(): self.one = lax.ppermute(shard, 'fsdp', xor_pairs('fsdp', 1))]
    dynamic_slice x6 -> x0, local copies, waits for them, and re-layouts: 7.96 us -> none  [columns(): return lax.dynamic_index_in_dim(grad, which, 2, keepdims=False)]
  transfers between devices with their start and end apart: 74 -> 83, of which waited for: 31 -> 31; matrix products, arithmetic and copies ran while one was open for 34% -> 30% of each run, Pallas kernels for 10% -> 11%
where the time goes in v3:
time: 589 us; the launch traced here: 583 us
  waiting for transfers between devices  208 us (35%)
  Pallas kernels  75.6 us (13%)
  other arithmetic  74.7 us (13%)
  starting transfers between devices  73.9 us (13%)
  local copies, waits for them, and re-layouts  68.7 us (12%)
  matrix products  66.3 us (11%)
  between operations  16.1 us (3%)
    ppermute x14, waiting for transfers between devices, halved(): return ([v[:half] for v in values], lax.ppermute(sent, 'tp', pairs), sent)  102 us
    dot_general x8, matrix products, dot_t(): lax.dot_general(left, right, (((1,), (1,)), ((), ())), preferred_element_...  36.1 us
    unnamed x152, local copies, waits for them, and re-layouts  29.1 us
    dot_general x9, matrix products, dotf(): return jnp.dot(left, right, preferred_element_type=F32)  25.9 us
    pallas_call x3, Pallas kernels, grad_kernel(): pl.pallas_call(kernel, grid=(wide // block,), in_specs=[pl.BlockSpec((row...  25.4 us
    pallas_call x2, Pallas kernels, attend_back(): pl.pallas_call(kernel, in_specs=[SCALARS] + [pl.BlockSpec()] * (10 + 2 *...  19.5 us
    ppermute x1, waiting for transfers between devices, body(): b0 = lax.ppermute(cur0, 'tp', near)  19.4 us
    concatenate x18, other arithmetic, stack(): return jnp.concatenate(parts, axis=0)  14.2 us
  transfers between devices with their start and end apart: 83, of which 31 were waited for; matrix products, arithmetic and copies ran while one was open for 30% of the time, Pallas kernels for 11%

profile of v3, /device:TPU:0, one launch (start us, length us, event | category | flops | bytes accessed | tf_op | source)
XLA Modules:
  0.0 583.2 jit_solution(6494033183606659801)
XLA Ops:
  17.4 7.3 %collective-permute-done.4 = f32[512,2048]{1,0:T(8,128)} collective-permute-done((f32[512,2048]{1,0:T(8,128)}, f32[512,2048]{1,0:T(8,128)}, u32[]{:S(2)}, u32[]{:S(2)}) %collective-permute-start.4) | collective-permute-done | bytes 4194336 | tf_op jit(solution)/shard_map/ppermute | solution.py:40
  31.2 3.3 broadcast_select_fusion.20
  43.0 3.9 arrange.3
  47.0 12.1 %collective-permute-done.1 = bf16[544,384]{1,0:T(8,128)(2,1)S(1)} collective-permute-done((bf16[544,384]{1,0:T(8,128)(2,1)S(1)}, bf16[544,384]{1,0:T(8,128)(2,1)S(1)}, u32[]{:S(2)}, u32[]{:S(2)}) %collective-permute-start.1) | collective-permute-done | bytes 417824 | tf_op jit(solution)/shard_map/ppermute | solution.py:184
  75.5 2.9 multiply_convert_fusion.1
  80.5 3.5 fusion.qkv_ref
  83.9 7.6 %attend_first.1 = (bf16[1024,256]{1,0:T(8,128)(2,1)}, bf16[1024,128]{1,0:T(8,128)(2,1)}, bf16[512,256]{1,0:T(8,128)(2,1)}, f32[512,4]{1,0:T(8,128)}) custom-call(s32[2]{0:T(128)} %pad_add_fusion.at_ref, f32[1024,384]{1,0:T(8,128)} %fusion.qkv_ref, f32[1024,128]{1,0:T(8,128)} %get-tuple-element.355.cos_ref, f32[1024,128]{1,0:T(8,128)} %get-tuple-element.353.sin_ref, ...), custom_call_target="tpu_custom_call" | custom-call | flops 8000000000 | bytes 1572864 | tf_op jit(solution)/shard_map/attend_first/pallas_call | solution.py:396
  96.6 3.2 collective-permute-done.10
  103.7 5.2 collective-permute-done.16
  109.8 5.9 %attend_next.1 = (bf16[512,256]{1,0:T(8,128)(2,1)}, f32[512,4]{1,0:T(8,128)}) custom-call(s32[2]{0:T(128)} %pad_add_fusion.at_ref, bf16[1024,256]{1,0:T(8,128)(2,1)} %get-tuple-element.126.q_ref, bf16[1024,128]{1,0:T(8,128)(2,1)} %get-tuple-element.128.kv_ref), custom_call_target="tpu_custom_call" | custom-call | flops 5000000000 | bytes 524288 | tf_op jit(solution)/shard_map/attend_next/pallas_call | solution.py:418
  132.5 3.1 fusion.79
  135.6 7.6 %collective-permute-done.14 = bf16[128,2048]{1,0:T(8,128)(2,1)S(1)} collective-permute-done((bf16[128,2048]{1,0:T(8,128)(2,1)S(1)}, bf16[128,2048]{1,0:T(8,128)(2,1)S(1)}, u32[]{:S(2)}, u32[]{:S(2)}) %collective-permute-start.14) | collective-permute-done | bytes 524320 | tf_op jit(solution)/shard_map/ppermute | solution.py:73
  143.6 16.0 %collective-permute-done.19 = bf16[128,2048]{1,0:T(8,128)(2,1)S(1)} collective-permute-done((bf16[128,2048]{1,0:T(8,128)(2,1)S(1)}, bf16[128,2048]{1,0:T(8,128)(2,1)S(1)}, u32[]{:S(2)}, u32[]{:S(2)}) %collective-permute-start.19) | collective-permute-done | bytes 524320 | tf_op jit(solution)/shard_map/ppermute | solution.py:73
  164.9 13.9 %collective-permute-done.21 = bf16[64,2048]{1,0:T(8,128)(2,1)S(1)} collective-permute-done((bf16[64,2048]{1,0:T(8,128)(2,1)S(1)}, bf16[64,2048]{1,0:T(8,128)(2,1)S(1)}, u32[]{:S(2)}, u32[]{:S(2)}) %collective-permute-start.21) | collective-permute-done | bytes 262176 | tf_op jit(solution)/shard_map/ppermute | solution.py:73
  180.4 4.0 collective-permute-done.20
  190.6 11.1 %collective-permute-done.23 = bf16[64,2048]{1,0:T(8,128)(2,1)S(1)} collective-permute-done((bf16[64,2048]{1,0:T(8,128)(2,1)S(1)}, bf16[64,2048]{1,0:T(8,128)(2,1)S(1)}, u32[]{:S(2)}, u32[]{:S(2)}) %collective-permute-start.23) | collective-permute-done | bytes 262176 | tf_op jit(solution)/shard_map/ppermute | solution.py:646
  201.8 3.4 collective-permute-start.27
  208.9 7.7 %fusion.96 = f32[512,2048]{1,0:T(8,128)S(1)} fusion(bf16[512,2048]{1,0:T(8,128)(2,1)} %constant_dynamic-update-slice_fusion.5.refs_0_, bf16[2048,2048]{1,0:T(8,128)(2,1)} %all-gather.4.cloned.1.call-done), kind=kOutput, calls=%fused_computation.357 | convolution fusion | flops 4294967296 | bytes 14680064 | tf_op jit(solution)/shard_map/dot_general | solution.py:19
  216.8 4.7 multiply_convert_fusion.6
  221.6 4.5 fusion.72
  229.1 6.3 %fusion.97 = f32[512,2048]{1,0:T(8,128)} fusion(bf16[512,2048]{1,0:T(8,128)(2,1)S(1)} %constant_dynamic-update-slice_fusion.10.refs_1_, bf16[2048,2048]{1,0:T(8,128)(2,1)S(1)} %copy-done.60), kind=kOutput, calls=%fused_computation.358 | convolution fusion | flops 4294967296 | bytes 14680064 | tf_op jit(solution)/shard_map/dot_general | solution.py:19
  237.6 7.5 %multiply_convert_fusion.3 = (bf16[512,1024]{1,0:T(8,128)(2,1)S(1)}, bf16[512,1024]{1,0:T(8,128)(2,1)S(1)}, bf16[512,1024]{1,0:T(8,128)(2,1)}) fusion(f32[512,2048]{1,0:T(8,128)} %fusion.97, bf16[512,2048]{1,0:T(8,128)(2,1)S(1)} %copy-done.31, bf16[1024,2048]{1,0:T(8,128)(2,1)} %all-gather.6.cloned.1.call-done), kind=kOutput, calls=%fused_computation.41 | convolution fusion | flops 2155347968 | bytes 13631488 | tf_op jit(solution)/shard_map/dot_general | solution.py:23
  245.3 4.5 collective-permute-done.31
  249.9 4.5 fusion.98
  260.4 11.0 %collective-permute-done.32 = bf16[64,2048]{1,0:T(8,128)(2,1)S(1)} collective-permute-done((bf16[64,2048]{1,0:T(8,128)(2,1)S(1)}, bf16[64,2048]{1,0:T(8,128)(2,1)S(1)}, u32[]{:S(2)}, u32[]{:S(2)}) %collective-permute-start.32) | collective-permute-done | bytes 262176 | tf_op jit(solution)/shard_map/ppermute | solution.py:73
  273.7 6.0 %convolution_convert_fusion.2 = bf16[64,2048]{1,0:T(8,128)(2,1)S(1)} fusion(bf16[64,2048]{1,0:T(8,128)(2,1)S(1)} %get-tuple-element.227, bf16[2048,2048]{1,0:T(8,128)(2,1)} %all-gather.8.cloned.1.call-done), kind=kOutput, calls=%fused_computation.18 | convolution fusion | flops 537001984 | bytes 8912896 | tf_op jit(solution)/shard_map/dot_general | solution.py:23
  280.4 8.4 %grad.3 = bf16[2048,1024]{1,0:T(8,128)(2,1)} custom-call(bf16[512,2048]{1,0:T(8,128)(2,1)} %constant_dynamic-update-slice_fusion.5.refs_0_, bf16[512,2048]{1,0:T(8,128)(2,1)} %copy-done.56, bf16[512,2048]{1,0:T(8,128)(2,1)} %pad_maximum_fusion.7.refs_2_, bf16[512,2048]{1,0:T(8,128)(2,1)} %copy-done.32), custom_call_target="tpu_custom_call" | custom-call | flops 8589934592 | bytes 8388608 | tf_op jit(solution)/shard_map/grad/pallas_call | solution.py:236
  288.9 13.7 %collective-permute-done.37 = bf16[128,2048]{1,0:T(8,128)(2,1)S(1)} collective-permute-done((bf16[128,2048]{1,0:T(8,128)(2,1)}, bf16[128,2048]{1,0:T(8,128)(2,1)S(1)}, u32[]{:S(2)}, u32[]{:S(2)}) %collective-permute-start.37) | collective-permute-done | bytes 524320 | tf_op jit(solution)/shard_map/ppermute | solution.py:73
  309.9 8.4 %grad.4 = bf16[2048,1024]{1,0:T(8,128)(2,1)} custom-call(bf16[512,2048]{1,0:T(8,128)(2,1)} %constant_dynamic-update-slice_fusion.5.refs_0_, bf16[512,2048]{1,0:T(8,128)(2,1)} %copy-done.56, bf16[512,2048]{1,0:T(8,128)(2,1)} %pad_maximum_fusion.7.refs_2_, bf16[512,2048]{1,0:T(8,128)(2,1)} %copy-done.32), custom_call_target="tpu_custom_call" | custom-call | flops 8589934592 | bytes 8388608 | tf_op jit(solution)/shard_map/grad/pallas_call | solution.py:236
  325.5 6.2 %convolution_convert_fusion.1 = bf16[64,2048]{1,0:T(8,128)(2,1)S(1)} fusion(bf16[64,2048]{1,0:T(8,128)(2,1)S(1)} %get-tuple-element.225, bf16[2048,2048]{1,0:T(8,128)(2,1)} %all-gather.8.cloned.1.call-done), kind=kOutput, calls=%fused_computation.17 | convolution fusion | flops 537001984 | bytes 8912896 | tf_op jit(solution)/shard_map/dot_general | solution.py:23
  342.0 8.3 %attend_back.2 = (bf16[512,256]{1,0:T(8,128)(2,1)}, bf16[512,256]{1,0:T(8,128)(2,1)}, f32[2,1024,128]{2,1,0:T(8,128)}, f32[2,1024,128]{2,1,0:T(8,128)}) custom-call(s32[2]{0:T(128)} %pad_add_fusion.at_ref, bf16[1024,256]{1,0:T(8,128)(2,1)} %get-tuple-element.126.q_ref, bf16[1024,128]{1,0:T(8,128)(2,1)} %get-tuple-element.128.kv_ref, ...), custom_call_target="tpu_custom_call" | custom-call | flops 8000000000 | bytes 1048576 | tf_op jit(solution)/shard_map/attend_back/pallas_call | solution.py:510
  355.5 11.2 %attend_back.3 = (bf16[512,256]{1,0:T(8,128)(2,1)}, bf16[512,256]{1,0:T(8,128)(2,1)}, bf16[1024,128]{1,0:T(8,128)(2,1)}, bf16[1024,128]{1,0:T(8,128)(2,1)}) custom-call(s32[2]{0:T(128)} %pad_add_fusion.at_ref, bf16[1024,256]{1,0:T(8,128)(2,1)} %get-tuple-element.126.q_ref, bf16[1024,128]{1,0:T(8,128)(2,1)} %get-tuple-element.128.kv_ref, ...), custom_call_target="tpu_custom_call" | custom-call | flops 8000000000 | bytes 1048576 | tf_op jit(solution)/shard_map/attend_back/pallas_call | solution.py:510
  393.5 6.4 %collective-permute-done.48 = bf16[256,2048]{1,0:T(8,128)(2,1)} collective-permute-done((bf16[256,2048]{1,0:T(8,128)(2,1)}, bf16[256,2048]{1,0:T(8,128)(2,1)}, u32[]{:S(2)}, u32[]{:S(2)}) %collective-permute-start.48) | collective-permute-done | bytes 1048608 | tf_op jit(solution)/shard_map/ppermute | solution.py:736
  399.9 8.6 %grad.5 = bf16[1024,2048]{1,0:T(8,128)(2,1)} custom-call(bf16[512,1024]{1,0:T(8,128)(2,1)} %get-tuple-element.176.refs_0_, bf16[512,1024]{1,0:T(8,128)(2,1)} %get-tuple-element.177.refs_1_, bf16[512,2048]{1,0:T(8,128)(2,1)} %pad_maximum_fusion.5.refs_2_, bf16[512,2048]{1,0:T(8,128)(2,1)} %pad_maximum_fusion.6.refs_3_), custom_call_target="tpu_custom_call" | custom-call | flops 8589934592 | bytes 6291456 | tf_op jit(solution)/shard_map/grad/pallas_call | solution.py:236
  415.4 3.4 slice_add_fusion.1
  432.4 4.9 output_grad.1
  444.4 4.3 convolution_convert_fusion
  448.9 6.8 %collective-permute-done.51 = bf16[64,2048]{1,0:T(8,128)(2,1)S(1)} collective-permute-done((bf16[64,2048]{1,0:T(8,128)(2,1)S(1)}, bf16[64,2048]{1,0:T(8,128)(2,1)S(1)}, u32[]{:S(2)}, u32[]{:S(2)}) %collective-permute-start.51) | collective-permute-done | bytes 262176 | tf_op jit(solution)/shard_map/ppermute | solution.py:73
  459.7 16.9 %collective-permute-done.59 = bf16[64,2048]{1,0:T(8,128)(2,1)S(1)} collective-permute-done((bf16[64,2048]{1,0:T(8,128)(2,1)S(1)}, bf16[64,2048]{1,0:T(8,128)(2,1)S(1)}, u32[]{:S(2)}, u32[]{:S(2)}) %collective-permute-start.59) | collective-permute-done | bytes 262176 | tf_op jit(solution)/shard_map/ppermute | solution.py:73
  477.1 3.4 collective-permute-start.61
  482.4 3.0 collective-permute-start.62
  488.3 19.4 %collective-permute-done.62 = bf16[128,2048]{1,0:T(8,128)(2,1)S(1)} collective-permute-done((bf16[128,2048]{1,0:T(8,128)(2,1)S(1)}, bf16[128,2048]{1,0:T(8,128)(2,1)S(1)}, u32[]{:S(2)}, u32[]{:S(2)}) %collective-permute-start.62) | collective-permute-done | bytes 524320 | tf_op jit(solution)/shard_map/ppermute | solution.py:796
  511.2 6.6 %collective-permute-done.60 = bf16[128,2048]{1,0:T(8,128)(2,1)S(1)} collective-permute-done((bf16[128,2048]{1,0:T(8,128)(2,1)S(1)}, bf16[128,2048]{1,0:T(8,128)(2,1)S(1)}, u32[]{:S(2)}, u32[]{:S(2)}) %collective-permute-start.60) | collective-permute-done | bytes 524320 | tf_op jit(solution)/shard_map/ppermute | solution.py:73
  522.2 5.2 collective-permute-done.66
  537.8 9.0 %collective-permute-done.63 = bf16[128,2048]{1,0:T(8,128)(2,1)S(1)} collective-permute-done((bf16[128,2048]{1,0:T(8,128)(2,1)S(1)}, bf16[128,2048]{1,0:T(8,128)(2,1)S(1)}, u32[]{:S(2)}, u32[]{:S(2)}) %collective-permute-start.63) | collective-permute-done | bytes 524320 | tf_op jit(solution)/shard_map/ppermute | solution.py:804
  551.1 4.2 arrange.4
  556.5 13.2 %collective-permute-done.73 = bf16[256,2048]{1,0:T(8,128)(2,1)S(1)} collective-permute-done((bf16[256,2048]{1,0:T(8,128)(2,1)}, bf16[256,2048]{1,0:T(8,128)(2,1)S(1)}, u32[]{:S(2)}, u32[]{:S(2)}) %collective-permute-start.73) | collective-permute-done | bytes 1048608 | tf_op jit(solution)/shard_map/ppermute | solution.py:824
  571.9 4.2 arrange.5
  (486 shorter events, 220.4 us)
Async XLA Ops:
  7.2 154.8 %all-gather.6.cloned.1.call-start = ((), (), s32[]{:S(2)}) async-start(), calls=%async_computation.4 | async-start | bytes 5242880 | tf_op jit(solution)/shard_map/all_gather | solution.py:591
  28.0 181.0 %all-gather.4.cloned.1.call-start = ((), (), s32[]{:S(2)}) async-start(), calls=%async_computation.3 | async-start | bytes 10485760 | tf_op jit(solution)/shard_map/all_gather | solution.py:590
  30.6 243.1 %all-gather.8.cloned.1.call-start = ((), (), s32[]{:S(2)}) async-start(), calls=%async_computation.5 | async-start | bytes 9437184 | tf_op jit(solution)/shard_map/all_gather | solution.py:613
  37.0 22.1 %collective-permute-start.1 = (bf16[544,384]{1,0:T(8,128)(2,1)S(1)}, bf16[544,384]{1,0:T(8,128)(2,1)S(1)}, u32[]{:S(2)}, u32[]{:S(2)}) collective-permute-start(bf16[544,384]{1,0:T(8,128)(2,1)S(1)} %pad_maximum_fusion.33), channel_id=1, source_target_pairs={{0,8},{8,0},{16,24},{24,16},{1,9},{9,1},{17,25},{25,17},{2,10},{10... | collective-permute-start | bytes 1253384 | tf_op jit(solution)/shard_map/ppermute | solution.py:184
  40.0 21.2 %collective-permute-start.2 = (bf16[544,384]{1,0:T(8,128)(2,1)S(1)}, bf16[544,384]{1,0:T(8,128)(2,1)S(1)}, u32[]{:S(2)}, u32[]{:S(2)}) collective-permute-start(bf16[544,384]{1,0:T(8,128)(2,1)S(1)} %pad_maximum_fusion.33), channel_id=1, source_target_pairs={{0,16},{8,24},{16,0},{24,8},{1,17},{9,25},{17,1},{25,9},{2,18},{10... | collective-permute-start | bytes 1253384 | tf_op jit(solution)/shard_map/ppermute | solution.py:185
  46.9 85.6 %collective-permute-start.24 = (bf16[512,2048]{1,0:T(8,128)(2,1)}, bf16[512,2048]{1,0:T(8,128)(2,1)}, u32[]{:S(2)}, u32[]{:S(2)}) collective-permute-start(bf16[512,2048]{1,0:T(8,128)(2,1)} %arrange.3), channel_id=1, source_target_pairs={{0,4},{4,0},{1,5},{5,1},{2,6},{6,2},{3,7},{7,3},{8,12},{12,8},{9,1... | collective-permute-start | bytes 6291464 | tf_op jit(solution)/shard_map/ppermute | solution.py:40
  69.9 21.7 %collective-permute-start.8 = (bf16[512,256]{1,0:T(8,128)(2,1)S(1)}, bf16[512,256]{1,0:T(8,128)(2,1)S(1)}, u32[]{:S(2)}, u32[]{:S(2)}) collective-permute-start(bf16[512,256]{1,0:T(8,128)(2,1)S(1)} %copy-done.26), channel_id=1, source_target_pairs={{0,8},{8,0},{16,24},{24,16},{1,9},{9,1},{17,25},{25,17},{2,10},{10... | collective-permute-start | bytes 786440 | tf_op jit(solution)/shard_map/ppermute | solution.py:184
  71.3 20.3 %collective-permute-start.9 = (bf16[512,256]{1,0:T(8,128)(2,1)S(1)}, bf16[512,256]{1,0:T(8,128)(2,1)S(1)}, u32[]{:S(2)}, u32[]{:S(2)}) collective-permute-start(bf16[512,256]{1,0:T(8,128)(2,1)S(1)} %copy-done.26), channel_id=1, source_target_pairs={{0,16},{8,24},{16,0},{24,8},{1,17},{9,25},{17,1},{25,9},{2,18},{10... | collective-permute-start | bytes 786440 | tf_op jit(solution)/shard_map/ppermute | solution.py:185
  72.8 21.8 %collective-permute-start.15 = (bf16[512,256]{1,0:T(8,128)(2,1)S(1)}, bf16[512,256]{1,0:T(8,128)(2,1)S(1)}, u32[]{:S(2)}, u32[]{:S(2)}) collective-permute-start(bf16[512,256]{1,0:T(8,128)(2,1)S(1)} %copy-done.26), channel_id=1, source_target_pairs={{0,2},{1,3},{2,0},{3,1},{4,6},{5,7},{6,4},{7,5},{8,10},{9,11},{10,... | collective-permute-start | bytes 786440 | tf_op jit(solution)/shard_map/ppermute | solution.py:86
  94.0 32.9 %collective-permute-start.13 = (bf16[256,256]{1,0:T(8,128)(2,1)}, bf16[256,256]{1,0:T(8,128)(2,1)}, u32[]{:S(2)}, u32[]{:S(2)}) collective-permute-start(bf16[256,256]{1,0:T(8,128)(2,1)} %get-tuple-element.307), channel_id=1, source_target_pairs={{0,4},{4,0},{1,5},{5,1},{2,6},{6,2},{3,7},{7,3},{8,12},{12,8},{9,1... | collective-permute-start | bytes 393224 | tf_op jit(solution)/shard_map/ppermute | solution.py:40
  132.1 27.5 %collective-permute-start.19 = (bf16[128,2048]{1,0:T(8,128)(2,1)S(1)}, bf16[128,2048]{1,0:T(8,128)(2,1)S(1)}, u32[]{:S(2)}, u32[]{:S(2)}) collective-permute-start(bf16[128,2048]{1,0:T(8,128)(2,1)S(1)} %slice.864), channel_id=1, source_target_pairs={{0,1},{1,0},{2,3},{3,2},{4,5},{5,4},{6,7},{7,6},{8,9},{9,8},{10,11... | collective-permute-start | bytes 1572872 | tf_op jit(solution)/shard_map/ppermute | solution.py:73
  143.4 17.3 %collective-permute-start.18 = (bf16[64,2048]{1,0:T(8,128)(2,1)S(1)}, bf16[64,2048]{1,0:T(8,128)(2,1)S(1)}, u32[]{:S(2)}, u32[]{:S(2)}) collective-permute-start(bf16[64,2048]{1,0:T(8,128)(2,1)S(1)} %slice.873), channel_id=1, source_target_pairs={{0,2},{1,3},{2,0},{3,1},{4,6},{5,7},{6,4},{7,5},{8,10},{9,11},{10,... | collective-permute-start | bytes 786440 | tf_op jit(solution)/shard_map/ppermute | solution.py:73
  159.7 19.1 %collective-permute-start.21 = (bf16[64,2048]{1,0:T(8,128)(2,1)S(1)}, bf16[64,2048]{1,0:T(8,128)(2,1)S(1)}, u32[]{:S(2)}, u32[]{:S(2)}) collective-permute-start(bf16[64,2048]{1,0:T(8,128)(2,1)S(1)} %slice.872), channel_id=1, source_target_pairs={{0,2},{1,3},{2,0},{3,1},{4,6},{5,7},{6,4},{7,5},{8,10},{9,11},{10,... | collective-permute-start | bytes 786440 | tf_op jit(solution)/shard_map/ppermute | solution.py:73
  162.0 252.1 %reduce-scatter.4.cloned.1.call-start = ((), (), s32[]{:S(2)}) async-start(), calls=%async_computation.6 | async-start | bytes 5242880 | tf_op jit(solution)/shard_map/reduce_scatter | solution.py:687
  162.8 21.5 %collective-permute-start.20 = (bf16[64,2048]{1,0:T(8,128)(2,1)S(1)}, bf16[64,2048]{1,0:T(8,128)(2,1)S(1)}, u32[]{:S(2)}, u32[]{:S(2)}) collective-permute-start(bf16[64,2048]{1,0:T(8,128)(2,1)S(1)} %get-tuple-element.232), channel_id=1, source_target_pairs={{0,2},{1,3},{2,0},{3,1},{4,6},{5,7},{6,4},{7,5},{8,10},{9,11},{10,... | collective-permute-start | bytes 786440 | tf_op jit(solution)/shard_map/ppermute | solution.py:644
  184.4 20.8 %collective-permute-start.22 = (bf16[128,2048]{1,0:T(8,128)(2,1)S(1)}, bf16[128,2048]{1,0:T(8,128)(2,1)S(1)}, u32[]{:S(2)}, u32[]{:S(2)}) collective-permute-start(bf16[128,2048]{1,0:T(8,128)(2,1)S(1)} %pad_maximum_fusion.26), channel_id=1, source_target_pairs={{0,1},{1,0},{2,3},{3,2},{4,5},{5,4},{6,7},{7,6},{8,9},{9,8},{10,11... | collective-permute-start | bytes 1572872 | tf_op jit(solution)/shard_map/ppermute | solution.py:648
  190.6 16.6 %collective-permute-start.25 = (bf16[128,2048]{1,0:T(8,128)(2,1)S(1)}, bf16[128,2048]{1,0:T(8,128)(2,1)S(1)}, u32[]{:S(2)}, u32[]{:S(2)}) collective-permute-start(bf16[128,2048]{1,0:T(8,128)(2,1)S(1)} %pad_maximum_fusion.26), channel_id=1, source_target_pairs={{0,4},{4,0},{1,5},{5,1},{2,6},{6,2},{3,7},{7,3},{8,12},{12,8},{9,1... | collective-permute-start | bytes 1572872 | tf_op jit(solution)/shard_map/ppermute | solution.py:40
  205.2 21.6 %collective-permute-start.28 = (bf16[128,2048]{1,0:T(8,128)(2,1)S(1)}, bf16[128,2048]{1,0:T(8,128)(2,1)}, u32[]{:S(2)}, u32[]{:S(2)}) collective-permute-start(bf16[128,2048]{1,0:T(8,128)(2,1)S(1)} %pad_maximum_fusion.27), channel_id=1, source_target_pairs={{0,4},{4,0},{1,5},{5,1},{2,6},{6,2},{3,7},{7,3},{8,12},{12,8},{9,1... | collective-permute-start | bytes 1572872 | tf_op jit(solution)/shard_map/ppermute | solution.py:40
  288.8 125.3 %reduce-scatter.6.cloned.1.call-start = ((), (), s32[]{:S(2)}) async-start(), calls=%async_computation.7 | async-start | bytes 5242880 | tf_op jit(solution)/shard_map/reduce_scatter | solution.py:687
  304.9 16.6 %collective-permute-start.38 = (bf16[64,2048]{1,0:T(8,128)(2,1)S(1)}, bf16[64,2048]{1,0:T(8,128)(2,1)S(1)}, u32[]{:S(2)}, u32[]{:S(2)}) collective-permute-start(bf16[64,2048]{1,0:T(8,128)(2,1)S(1)} %slice.870), channel_id=1, source_target_pairs={{0,2},{1,3},{2,0},{3,1},{4,6},{5,7},{6,4},{7,5},{8,10},{9,11},{10,... | collective-permute-start | bytes 786440 | tf_op jit(solution)/shard_map/ppermute | solution.py:73
  305.5 29.8 %collective-permute-start.34 = (bf16[64,512]{1,0:T(8,128)(2,1)}, bf16[64,512]{1,0:T(8,128)(2,1)}, u32[]{:S(2)}, u32[]{:S(2)}) collective-permute-start(bf16[64,512]{1,0:T(8,128)(2,1)} %get-tuple-element.330), channel_id=1, source_target_pairs={{0,2},{1,3},{2,0},{3,1},{4,6},{5,7},{6,4},{7,5},{8,10},{9,11},{10,... | collective-permute-start | bytes 196616 | tf_op jit(solution)/shard_map/ppermute | solution.py:706
  307.9 28.9 %collective-permute-start.35 = (bf16[64,512]{1,0:T(8,128)(2,1)}, bf16[64,512]{1,0:T(8,128)(2,1)}, u32[]{:S(2)}, u32[]{:S(2)}) collective-permute-start(bf16[64,512]{1,0:T(8,128)(2,1)} %get-tuple-element.329), channel_id=1, source_target_pairs={{0,1},{1,0},{2,3},{3,2},{4,5},{5,4},{6,7},{7,6},{8,9},{9,8},{10,11... | collective-permute-start | bytes 196616 | tf_op jit(solution)/shard_map/ppermute | solution.py:706
  308.2 28.6 %collective-permute-start.36 = (bf16[64,512]{1,0:T(8,128)(2,1)}, bf16[64,512]{1,0:T(8,128)(2,1)}, u32[]{:S(2)}, u32[]{:S(2)}) collective-permute-start(bf16[64,512]{1,0:T(8,128)(2,1)} %get-tuple-element.328), channel_id=1, source_target_pairs={{0,3},{1,2},{2,1},{3,0},{4,7},{5,6},{6,5},{7,4},{8,11},{9,10},{10,... | collective-permute-start | bytes 196616 | tf_op jit(solution)/shard_map/ppermute | solution.py:706
  318.3 211.1 %reduce-scatter.8.cloned.1.call-start = ((), (), s32[]{:S(2)}) async-start(), calls=%async_computation.8 | async-start | bytes 5242880 | tf_op jit(solution)/shard_map/reduce_scatter | solution.py:687
  332.4 17.9 %collective-permute-start.40 = (bf16[64,512]{1,0:T(8,128)(2,1)}, bf16[64,512]{1,0:T(8,128)(2,1)}, u32[]{:S(2)}, u32[]{:S(2)}) collective-permute-start(bf16[64,512]{1,0:T(8,128)(2,1)} %get-tuple-element.334), channel_id=1, source_target_pairs={{0,2},{1,3},{2,0},{3,1},{4,6},{5,7},{6,4},{7,5},{8,10},{9,11},{10,... | collective-permute-start | bytes 196616 | tf_op jit(solution)/shard_map/ppermute | solution.py:706
  332.4 17.9 %collective-permute-start.41 = (bf16[64,512]{1,0:T(8,128)(2,1)}, bf16[64,512]{1,0:T(8,128)(2,1)}, u32[]{:S(2)}, u32[]{:S(2)}) collective-permute-start(bf16[64,512]{1,0:T(8,128)(2,1)} %get-tuple-element.333), channel_id=1, source_target_pairs={{0,1},{1,0},{2,3},{3,2},{4,5},{5,4},{6,7},{7,6},{8,9},{9,8},{10,11... | collective-permute-start | bytes 196616 | tf_op jit(solution)/shard_map/ppermute | solution.py:706
  340.1 27.7 %collective-permute-start.44 = (bf16[128,2048]{1,0:T(8,128)(2,1)S(1)}, bf16[128,2048]{1,0:T(8,128)(2,1)}, u32[]{:S(2)}, u32[]{:S(2)}) collective-permute-start(bf16[128,2048]{1,0:T(8,128)(2,1)S(1)} %pad_maximum_fusion.28), channel_id=1, source_target_pairs={{0,2},{1,3},{2,0},{3,1},{4,6},{5,7},{6,4},{7,5},{8,10},{9,11},{10,... | collective-permute-start | bytes 1572872 | tf_op jit(solution)/shard_map/ppermute | solution.py:726
  373.5 26.4 %collective-permute-start.48 = (bf16[256,2048]{1,0:T(8,128)(2,1)}, bf16[256,2048]{1,0:T(8,128)(2,1)}, u32[]{:S(2)}, u32[]{:S(2)}) collective-permute-start(bf16[256,2048]{1,0:T(8,128)(2,1)} %constant_dynamic-update-slice_fusion.22), channel_id=1, source_target_pairs={{0,1},{1,0},{2,3},{3,2},{4,5},{5,4},{6,7},{7,6},{8,9},{9,8},{10,11... | collective-permute-start | bytes 3145736 | tf_op jit(solution)/shard_map/ppermute | solution.py:736
  390.1 23.9 %collective-permute-start.47 = (bf16[512,2048]{1,0:T(8,128)(2,1)}, bf16[512,2048]{1,0:T(8,128)(2,1)}, u32[]{:S(2)}, u32[]{:S(2)}) collective-permute-start(bf16[512,2048]{1,0:T(8,128)(2,1)} %pad_maximum_fusion.9), channel_id=1, source_target_pairs={{0,4},{4,0},{1,5},{5,1},{2,6},{6,2},{3,7},{7,3},{8,12},{12,8},{9,1... | collective-permute-start | bytes 6291464 | tf_op jit(solution)/shard_map/ppermute | solution.py:40
  391.4 19.8 %collective-permute-start.50 = (bf16[128,2048]{1,0:T(8,128)(2,1)}, bf16[128,2048]{1,0:T(8,128)(2,1)}, u32[]{:S(2)}, u32[]{:S(2)}) collective-permute-start(bf16[128,2048]{1,0:T(8,128)(2,1)} %slice.861), channel_id=1, source_target_pairs={{0,1},{1,0},{2,3},{3,2},{4,5},{5,4},{6,7},{7,6},{8,9},{9,8},{10,11... | collective-permute-start | bytes 1572872 | tf_op jit(solution)/shard_map/ppermute | solution.py:73
  391.7 33.5 %collective-permute-start.52 = (bf16[128,2048]{1,0:T(8,128)(2,1)}, bf16[128,2048]{1,0:T(8,128)(2,1)}, u32[]{:S(2)}, u32[]{:S(2)}) collective-permute-start(bf16[128,2048]{1,0:T(8,128)(2,1)} %slice.860), channel_id=1, source_target_pairs={{0,1},{1,0},{2,3},{3,2},{4,5},{5,4},{6,7},{7,6},{8,9},{9,8},{10,11... | collective-permute-start | bytes 1572872 | tf_op jit(solution)/shard_map/ppermute | solution.py:73
  439.9 15.9 %collective-permute-start.51 = (bf16[64,2048]{1,0:T(8,128)(2,1)S(1)}, bf16[64,2048]{1,0:T(8,128)(2,1)S(1)}, u32[]{:S(2)}, u32[]{:S(2)}) collective-permute-start(bf16[64,2048]{1,0:T(8,128)(2,1)S(1)} %copy-done.52), channel_id=1, source_target_pairs={{0,2},{1,3},{2,0},{3,1},{4,6},{5,7},{6,4},{7,5},{8,10},{9,11},{10,... | collective-permute-start | bytes 786440 | tf_op jit(solution)/shard_map/ppermute | solution.py:73
  441.8 43.7 %collective-permute-start.49 = (bf16[256,2048]{1,0:T(8,128)(2,1)}, bf16[256,2048]{1,0:T(8,128)(2,1)S(1)}, u32[]{:S(2)}, u32[]{:S(2)}) collective-permute-start(bf16[256,2048]{1,0:T(8,128)(2,1)} %pad_maximum_fusion.16), channel_id=1, source_target_pairs={{0,1},{1,0},{2,3},{3,2},{4,5},{5,4},{6,7},{7,6},{8,9},{9,8},{10,11... | collective-permute-start | bytes 3145736 | tf_op jit(solution)/shard_map/ppermute | solution.py:73
  443.3 33.3 %collective-permute-start.59 = (bf16[64,2048]{1,0:T(8,128)(2,1)S(1)}, bf16[64,2048]{1,0:T(8,128)(2,1)S(1)}, u32[]{:S(2)}, u32[]{:S(2)}) collective-permute-start(bf16[64,2048]{1,0:T(8,128)(2,1)S(1)} %copy-done.53), channel_id=1, source_target_pairs={{0,2},{1,3},{2,0},{3,1},{4,6},{5,7},{6,4},{7,5},{8,10},{9,11},{10,... | collective-permute-start | bytes 786440 | tf_op jit(solution)/shard_map/ppermute | solution.py:73
  456.2 26.2 %collective-permute-start.56 = (bf16[64,2048]{1,0:T(8,128)(2,1)S(1)}, bf16[64,2048]{1,0:T(8,128)(2,1)S(1)}, u32[]{:S(2)}, u32[]{:S(2)}) collective-permute-start(bf16[64,2048]{1,0:T(8,128)(2,1)S(1)} %fusion.31), channel_id=1, source_target_pairs={{0,2},{1,3},{2,0},{3,1},{4,6},{5,7},{6,4},{7,5},{8,10},{9,11},{10,... | collective-permute-start | bytes 786440 | tf_op jit(solution)/shard_map/ppermute | solution.py:789
  456.8 23.8 %collective-permute-start.57 = (bf16[2,256,640]{2,1,0:T(8,128)(2,1)S(1)}, bf16[2,256,640]{2,1,0:T(8,128)(2,1)S(1)}, u32[]{:S(2)}, u32[]{:S(2)}) collective-permute-start(bf16[2,256,640]{2,1,0:T(8,128)(2,1)S(1)} %pad_maximum_fusion.23), channel_id=1, source_target_pairs={{0,8},{8,0},{16,24},{24,16},{1,9},{9,1},{17,25},{25,17},{2,10},{10... | collective-permute-start | bytes 1966088 | tf_op jit(solution)/shard_map/ppermute | solution.py:149
  458.6 22.1 %collective-permute-start.58 = (bf16[2,256,640]{2,1,0:T(8,128)(2,1)S(1)}, bf16[2,256,640]{2,1,0:T(8,128)(2,1)S(1)}, u32[]{:S(2)}, u32[]{:S(2)}) collective-permute-start(bf16[2,256,640]{2,1,0:T(8,128)(2,1)S(1)} %pad_maximum_fusion.24), channel_id=1, source_target_pairs={{0,16},{8,24},{16,0},{24,8},{1,17},{9,25},{17,1},{25,9},{2,18},{10... | collective-permute-start | bytes 1966088 | tf_op jit(solution)/shard_map/ppermute | solution.py:150
  477.1 32.0 %collective-permute-start.61 = (bf16[64,2048]{1,0:T(8,128)(2,1)S(1)}, bf16[64,2048]{1,0:T(8,128)(2,1)S(1)}, u32[]{:S(2)}, u32[]{:S(2)}) collective-permute-start(bf16[64,2048]{1,0:T(8,128)(2,1)S(1)} %fusion.24), channel_id=1, source_target_pairs={{0,2},{1,3},{2,0},{3,1},{4,6},{5,7},{6,4},{7,5},{8,10},{9,11},{10,... | collective-permute-start | bytes 786440 | tf_op jit(solution)/shard_map/ppermute | solution.py:791
  480.8 46.7 %collective-permute-start.67 = (bf16[256,640]{1,0:T(8,128)(2,1)S(1)}, bf16[256,640]{1,0:T(8,128)(2,1)S(1)}, u32[]{:S(2)}, u32[]{:S(2)}) collective-permute-start(bf16[256,640]{1,0:T(8,128)(2,1)S(1)} %fusion.51), channel_id=1, source_target_pairs={{0,8},{8,0},{16,24},{24,16},{1,9},{9,1},{17,25},{25,17},{2,10},{10... | collective-permute-start | bytes 983048 | tf_op jit(solution)/shard_map/ppermute | solution.py:164
  482.4 25.3 %collective-permute-start.62 = (bf16[128,2048]{1,0:T(8,128)(2,1)S(1)}, bf16[128,2048]{1,0:T(8,128)(2,1)S(1)}, u32[]{:S(2)}, u32[]{:S(2)}) collective-permute-start(bf16[128,2048]{1,0:T(8,128)(2,1)S(1)} %pad_maximum_fusion.29), channel_id=1, source_target_pairs={{0,1},{1,0},{2,3},{3,2},{4,5},{5,4},{6,7},{7,6},{8,9},{9,8},{10,11... | collective-permute-start | bytes 1572872 | tf_op jit(solution)/shard_map/ppermute | solution.py:796
  485.9 31.9 %collective-permute-start.60 = (bf16[128,2048]{1,0:T(8,128)(2,1)S(1)}, bf16[128,2048]{1,0:T(8,128)(2,1)S(1)}, u32[]{:S(2)}, u32[]{:S(2)}) collective-permute-start(bf16[128,2048]{1,0:T(8,128)(2,1)S(1)} %pad_maximum_fusion.30), channel_id=1, source_target_pairs={{0,2},{1,3},{2,0},{3,1},{4,6},{5,7},{6,4},{7,5},{8,10},{9,11},{10,... | collective-permute-start | bytes 1572872 | tf_op jit(solution)/shard_map/ppermute | solution.py:73
  486.6 33.2 %collective-permute-start.70 = (f32[2,2048]{1,0:T(2,128)S(1)}, f32[2,2048]{1,0:T(2,128)S(1)}, u32[]{:S(2)}, u32[]{:S(2)}) collective-permute-start(f32[2,2048]{1,0:T(2,128)S(1)} %fusion.69), channel_id=1, source_target_pairs={{0,8},{8,0},{16,24},{24,16},{1,9},{9,1},{17,25},{25,17},{2,10},{10... | collective-permute-start | bytes 49160 | tf_op jit(solution)/shard_map/ppermute | solution.py:220
  519.8 27.0 %collective-permute-start.64 = (bf16[128,2048]{1,0:T(8,128)(2,1)}, bf16[128,2048]{1,0:T(8,128)(2,1)}, u32[]{:S(2)}, u32[]{:S(2)}) collective-permute-start(bf16[128,2048]{1,0:T(8,128)(2,1)} %pad_maximum_fusion.31), channel_id=1, source_target_pairs={{0,1},{1,0},{2,3},{3,2},{4,5},{5,4},{6,7},{7,6},{8,9},{9,8},{10,11... | collective-permute-start | bytes 1572872 | tf_op jit(solution)/shard_map/ppermute | solution.py:801
  519.9 26.9 %collective-permute-start.63 = (bf16[128,2048]{1,0:T(8,128)(2,1)S(1)}, bf16[128,2048]{1,0:T(8,128)(2,1)S(1)}, u32[]{:S(2)}, u32[]{:S(2)}) collective-permute-start(bf16[128,2048]{1,0:T(8,128)(2,1)S(1)} %pad_maximum_fusion.32), channel_id=1, source_target_pairs={{0,2},{1,3},{2,0},{3,1},{4,6},{5,7},{6,4},{7,5},{8,10},{9,11},{10,... | collective-permute-start | bytes 1572872 | tf_op jit(solution)/shard_map/ppermute | solution.py:804
  522.0 33.2 %collective-permute-start.74 = (f32[2,2048]{1,0:T(2,128)S(1)}, f32[2,2048]{1,0:T(2,128)S(1)}, u32[]{:S(2)}, u32[]{:S(2)}) collective-permute-start(f32[2,2048]{1,0:T(2,128)S(1)} %add_add_fusion.1), channel_id=1, source_target_pairs={{0,1},{1,0},{2,3},{3,2},{4,5},{5,4},{6,7},{7,6},{8,9},{9,8},{10,11... | collective-permute-start | bytes 49160 | tf_op jit(solution)/shard_map/ppermute | solution.py:220
  527.4 27.8 %collective-permute-start.75 = (f32[2,2048]{1,0:T(2,128)S(1)}, f32[2,2048]{1,0:T(2,128)S(1)}, u32[]{:S(2)}, u32[]{:S(2)}) collective-permute-start(f32[2,2048]{1,0:T(2,128)S(1)} %add_add_fusion.1), channel_id=1, source_target_pairs={{0,2},{1,3},{2,0},{3,1},{4,6},{5,7},{6,4},{7,5},{8,10},{9,11},{10,... | collective-permute-start | bytes 49160 | tf_op jit(solution)/shard_map/ppermute | solution.py:220
  534.4 20.9 %collective-permute-start.76 = (f32[2,2048]{1,0:T(2,128)S(1)}, f32[2,2048]{1,0:T(2,128)S(1)}, u32[]{:S(2)}, u32[]{:S(2)}) collective-permute-start(f32[2,2048]{1,0:T(2,128)S(1)} %add_add_fusion.1), channel_id=1, source_target_pairs={{0,3},{1,2},{2,1},{3,0},{4,7},{5,6},{6,5},{7,4},{8,11},{9,10},{10,... | collective-permute-start | bytes 49160 | tf_op jit(solution)/shard_map/ppermute | solution.py:220
  547.9 21.8 %collective-permute-start.73 = (bf16[256,2048]{1,0:T(8,128)(2,1)}, bf16[256,2048]{1,0:T(8,128)(2,1)S(1)}, u32[]{:S(2)}, u32[]{:S(2)}) collective-permute-start(bf16[256,2048]{1,0:T(8,128)(2,1)} %pad_maximum_fusion.17), channel_id=1, source_target_pairs={{0,1},{1,0},{2,3},{3,2},{4,5},{5,4},{6,7},{7,6},{8,9},{9,8},{10,11... | collective-permute-start | bytes 3145736 | tf_op jit(solution)/shard_map/ppermute | solution.py:824
  (102 other events, 752.2 us)
Sparse Core Ops, SparseCore 0:
  28.1 72.1 all-gather.5
  102.7 87.4 all-gather.3
  192.2 55.8 all-gather.7
  288.9 51.4 reduce-scatter.3
  343.2 52.5 reduce-scatter.5
  408.7 52.5 reduce-scatter.7

commit v4 on v3

--- a/solution.py
+++ b/solution.py
@@ -765,7 +765,6 @@
     k1, g1, t1 = halved(v1, far)
     k_out, g_out, t_out = halved(down, near)
     d_qkv = stack(*[joined(q, d_kv, h, s) for s in range(2) for h, q in enumerate((dq_0, dq_1))])
-    g_qkv = dot_0(normed, after(d_qkv, t0, t1, t_out)).astype(BF)
 
     def input_of(h, d_hidden, total):
         d_rows, gain = norm_backward(slice_of(rows, h), slice_of(scale_own, h), gain_a, total)
@@ -776,6 +775,11 @@
     keep, send = output_grad(
         core.astype(jnp.int32).reshape(1), [a[0] for a in attn_own], [a[1] for a in attn_own], dh_all, shard, fsdp
     )
+    gain_0, c0 = input_of(0, dh_0, summed(k0, after(g0, keep))[0])
+    a0 = lax.ppermute(c0, "tp", far)
+    gain_1, c1 = input_of(1, dh_1, summed(k1, after(g1, c0))[0])
+    a1 = lax.ppermute(c1, "tp", far)
+    g_qkv = dot_0(normed, after(d_qkv, c0)).astype(BF)
     g_output = (keep.astype(F32) + swap(send).astype(F32)).astype(BF)
     g_qkv = g_qkv.reshape(fsdp, -1, narrow)
     joint = g_qkv.shape[1] == g_output.shape[1]
@@ -785,12 +789,8 @@
         reduce = [Scatter(g_qkv), Scatter(g_output)]
     firsts = [item.first_sent for item in reduce]
 
-    gain_0, c0 = input_of(0, dh_0, summed(k0, after(g0, g_qkv, g_output, *firsts))[0])
-    a0 = lax.ppermute(c0, "tp", far)
-    gain_1, c1 = input_of(1, dh_1, summed(k1, after(g1, c0))[0])
-    a1 = lax.ppermute(c1, "tp", far)
     for item in reduce:
-        item.second(c1)
+        item.second(c1, *firsts)
     tokens = [r.token for r in reduce]
     cur0 = stack(c0, after(a0, *tokens))
     b0 = lax.ppermute(cur0, "tp", near)

time: 589 us -> 585 us (level)
  waiting for transfers between devices: 208 us -> 190 us
  other arithmetic: 74.7 us -> 89.8 us
    ppermute x14, waiting for transfers between devices: 102 us -> 82.4 us  [halved(): return ([v[:half] for v in values], lax.ppermute(sent, 'tp', pairs), sent)]
    ppermute x1, waiting for transfers between devices: 0.01 us -> 8.47 us  [__init__(): self.by_near = lax.ppermute(to_near, 'fsdp', self.near)]
    unnamed x152 -> x154, local copies, waits for them, and re-layouts: 29.1 us -> 27.2 us
  transfers between devices with their start and end apart: 83 -> 83, of which waited for: 31 -> 30; matrix products, arithmetic and copies ran while one was open for 30% -> 33% of each run, Pallas kernels for 11% -> 11%
where the time goes in v4:
time: 585 us; the launch traced here: 579 us
  waiting for transfers between devices  190 us (32%)
  other arithmetic  89.8 us (15%)
  Pallas kernels  75.5 us (13%)
  starting transfers between devices  72.9 us (12%)
  local copies, waits for them, and re-layouts  69.1 us (12%)
  matrix products  66.5 us (11%)
  between operations  16 us (3%)
    ppermute x14, waiting for transfers between devices, halved(): return ([v[:half] for v in values], lax.ppermute(sent, 'tp', pairs), sent)  82.4 us
    dot_general x8, matrix products, dot_t(): lax.dot_general(left, right, (((1,), (1,)), ((), ())), preferred_element_...  36.5 us
    unnamed x154, local copies, waits for them, and re-layouts  27.2 us
    dot_general x9, matrix products, dotf(): return jnp.dot(left, right, preferred_element_type=F32)  25.9 us
    pallas_call x3, Pallas kernels, grad_kernel(): pl.pallas_call(kernel, grid=(wide // block,), in_specs=[pl.BlockSpec((row...  25.4 us
    pallas_call x2, Pallas kernels, attend_back(): pl.pallas_call(kernel, in_specs=[SCALARS] + [pl.BlockSpec()] * (10 + 2 *...  19.5 us
    ppermute x1, waiting for transfers between devices, body(): b0 = lax.ppermute(cur0, 'tp', near)  15.9 us
    concatenate x18, other arithmetic, stack(): return jnp.concatenate(parts, axis=0)  15.6 us
  transfers between devices with their start and end apart: 83, of which 30 were waited for; matrix products, arithmetic and copies ran while one was open for 33% of the time, Pallas kernels for 11%

profile of v4, /device:TPU:0, one launch (start us, length us, event | category | flops | bytes accessed | tf_op | source)
XLA Modules:
  0.0 579.4 jit_solution(9874476249090343912)
XLA Ops:
  19.1 6.3 %collective-permute-done.4 = f32[512,2048]{1,0:T(8,128)} collective-permute-done((f32[512,2048]{1,0:T(8,128)}, f32[512,2048]{1,0:T(8,128)}, u32[]{:S(2)}, u32[]{:S(2)}) %collective-permute-start.4) | collective-permute-done | bytes 4194336 | tf_op jit(solution)/shard_map/ppermute | solution.py:40
  33.5 3.2 broadcast_select_fusion.20
  39.4 3.0 collective-permute-start.1
  45.5 3.9 arrange.3
  49.5 12.4 %collective-permute-done.1 = bf16[544,384]{1,0:T(8,128)(2,1)S(1)} collective-permute-done((bf16[544,384]{1,0:T(8,128)(2,1)}, bf16[544,384]{1,0:T(8,128)(2,1)S(1)}, u32[]{:S(2)}, u32[]{:S(2)}) %collective-permute-start.1) | collective-permute-done | bytes 417824 | tf_op jit(solution)/shard_map/ppermute | solution.py:184
  82.3 2.9 multiply_convert_fusion.1
  87.2 3.5 fusion.qkv_ref
  90.7 7.6 %attend_first.1 = (bf16[1024,256]{1,0:T(8,128)(2,1)}, bf16[1024,128]{1,0:T(8,128)(2,1)}, bf16[512,256]{1,0:T(8,128)(2,1)}, f32[512,4]{1,0:T(8,128)}) custom-call(s32[2]{0:T(128)} %pad_add_fusion.at_ref, f32[1024,384]{1,0:T(8,128)} %fusion.qkv_ref, f32[1024,128]{1,0:T(8,128)} %get-tuple-element.355.cos_ref, f32[1024,128]{1,0:T(8,128)} %get-tuple-element.353.sin_ref, ...), custom_call_target="tpu_custom_call" | custom-call | flops 8000000000 | bytes 1572864 | tf_op jit(solution)/shard_map/attend_first/pallas_call | solution.py:396
  110.2 6.2 %collective-permute-done.16 = bf16[1024,256]{1,0:T(8,128)(2,1)S(1)} collective-permute-done((bf16[1024,256]{1,0:T(8,128)(2,1)S(1)}, bf16[1024,256]{1,0:T(8,128)(2,1)S(1)}, u32[]{:S(2)}, u32[]{:S(2)}) %collective-permute-start.16) | collective-permute-done | bytes 524320 | tf_op jit(solution)/shard_map/ppermute | solution.py:87
  117.2 5.8 %attend_next.1 = (bf16[512,256]{1,0:T(8,128)(2,1)}, f32[512,4]{1,0:T(8,128)}) custom-call(s32[2]{0:T(128)} %pad_add_fusion.at_ref, bf16[1024,256]{1,0:T(8,128)(2,1)} %get-tuple-element.126.q_ref, bf16[1024,128]{1,0:T(8,128)(2,1)} %get-tuple-element.128.kv_ref), custom_call_target="tpu_custom_call" | custom-call | flops 5000000000 | bytes 524288 | tf_op jit(solution)/shard_map/attend_next/pallas_call | solution.py:418
  139.8 3.1 fusion.79
  142.9 7.6 %collective-permute-done.14 = bf16[128,2048]{1,0:T(8,128)(2,1)S(1)} collective-permute-done((bf16[128,2048]{1,0:T(8,128)(2,1)S(1)}, bf16[128,2048]{1,0:T(8,128)(2,1)S(1)}, u32[]{:S(2)}, u32[]{:S(2)}) %collective-permute-start.14) | collective-permute-done | bytes 524320 | tf_op jit(solution)/shard_map/ppermute | solution.py:73
  151.6 15.3 %collective-permute-done.19 = bf16[128,2048]{1,0:T(8,128)(2,1)S(1)} collective-permute-done((bf16[128,2048]{1,0:T(8,128)(2,1)S(1)}, bf16[128,2048]{1,0:T(8,128)(2,1)S(1)}, u32[]{:S(2)}, u32[]{:S(2)}) %collective-permute-start.19) | collective-permute-done | bytes 524320 | tf_op jit(solution)/shard_map/ppermute | solution.py:73
  172.2 13.9 %collective-permute-done.21 = bf16[64,2048]{1,0:T(8,128)(2,1)S(1)} collective-permute-done((bf16[64,2048]{1,0:T(8,128)(2,1)S(1)}, bf16[64,2048]{1,0:T(8,128)(2,1)S(1)}, u32[]{:S(2)}, u32[]{:S(2)}) %collective-permute-start.21) | collective-permute-done | bytes 262176 | tf_op jit(solution)/shard_map/ppermute | solution.py:73
  187.7 4.0 collective-permute-done.20
  197.9 11.1 %collective-permute-done.23 = bf16[64,2048]{1,0:T(8,128)(2,1)S(1)} collective-permute-done((bf16[64,2048]{1,0:T(8,128)(2,1)S(1)}, bf16[64,2048]{1,0:T(8,128)(2,1)S(1)}, u32[]{:S(2)}, u32[]{:S(2)}) %collective-permute-start.23) | collective-permute-done | bytes 262176 | tf_op jit(solution)/shard_map/ppermute | solution.py:646
  209.1 3.4 collective-permute-start.27
  216.3 7.7 %fusion.96 = f32[512,2048]{1,0:T(8,128)S(1)} fusion(bf16[512,2048]{1,0:T(8,128)(2,1)} %constant_dynamic-update-slice_fusion.5.refs_0_, bf16[2048,2048]{1,0:T(8,128)(2,1)} %all-gather.4.cloned.1.call-done), kind=kOutput, calls=%fused_computation.357 | convolution fusion | flops 4294967296 | bytes 14680064 | tf_op jit(solution)/shard_map/dot_general | solution.py:19
  224.2 4.7 multiply_convert_fusion.6
  228.9 4.5 fusion.72
  236.4 6.3 %fusion.97 = f32[512,2048]{1,0:T(8,128)} fusion(bf16[512,2048]{1,0:T(8,128)(2,1)S(1)} %constant_dynamic-update-slice_fusion.10.refs_1_, bf16[2048,2048]{1,0:T(8,128)(2,1)S(1)} %copy-done.61), kind=kOutput, calls=%fused_computation.358 | convolution fusion | flops 4294967296 | bytes 14680064 | tf_op jit(solution)/shard_map/dot_general | solution.py:19
  244.9 7.9 %multiply_convert_fusion.3 = (bf16[512,1024]{1,0:T(8,128)(2,1)S(1)}, bf16[512,1024]{1,0:T(8,128)(2,1)S(1)}, bf16[512,1024]{1,0:T(8,128)(2,1)}) fusion(f32[512,2048]{1,0:T(8,128)} %fusion.97, bf16[512,2048]{1,0:T(8,128)(2,1)S(1)} %copy-done.30, bf16[1024,2048]{1,0:T(8,128)(2,1)} %all-gather.6.cloned.1.call-done), kind=kOutput, calls=%fused_computation.41 | convolution fusion | flops 2155347968 | bytes 13631488 | tf_op jit(solution)/shard_map/dot_general | solution.py:23
  253.0 4.1 collective-permute-done.31
  257.2 4.5 fusion.98
  267.0 11.8 %collective-permute-done.32 = bf16[64,2048]{1,0:T(8,128)(2,1)S(1)} collective-permute-done((bf16[64,2048]{1,0:T(8,128)(2,1)S(1)}, bf16[64,2048]{1,0:T(8,128)(2,1)S(1)}, u32[]{:S(2)}, u32[]{:S(2)}) %collective-permute-start.32) | collective-permute-done | bytes 262176 | tf_op jit(solution)/shard_map/ppermute | solution.py:73
  281.1 6.0 %convolution_convert_fusion.2 = bf16[64,2048]{1,0:T(8,128)(2,1)S(1)} fusion(bf16[64,2048]{1,0:T(8,128)(2,1)S(1)} %get-tuple-element.227, bf16[2048,2048]{1,0:T(8,128)(2,1)} %all-gather.8.cloned.1.call-done), kind=kOutput, calls=%fused_computation.18 | convolution fusion | flops 537001984 | bytes 8912896 | tf_op jit(solution)/shard_map/dot_general | solution.py:23
  287.8 8.4 %grad.3 = bf16[2048,1024]{1,0:T(8,128)(2,1)} custom-call(bf16[512,2048]{1,0:T(8,128)(2,1)} %constant_dynamic-update-slice_fusion.5.refs_0_, bf16[512,2048]{1,0:T(8,128)(2,1)} %copy-done.56, bf16[512,2048]{1,0:T(8,128)(2,1)} %pad_maximum_fusion.7.refs_2_, bf16[512,2048]{1,0:T(8,128)(2,1)} %copy-done.31), custom_call_target="tpu_custom_call" | custom-call | flops 8589934592 | bytes 8388608 | tf_op jit(solution)/shard_map/grad/pallas_call | solution.py:236
  296.3 13.4 %collective-permute-done.37 = bf16[128,2048]{1,0:T(8,128)(2,1)S(1)} collective-permute-done((bf16[128,2048]{1,0:T(8,128)(2,1)S(1)}, bf16[128,2048]{1,0:T(8,128)(2,1)S(1)}, u32[]{:S(2)}, u32[]{:S(2)}) %collective-permute-start.37) | collective-permute-done | bytes 524320 | tf_op jit(solution)/shard_map/ppermute | solution.py:73
  317.0 8.4 %grad.4 = bf16[2048,1024]{1,0:T(8,128)(2,1)} custom-call(bf16[512,2048]{1,0:T(8,128)(2,1)} %constant_dynamic-update-slice_fusion.5.refs_0_, bf16[512,2048]{1,0:T(8,128)(2,1)} %copy-done.56, bf16[512,2048]{1,0:T(8,128)(2,1)} %pad_maximum_fusion.7.refs_2_, bf16[512,2048]{1,0:T(8,128)(2,1)} %copy-done.31), custom_call_target="tpu_custom_call" | custom-call | flops 8589934592 | bytes 8388608 | tf_op jit(solution)/shard_map/grad/pallas_call | solution.py:236
  325.8 2.8 collective-permute-done.38
  332.7 6.2 %convolution_convert_fusion.1 = bf16[64,2048]{1,0:T(8,128)(2,1)S(1)} fusion(bf16[64,2048]{1,0:T(8,128)(2,1)S(1)} %get-tuple-element.225, bf16[2048,2048]{1,0:T(8,128)(2,1)} %all-gather.8.cloned.1.call-done), kind=kOutput, calls=%fused_computation.17 | convolution fusion | flops 537001984 | bytes 8912896 | tf_op jit(solution)/shard_map/dot_general | solution.py:23
  349.2 8.3 %attend_back.2 = (bf16[512,256]{1,0:T(8,128)(2,1)}, bf16[512,256]{1,0:T(8,128)(2,1)}, f32[2,1024,128]{2,1,0:T(8,128)}, f32[2,1024,128]{2,1,0:T(8,128)}) custom-call(s32[2]{0:T(128)} %pad_add_fusion.at_ref, bf16[1024,256]{1,0:T(8,128)(2,1)} %get-tuple-element.126.q_ref, bf16[1024,128]{1,0:T(8,128)(2,1)} %get-tuple-element.128.kv_ref, ...), custom_call_target="tpu_custom_call" | custom-call | flops 8000000000 | bytes 1048576 | tf_op jit(solution)/shard_map/attend_back/pallas_call | solution.py:510
  362.7 11.3 %attend_back.3 = (bf16[512,256]{1,0:T(8,128)(2,1)}, bf16[512,256]{1,0:T(8,128)(2,1)}, bf16[1024,128]{1,0:T(8,128)(2,1)}, bf16[1024,128]{1,0:T(8,128)(2,1)}) custom-call(s32[2]{0:T(128)} %pad_add_fusion.at_ref, bf16[1024,256]{1,0:T(8,128)(2,1)} %get-tuple-element.126.q_ref, bf16[1024,128]{1,0:T(8,128)(2,1)} %get-tuple-element.128.kv_ref, ...), custom_call_target="tpu_custom_call" | custom-call | flops 8000000000 | bytes 1048576 | tf_op jit(solution)/shard_map/attend_back/pallas_call | solution.py:510
  404.7 5.3 collective-permute-done.48
  409.9 8.6 %grad.5 = bf16[1024,2048]{1,0:T(8,128)(2,1)} custom-call(bf16[512,1024]{1,0:T(8,128)(2,1)} %get-tuple-element.176.refs_0_, bf16[512,1024]{1,0:T(8,128)(2,1)} %get-tuple-element.177.refs_1_, bf16[512,2048]{1,0:T(8,128)(2,1)} %pad_maximum_fusion.5.refs_2_, bf16[512,2048]{1,0:T(8,128)(2,1)} %pad_maximum_fusion.6.refs_3_), custom_call_target="tpu_custom_call" | custom-call | flops 8589934592 | bytes 6291456 | tf_op jit(solution)/shard_map/grad/pallas_call | solution.py:236
  426.0 3.5 slice_add_fusion.1
  445.0 4.9 output_grad.1
  454.3 4.0 convolution_convert_fusion
  458.4 6.7 %collective-permute-done.59 = bf16[64,2048]{1,0:T(8,128)(2,1)} collective-permute-done((bf16[64,2048]{1,0:T(8,128)(2,1)}, bf16[64,2048]{1,0:T(8,128)(2,1)}, u32[]{:S(2)}, u32[]{:S(2)}) %collective-permute-start.59) | collective-permute-done | bytes 262176 | tf_op jit(solution)/shard_map/ppermute | solution.py:73
  471.1 3.5 collective-permute-start.61
  474.7 8.5 %collective-permute-done.57 = bf16[2,256,640]{2,1,0:T(8,128)(2,1)S(1)} collective-permute-done((bf16[2,256,640]{2,1,0:T(8,128)(2,1)S(1)}, bf16[2,256,640]{2,1,0:T(8,128)(2,1)S(1)}, u32[]{:S(2)}, u32[]{:S(2)}) %collective-permute-start.57) | collective-permute-done | bytes 655392 | tf_op jit(solution)/shard_map/ppermute | solution.py:149
  491.2 15.9 %collective-permute-done.62 = bf16[128,2048]{1,0:T(8,128)(2,1)S(1)} collective-permute-done((bf16[128,2048]{1,0:T(8,128)(2,1)S(1)}, bf16[128,2048]{1,0:T(8,128)(2,1)S(1)}, u32[]{:S(2)}, u32[]{:S(2)}) %collective-permute-start.62) | collective-permute-done | bytes 524320 | tf_op jit(solution)/shard_map/ppermute | solution.py:796
  511.1 3.4 collective-permute-done.60
  519.2 3.3 collective-permute-done.66
  532.8 9.4 %collective-permute-done.63 = bf16[128,2048]{1,0:T(8,128)(2,1)} collective-permute-done((bf16[128,2048]{1,0:T(8,128)(2,1)}, bf16[128,2048]{1,0:T(8,128)(2,1)}, u32[]{:S(2)}, u32[]{:S(2)}) %collective-permute-start.63) | collective-permute-done | bytes 524320 | tf_op jit(solution)/shard_map/ppermute | solution.py:804
  546.6 4.2 arrange.4
  552.7 12.0 %collective-permute-done.73 = bf16[256,2048]{1,0:T(8,128)(2,1)} collective-permute-done((bf16[256,2048]{1,0:T(8,128)(2,1)S(1)}, bf16[256,2048]{1,0:T(8,128)(2,1)}, u32[]{:S(2)}, u32[]{:S(2)}) %collective-permute-start.73) | collective-permute-done | bytes 1048608 | tf_op jit(solution)/shard_map/ppermute | solution.py:824
  568.2 4.2 arrange.5
  (488 shorter events, 236.4 us)
Async XLA Ops:
  7.2 162.1 %all-gather.6.cloned.1.call-start = ((), (), s32[]{:S(2)}) async-start(), calls=%async_computation.4 | async-start | bytes 5242880 | tf_op jit(solution)/shard_map/all_gather | solution.py:591
  29.6 186.6 %all-gather.4.cloned.1.call-start = ((), (), s32[]{:S(2)}) async-start(), calls=%async_computation.3 | async-start | bytes 10485760 | tf_op jit(solution)/shard_map/all_gather | solution.py:590
  32.3 248.8 %all-gather.8.cloned.1.call-start = ((), (), s32[]{:S(2)}) async-start(), calls=%async_computation.5 | async-start | bytes 9437184 | tf_op jit(solution)/shard_map/all_gather | solution.py:613
  39.4 22.5 %collective-permute-start.1 = (bf16[544,384]{1,0:T(8,128)(2,1)}, bf16[544,384]{1,0:T(8,128)(2,1)S(1)}, u32[]{:S(2)}, u32[]{:S(2)}) collective-permute-start(bf16[544,384]{1,0:T(8,128)(2,1)} %pad_maximum_fusion.33), channel_id=1, source_target_pairs={{0,8},{8,0},{16,24},{24,16},{1,9},{9,1},{17,25},{25,17},{2,10},{10... | collective-permute-start | bytes 1253384 | tf_op jit(solution)/shard_map/ppermute | solution.py:184
  42.4 20.9 %collective-permute-start.2 = (bf16[544,384]{1,0:T(8,128)(2,1)}, bf16[544,384]{1,0:T(8,128)(2,1)S(1)}, u32[]{:S(2)}, u32[]{:S(2)}) collective-permute-start(bf16[544,384]{1,0:T(8,128)(2,1)} %pad_maximum_fusion.33), channel_id=1, source_target_pairs={{0,16},{8,24},{16,0},{24,8},{1,17},{9,25},{17,1},{25,9},{2,18},{10... | collective-permute-start | bytes 1253384 | tf_op jit(solution)/shard_map/ppermute | solution.py:185
  49.4 90.4 %collective-permute-start.24 = (bf16[512,2048]{1,0:T(8,128)(2,1)}, bf16[512,2048]{1,0:T(8,128)(2,1)}, u32[]{:S(2)}, u32[]{:S(2)}) collective-permute-start(bf16[512,2048]{1,0:T(8,128)(2,1)} %arrange.3), channel_id=1, source_target_pairs={{0,4},{4,0},{1,5},{5,1},{2,6},{6,2},{3,7},{7,3},{8,12},{12,8},{9,1... | collective-permute-start | bytes 6291464 | tf_op jit(solution)/shard_map/ppermute | solution.py:40
  77.5 20.8 %collective-permute-start.8 = (bf16[512,256]{1,0:T(8,128)(2,1)S(1)}, bf16[512,256]{1,0:T(8,128)(2,1)S(1)}, u32[]{:S(2)}, u32[]{:S(2)}) collective-permute-start(bf16[512,256]{1,0:T(8,128)(2,1)S(1)} %copy-done.25), channel_id=1, source_target_pairs={{0,8},{8,0},{16,24},{24,16},{1,9},{9,1},{17,25},{25,17},{2,10},{10... | collective-permute-start | bytes 786440 | tf_op jit(solution)/shard_map/ppermute | solution.py:184
  78.0 20.3 %collective-permute-start.9 = (bf16[512,256]{1,0:T(8,128)(2,1)S(1)}, bf16[512,256]{1,0:T(8,128)(2,1)S(1)}, u32[]{:S(2)}, u32[]{:S(2)}) collective-permute-start(bf16[512,256]{1,0:T(8,128)(2,1)S(1)} %copy-done.25), channel_id=1, source_target_pairs={{0,16},{8,24},{16,0},{24,8},{1,17},{9,25},{17,1},{25,9},{2,18},{10... | collective-permute-start | bytes 786440 | tf_op jit(solution)/shard_map/ppermute | solution.py:185
  80.0 22.2 %collective-permute-start.15 = (bf16[512,256]{1,0:T(8,128)(2,1)S(1)}, bf16[512,256]{1,0:T(8,128)(2,1)S(1)}, u32[]{:S(2)}, u32[]{:S(2)}) collective-permute-start(bf16[512,256]{1,0:T(8,128)(2,1)S(1)} %copy-done.25), channel_id=1, source_target_pairs={{0,2},{1,3},{2,0},{3,1},{4,6},{5,7},{6,4},{7,5},{8,10},{9,11},{10,... | collective-permute-start | bytes 786440 | tf_op jit(solution)/shard_map/ppermute | solution.py:86
  100.6 33.6 %collective-permute-start.13 = (bf16[256,256]{1,0:T(8,128)(2,1)}, bf16[256,256]{1,0:T(8,128)(2,1)}, u32[]{:S(2)}, u32[]{:S(2)}) collective-permute-start(bf16[256,256]{1,0:T(8,128)(2,1)} %get-tuple-element.315), channel_id=1, source_target_pairs={{0,4},{4,0},{1,5},{5,1},{2,6},{6,2},{3,7},{7,3},{8,12},{12,8},{9,1... | collective-permute-start | bytes 393224 | tf_op jit(solution)/shard_map/ppermute | solution.py:40
  108.8 15.9 %collective-permute-start.12 = (bf16[512,1024]{1,0:T(8,128)(2,1)}, bf16[512,1024]{1,0:T(8,128)(2,1)}, u32[]{:S(2)}, u32[]{:S(2)}) collective-permute-start(bf16[512,1024]{1,0:T(8,128)(2,1)} %pad_maximum_fusion.15), channel_id=1, source_target_pairs={{0,4},{4,0},{1,5},{5,1},{2,6},{6,2},{3,7},{7,3},{8,12},{12,8},{9,1... | collective-permute-start | bytes 3145736 | tf_op jit(solution)/shard_map/ppermute | solution.py:40
  139.2 27.7 %collective-permute-start.19 = (bf16[128,2048]{1,0:T(8,128)(2,1)S(1)}, bf16[128,2048]{1,0:T(8,128)(2,1)S(1)}, u32[]{:S(2)}, u32[]{:S(2)}) collective-permute-start(bf16[128,2048]{1,0:T(8,128)(2,1)S(1)} %slice.864), channel_id=1, source_target_pairs={{0,1},{1,0},{2,3},{3,2},{4,5},{5,4},{6,7},{7,6},{8,9},{9,8},{10,11... | collective-permute-start | bytes 1572872 | tf_op jit(solution)/shard_map/ppermute | solution.py:73
  150.7 17.3 %collective-permute-start.18 = (bf16[64,2048]{1,0:T(8,128)(2,1)S(1)}, bf16[64,2048]{1,0:T(8,128)(2,1)S(1)}, u32[]{:S(2)}, u32[]{:S(2)}) collective-permute-start(bf16[64,2048]{1,0:T(8,128)(2,1)S(1)} %slice.873), channel_id=1, source_target_pairs={{0,2},{1,3},{2,0},{3,1},{4,6},{5,7},{6,4},{7,5},{8,10},{9,11},{10,... | collective-permute-start | bytes 786440 | tf_op jit(solution)/shard_map/ppermute | solution.py:73
  167.1 19.1 %collective-permute-start.21 = (bf16[64,2048]{1,0:T(8,128)(2,1)S(1)}, bf16[64,2048]{1,0:T(8,128)(2,1)S(1)}, u32[]{:S(2)}, u32[]{:S(2)}) collective-permute-start(bf16[64,2048]{1,0:T(8,128)(2,1)S(1)} %slice.872), channel_id=1, source_target_pairs={{0,2},{1,3},{2,0},{3,1},{4,6},{5,7},{6,4},{7,5},{8,10},{9,11},{10,... | collective-permute-start | bytes 786440 | tf_op jit(solution)/shard_map/ppermute | solution.py:73
  169.3 255.5 %reduce-scatter.4.cloned.1.call-start = ((), (), s32[]{:S(2)}) async-start(), calls=%async_computation.6 | async-start | bytes 5242880 | tf_op jit(solution)/shard_map/reduce_scatter | solution.py:687
  170.2 21.5 %collective-permute-start.20 = (bf16[64,2048]{1,0:T(8,128)(2,1)S(1)}, bf16[64,2048]{1,0:T(8,128)(2,1)S(1)}, u32[]{:S(2)}, u32[]{:S(2)}) collective-permute-start(bf16[64,2048]{1,0:T(8,128)(2,1)S(1)} %get-tuple-element.232), channel_id=1, source_target_pairs={{0,2},{1,3},{2,0},{3,1},{4,6},{5,7},{6,4},{7,5},{8,10},{9,11},{10,... | collective-permute-start | bytes 786440 | tf_op jit(solution)/shard_map/ppermute | solution.py:644
  191.7 20.8 %collective-permute-start.22 = (bf16[128,2048]{1,0:T(8,128)(2,1)S(1)}, bf16[128,2048]{1,0:T(8,128)(2,1)S(1)}, u32[]{:S(2)}, u32[]{:S(2)}) collective-permute-start(bf16[128,2048]{1,0:T(8,128)(2,1)S(1)} %pad_maximum_fusion.26), channel_id=1, source_target_pairs={{0,1},{1,0},{2,3},{3,2},{4,5},{5,4},{6,7},{7,6},{8,9},{9,8},{10,11... | collective-permute-start | bytes 1572872 | tf_op jit(solution)/shard_map/ppermute | solution.py:648
  197.9 16.7 %collective-permute-start.25 = (bf16[128,2048]{1,0:T(8,128)(2,1)S(1)}, bf16[128,2048]{1,0:T(8,128)(2,1)S(1)}, u32[]{:S(2)}, u32[]{:S(2)}) collective-permute-start(bf16[128,2048]{1,0:T(8,128)(2,1)S(1)} %pad_maximum_fusion.26), channel_id=1, source_target_pairs={{0,4},{4,0},{1,5},{5,1},{2,6},{6,2},{3,7},{7,3},{8,12},{12,8},{9,1... | collective-permute-start | bytes 1572872 | tf_op jit(solution)/shard_map/ppermute | solution.py:40
  212.5 21.6 %collective-permute-start.28 = (bf16[128,2048]{1,0:T(8,128)(2,1)S(1)}, bf16[128,2048]{1,0:T(8,128)(2,1)}, u32[]{:S(2)}, u32[]{:S(2)}) collective-permute-start(bf16[128,2048]{1,0:T(8,128)(2,1)S(1)} %pad_maximum_fusion.27), channel_id=1, source_target_pairs={{0,4},{4,0},{1,5},{5,1},{2,6},{6,2},{3,7},{7,3},{8,12},{12,8},{9,1... | collective-permute-start | bytes 1572872 | tf_op jit(solution)/shard_map/ppermute | solution.py:40
  296.2 128.6 %reduce-scatter.6.cloned.1.call-start = ((), (), s32[]{:S(2)}) async-start(), calls=%async_computation.7 | async-start | bytes 5242880 | tf_op jit(solution)/shard_map/reduce_scatter | solution.py:687
  312.1 16.6 %collective-permute-start.38 = (bf16[64,2048]{1,0:T(8,128)(2,1)S(1)}, bf16[64,2048]{1,0:T(8,128)(2,1)S(1)}, u32[]{:S(2)}, u32[]{:S(2)}) collective-permute-start(bf16[64,2048]{1,0:T(8,128)(2,1)S(1)} %slice.870), channel_id=1, source_target_pairs={{0,2},{1,3},{2,0},{3,1},{4,6},{5,7},{6,4},{7,5},{8,10},{9,11},{10,... | collective-permute-start | bytes 786440 | tf_op jit(solution)/shard_map/ppermute | solution.py:73
  312.6 29.7 %collective-permute-start.34 = (bf16[64,512]{1,0:T(8,128)(2,1)}, bf16[64,512]{1,0:T(8,128)(2,1)}, u32[]{:S(2)}, u32[]{:S(2)}) collective-permute-start(bf16[64,512]{1,0:T(8,128)(2,1)} %get-tuple-element.330), channel_id=1, source_target_pairs={{0,2},{1,3},{2,0},{3,1},{4,6},{5,7},{6,4},{7,5},{8,10},{9,11},{10,... | collective-permute-start | bytes 196616 | tf_op jit(solution)/shard_map/ppermute | solution.py:706
  315.1 28.9 %collective-permute-start.35 = (bf16[64,512]{1,0:T(8,128)(2,1)}, bf16[64,512]{1,0:T(8,128)(2,1)}, u32[]{:S(2)}, u32[]{:S(2)}) collective-permute-start(bf16[64,512]{1,0:T(8,128)(2,1)} %get-tuple-element.329), channel_id=1, source_target_pairs={{0,1},{1,0},{2,3},{3,2},{4,5},{5,4},{6,7},{7,6},{8,9},{9,8},{10,11... | collective-permute-start | bytes 196616 | tf_op jit(solution)/shard_map/ppermute | solution.py:706
  315.4 28.6 %collective-permute-start.36 = (bf16[64,512]{1,0:T(8,128)(2,1)}, bf16[64,512]{1,0:T(8,128)(2,1)}, u32[]{:S(2)}, u32[]{:S(2)}) collective-permute-start(bf16[64,512]{1,0:T(8,128)(2,1)} %get-tuple-element.328), channel_id=1, source_target_pairs={{0,3},{1,2},{2,1},{3,0},{4,7},{5,6},{6,5},{7,4},{8,11},{9,10},{10,... | collective-permute-start | bytes 196616 | tf_op jit(solution)/shard_map/ppermute | solution.py:706
  325.4 199.7 %reduce-scatter.8.cloned.1.call-start = ((), (), s32[]{:S(2)}) async-start(), calls=%async_computation.8 | async-start | bytes 5242880 | tf_op jit(solution)/shard_map/reduce_scatter | solution.py:687
  339.6 17.9 %collective-permute-start.40 = (bf16[64,512]{1,0:T(8,128)(2,1)}, bf16[64,512]{1,0:T(8,128)(2,1)}, u32[]{:S(2)}, u32[]{:S(2)}) collective-permute-start(bf16[64,512]{1,0:T(8,128)(2,1)} %get-tuple-element.334), channel_id=1, source_target_pairs={{0,2},{1,3},{2,0},{3,1},{4,6},{5,7},{6,4},{7,5},{8,10},{9,11},{10,... | collective-permute-start | bytes 196616 | tf_op jit(solution)/shard_map/ppermute | solution.py:706
  339.6 17.9 %collective-permute-start.41 = (bf16[64,512]{1,0:T(8,128)(2,1)}, bf16[64,512]{1,0:T(8,128)(2,1)}, u32[]{:S(2)}, u32[]{:S(2)}) collective-permute-start(bf16[64,512]{1,0:T(8,128)(2,1)} %get-tuple-element.333), channel_id=1, source_target_pairs={{0,1},{1,0},{2,3},{3,2},{4,5},{5,4},{6,7},{7,6},{8,9},{9,8},{10,11... | collective-permute-start | bytes 196616 | tf_op jit(solution)/shard_map/ppermute | solution.py:706
  347.2 27.7 %collective-permute-start.44 = (bf16[128,2048]{1,0:T(8,128)(2,1)S(1)}, bf16[128,2048]{1,0:T(8,128)(2,1)}, u32[]{:S(2)}, u32[]{:S(2)}) collective-permute-start(bf16[128,2048]{1,0:T(8,128)(2,1)S(1)} %pad_maximum_fusion.28), channel_id=1, source_target_pairs={{0,2},{1,3},{2,0},{3,1},{4,6},{5,7},{6,4},{7,5},{8,10},{9,11},{10,... | collective-permute-start | bytes 1572872 | tf_op jit(solution)/shard_map/ppermute | solution.py:726
  383.5 26.4 %collective-permute-start.48 = (bf16[256,2048]{1,0:T(8,128)(2,1)}, bf16[256,2048]{1,0:T(8,128)(2,1)}, u32[]{:S(2)}, u32[]{:S(2)}) collective-permute-start(bf16[256,2048]{1,0:T(8,128)(2,1)} %constant_dynamic-update-slice_fusion.22), channel_id=1, source_target_pairs={{0,1},{1,0},{2,3},{3,2},{4,5},{5,4},{6,7},{7,6},{8,9},{9,8},{10,11... | collective-permute-start | bytes 3145736 | tf_op jit(solution)/shard_map/ppermute | solution.py:736
  401.6 23.2 %collective-permute-start.47 = (bf16[512,2048]{1,0:T(8,128)(2,1)}, bf16[512,2048]{1,0:T(8,128)(2,1)}, u32[]{:S(2)}, u32[]{:S(2)}) collective-permute-start(bf16[512,2048]{1,0:T(8,128)(2,1)} %pad_maximum_fusion.9), channel_id=1, source_target_pairs={{0,4},{4,0},{1,5},{5,1},{2,6},{6,2},{3,7},{7,3},{8,12},{12,8},{9,1... | collective-permute-start | bytes 6291464 | tf_op jit(solution)/shard_map/ppermute | solution.py:40
  402.6 18.4 %collective-permute-start.50 = (bf16[128,2048]{1,0:T(8,128)(2,1)}, bf16[128,2048]{1,0:T(8,128)(2,1)S(1)}, u32[]{:S(2)}, u32[]{:S(2)}) collective-permute-start(bf16[128,2048]{1,0:T(8,128)(2,1)} %slice.861), channel_id=1, source_target_pairs={{0,1},{1,0},{2,3},{3,2},{4,5},{5,4},{6,7},{7,6},{8,9},{9,8},{10,11... | collective-permute-start | bytes 1572872 | tf_op jit(solution)/shard_map/ppermute | solution.py:73
  403.8 34.2 %collective-permute-start.52 = (bf16[128,2048]{1,0:T(8,128)(2,1)}, bf16[128,2048]{1,0:T(8,128)(2,1)}, u32[]{:S(2)}, u32[]{:S(2)}) collective-permute-start(bf16[128,2048]{1,0:T(8,128)(2,1)} %slice.860), channel_id=1, source_target_pairs={{0,1},{1,0},{2,3},{3,2},{4,5},{5,4},{6,7},{7,6},{8,9},{9,8},{10,11... | collective-permute-start | bytes 1572872 | tf_op jit(solution)/shard_map/ppermute | solution.py:73
  423.1 26.8 %collective-permute-start.51 = (bf16[64,2048]{1,0:T(8,128)(2,1)}, bf16[64,2048]{1,0:T(8,128)(2,1)S(1)}, u32[]{:S(2)}, u32[]{:S(2)}) collective-permute-start(bf16[64,2048]{1,0:T(8,128)(2,1)} %slice.869), channel_id=1, source_target_pairs={{0,2},{1,3},{2,0},{3,1},{4,6},{5,7},{6,4},{7,5},{8,10},{9,11},{10,... | collective-permute-start | bytes 786440 | tf_op jit(solution)/shard_map/ppermute | solution.py:73
  432.0 55.4 %collective-permute-start.49 = (bf16[256,2048]{1,0:T(8,128)(2,1)}, bf16[256,2048]{1,0:T(8,128)(2,1)}, u32[]{:S(2)}, u32[]{:S(2)}) collective-permute-start(bf16[256,2048]{1,0:T(8,128)(2,1)} %pad_maximum_fusion.16), channel_id=1, source_target_pairs={{0,1},{1,0},{2,3},{3,2},{4,5},{5,4},{6,7},{7,6},{8,9},{9,8},{10,11... | collective-permute-start | bytes 3145736 | tf_op jit(solution)/shard_map/ppermute | solution.py:73
  440.3 24.8 %collective-permute-start.59 = (bf16[64,2048]{1,0:T(8,128)(2,1)}, bf16[64,2048]{1,0:T(8,128)(2,1)}, u32[]{:S(2)}, u32[]{:S(2)}) collective-permute-start(bf16[64,2048]{1,0:T(8,128)(2,1)} %slice.868), channel_id=1, source_target_pairs={{0,2},{1,3},{2,0},{3,1},{4,6},{5,7},{6,4},{7,5},{8,10},{9,11},{10,... | collective-permute-start | bytes 786440 | tf_op jit(solution)/shard_map/ppermute | solution.py:73
  450.0 16.5 %collective-permute-start.56 = (bf16[4,512,256]{2,1,0:T(8,128)(2,1)}, bf16[4,512,256]{2,1,0:T(8,128)(2,1)S(1)}, u32[]{:S(2)}, u32[]{:S(2)}) collective-permute-start(bf16[4,512,256]{2,1,0:T(8,128)(2,1)} %get-tuple-element.190), channel_id=1, source_target_pairs={{0,4},{4,0},{1,5},{5,1},{2,6},{6,2},{3,7},{7,3},{8,12},{12,8},{9,1... | collective-permute-start | bytes 3145736 | tf_op jit(solution)/shard_map/ppermute | solution.py:40
  452.9 31.8 %collective-permute-start.55 = (bf16[64,2048]{1,0:T(8,128)(2,1)S(1)}, bf16[64,2048]{1,0:T(8,128)(2,1)S(1)}, u32[]{:S(2)}, u32[]{:S(2)}) collective-permute-start(bf16[64,2048]{1,0:T(8,128)(2,1)S(1)} %fusion.31), channel_id=1, source_target_pairs={{0,2},{1,3},{2,0},{3,1},{4,6},{5,7},{6,4},{7,5},{8,10},{9,11},{10,... | collective-permute-start | bytes 786440 | tf_op jit(solution)/shard_map/ppermute | solution.py:779
  471.1 37.9 %collective-permute-start.61 = (bf16[64,2048]{1,0:T(8,128)(2,1)S(1)}, bf16[64,2048]{1,0:T(8,128)(2,1)S(1)}, u32[]{:S(2)}, u32[]{:S(2)}) collective-permute-start(bf16[64,2048]{1,0:T(8,128)(2,1)S(1)} %fusion.24), channel_id=1, source_target_pairs={{0,2},{1,3},{2,0},{3,1},{4,6},{5,7},{6,4},{7,5},{8,10},{9,11},{10,... | collective-permute-start | bytes 786440 | tf_op jit(solution)/shard_map/ppermute | solution.py:781
  483.2 39.3 %collective-permute-start.67 = (bf16[256,640]{1,0:T(8,128)(2,1)S(1)}, bf16[256,640]{1,0:T(8,128)(2,1)S(1)}, u32[]{:S(2)}, u32[]{:S(2)}) collective-permute-start(bf16[256,640]{1,0:T(8,128)(2,1)S(1)} %fusion.51), channel_id=1, source_target_pairs={{0,8},{8,0},{16,24},{24,16},{1,9},{9,1},{17,25},{25,17},{2,10},{10... | collective-permute-start | bytes 983048 | tf_op jit(solution)/shard_map/ppermute | solution.py:164
  484.8 22.3 %collective-permute-start.62 = (bf16[128,2048]{1,0:T(8,128)(2,1)S(1)}, bf16[128,2048]{1,0:T(8,128)(2,1)S(1)}, u32[]{:S(2)}, u32[]{:S(2)}) collective-permute-start(bf16[128,2048]{1,0:T(8,128)(2,1)S(1)} %pad_maximum_fusion.29), channel_id=1, source_target_pairs={{0,1},{1,0},{2,3},{3,2},{4,5},{5,4},{6,7},{7,6},{8,9},{9,8},{10,11... | collective-permute-start | bytes 1572872 | tf_op jit(solution)/shard_map/ppermute | solution.py:796
  489.1 25.4 %collective-permute-start.60 = (bf16[128,2048]{1,0:T(8,128)(2,1)S(1)}, bf16[128,2048]{1,0:T(8,128)(2,1)S(1)}, u32[]{:S(2)}, u32[]{:S(2)}) collective-permute-start(bf16[128,2048]{1,0:T(8,128)(2,1)S(1)} %pad_maximum_fusion.30), channel_id=1, source_target_pairs={{0,2},{1,3},{2,0},{3,1},{4,6},{5,7},{6,4},{7,5},{8,10},{9,11},{10,... | collective-permute-start | bytes 1572872 | tf_op jit(solution)/shard_map/ppermute | solution.py:73
  490.5 26.3 %collective-permute-start.70 = (f32[2,2048]{1,0:T(2,128)S(1)}, f32[2,2048]{1,0:T(2,128)S(1)}, u32[]{:S(2)}, u32[]{:S(2)}) collective-permute-start(f32[2,2048]{1,0:T(2,128)S(1)} %fusion.69), channel_id=1, source_target_pairs={{0,8},{8,0},{16,24},{24,16},{1,9},{9,1},{17,25},{25,17},{2,10},{10... | collective-permute-start | bytes 49160 | tf_op jit(solution)/shard_map/ppermute | solution.py:220
  516.8 25.4 %collective-permute-start.64 = (bf16[128,2048]{1,0:T(8,128)(2,1)}, bf16[128,2048]{1,0:T(8,128)(2,1)}, u32[]{:S(2)}, u32[]{:S(2)}) collective-permute-start(bf16[128,2048]{1,0:T(8,128)(2,1)} %pad_maximum_fusion.31), channel_id=1, source_target_pairs={{0,1},{1,0},{2,3},{3,2},{4,5},{5,4},{6,7},{7,6},{8,9},{9,8},{10,11... | collective-permute-start | bytes 1572872 | tf_op jit(solution)/shard_map/ppermute | solution.py:801
  516.8 25.4 %collective-permute-start.63 = (bf16[128,2048]{1,0:T(8,128)(2,1)}, bf16[128,2048]{1,0:T(8,128)(2,1)}, u32[]{:S(2)}, u32[]{:S(2)}) collective-permute-start(bf16[128,2048]{1,0:T(8,128)(2,1)} %pad_maximum_fusion.32), channel_id=1, source_target_pairs={{0,2},{1,3},{2,0},{3,1},{4,6},{5,7},{6,4},{7,5},{8,10},{9,11},{10,... | collective-permute-start | bytes 1572872 | tf_op jit(solution)/shard_map/ppermute | solution.py:804
  519.1 31.7 %collective-permute-start.74 = (f32[2,2048]{1,0:T(2,128)S(1)}, f32[2,2048]{1,0:T(2,128)}, u32[]{:S(2)}, u32[]{:S(2)}) collective-permute-start(f32[2,2048]{1,0:T(2,128)S(1)} %add_add_fusion.1), channel_id=1, source_target_pairs={{0,1},{1,0},{2,3},{3,2},{4,5},{5,4},{6,7},{7,6},{8,9},{9,8},{10,11... | collective-permute-start | bytes 49160 | tf_op jit(solution)/shard_map/ppermute | solution.py:220
  522.5 28.3 %collective-permute-start.75 = (f32[2,2048]{1,0:T(2,128)S(1)}, f32[2,2048]{1,0:T(2,128)}, u32[]{:S(2)}, u32[]{:S(2)}) collective-permute-start(f32[2,2048]{1,0:T(2,128)S(1)} %add_add_fusion.1), channel_id=1, source_target_pairs={{0,2},{1,3},{2,0},{3,1},{4,6},{5,7},{6,4},{7,5},{8,10},{9,11},{10,... | collective-permute-start | bytes 49160 | tf_op jit(solution)/shard_map/ppermute | solution.py:220
  530.0 20.8 %collective-permute-start.76 = (f32[2,2048]{1,0:T(2,128)S(1)}, f32[2,2048]{1,0:T(2,128)S(1)}, u32[]{:S(2)}, u32[]{:S(2)}) collective-permute-start(f32[2,2048]{1,0:T(2,128)S(1)} %add_add_fusion.1), channel_id=1, source_target_pairs={{0,3},{1,2},{2,1},{3,0},{4,7},{5,6},{6,5},{7,4},{8,11},{9,10},{10,... | collective-permute-start | bytes 49160 | tf_op jit(solution)/shard_map/ppermute | solution.py:220
  543.4 21.3 %collective-permute-start.73 = (bf16[256,2048]{1,0:T(8,128)(2,1)S(1)}, bf16[256,2048]{1,0:T(8,128)(2,1)}, u32[]{:S(2)}, u32[]{:S(2)}) collective-permute-start(bf16[256,2048]{1,0:T(8,128)(2,1)S(1)} %pad_maximum_fusion.17), channel_id=1, source_target_pairs={{0,1},{1,0},{2,3},{3,2},{4,5},{5,4},{6,7},{7,6},{8,9},{9,8},{10,11... | collective-permute-start | bytes 3145736 | tf_op jit(solution)/shard_map/ppermute | solution.py:824
  (103 other events, 659.9 us)
Sparse Core Ops, SparseCore 0:
  29.7 70.9 all-gather.5
  103.1 89.2 all-gather.3
  194.3 55.8 all-gather.7
  296.3 51.3 reduce-scatter.3
  350.5 52.5 reduce-scatter.5
  418.7 52.4 reduce-scatter.7

commit v5 on v4

--- a/solution.py
+++ b/solution.py
@@ -749,22 +749,22 @@
     d1 = parts[1][:span] + sent[1].astype(F32)
     k0, g0, t0 = halved([d0], near)
     k1, g1, t1 = halved([d1], near)
-    down = [dotf(i, wd) for i in lax.optimization_barrier(tuple(inner) + (t0, t1))[:2]]
+    d_qkv = stack(*[joined(q, d_kv, h, s) for s in range(2) for h, q in enumerate((dq_0, dq_1))])
+    down = [dotf(i, wd) for i in lax.optimization_barrier(tuple(inner) + (t0, t1, d_qkv))[:2]]
     s_down = swap(stack(*[d[span:].astype(BF) for d in down]))
     g_down = grad_kernel(inner, lax.optimization_barrier(tuple(cots) + (*down, b_dh))[:2], 0, width, 512)
-    r_gate, r_up, r_down = reduced(g_gate, 0), reduced(g_up, 0), reduced(g_down, 1)
     down = [
         d[:span] + after(s_down, g_down)[n * span : (n + 1) * span].astype(F32) for n, d in enumerate(down)
     ]
     v0 = summed(k0, after(g0, g_down))
     k0, g0, t0 = halved(v0, far)
+    r_gate, r_up, r_down = reduced(g_gate, 0), reduced(g_up, 0), reduced(after(g_down, t0), 1)
     r_gate, r_up = lax.optimization_barrier((r_gate, r_up, t0))[:2]
     s_gate = pair(half_of(r_gate, core, 0), swap(half_of(r_gate, other, 0)), core, 1).astype(F32)
     s_up = pair(half_of(r_up, core, 0), swap(half_of(r_up, other, 0)), core, 1).astype(F32)
     v1 = summed(k1, after(g1, t0, s_gate, s_up))
     k1, g1, t1 = halved(v1, far)
     k_out, g_out, t_out = halved(down, near)
-    d_qkv = stack(*[joined(q, d_kv, h, s) for s in range(2) for h, q in enumerate((dq_0, dq_1))])
 
     def input_of(h, d_hidden, total):
         d_rows, gain = norm_backward(slice_of(rows, h), slice_of(scale_own, h), gain_a, total)

time: 585 us -> 595 us (1.017)
  waiting for transfers between devices: 190 us -> 209 us
    ppermute x14, waiting for transfers between devices: 82.4 us -> 93.9 us  [halved(): return ([v[:half] for v in values], lax.ppermute(sent, 'tp', pairs), sent)]
    unnamed x154 -> x148, local copies, waits for them, and re-layouts: 27.2 us -> 24.8 us
  transfers between devices with their start and end apart: 83 -> 83, of which waited for: 30 -> 32; matrix products, arithmetic and copies ran while one was open for 33% -> 31% of each run, Pallas kernels for 11% -> 11%
where the time goes in v5:
time: 595 us; the launch traced here: 589 us
  waiting for transfers between devices  209 us (35%)
  other arithmetic  88.6 us (15%)
  Pallas kernels  75.1 us (13%)
  starting transfers between devices  68.1 us (11%)
  matrix products  66.4 us (11%)
  local copies, waits for them, and re-layouts  65.8 us (11%)
  between operations  16 us (3%)
    ppermute x14, waiting for transfers between devices, halved(): return ([v[:half] for v in values], lax.ppermute(sent, 'tp', pairs), sent)  93.9 us
    dot_general x8, matrix products, dot_t(): lax.dot_general(left, right, (((1,), (1,)), ((), ())), preferred_element_...  36.5 us
    dot_general x9, matrix products, dotf(): return jnp.dot(left, right, preferred_element_type=F32)  25.9 us
    pallas_call x3, Pallas kernels, grad_kernel(): pl.pallas_call(kernel, grid=(wide // block,), in_specs=[pl.BlockSpec((row...  25.4 us
    unnamed x148, local copies, waits for them, and re-layouts  24.8 us
    pallas_call x2, Pallas kernels, attend_back(): pl.pallas_call(kernel, in_specs=[SCALARS] + [pl.BlockSpec()] * (10 + 2 *...  19.1 us
    ppermute x1, waiting for transfers between devices, body(): b0 = lax.ppermute(cur0, 'tp', near)  16.6 us
    concatenate x18, other arithmetic, stack(): return jnp.concatenate(parts, axis=0)  15.8 us
  transfers between devices with their start and end apart: 83, of which 32 were waited for; matrix products, arithmetic and copies ran while one was open for 31% of the time, Pallas kernels for 11%

profile of v5, /device:TPU:0, one launch (start us, length us, event | category | flops | bytes accessed | tf_op | source)
XLA Modules:
  0.0 588.7 jit_solution(10690492263214853950)
XLA Ops:
  19.1 6.3 %collective-permute-done.4 = f32[512,2048]{1,0:T(8,128)} collective-permute-done((f32[512,2048]{1,0:T(8,128)}, f32[512,2048]{1,0:T(8,128)}, u32[]{:S(2)}, u32[]{:S(2)}) %collective-permute-start.4) | collective-permute-done | bytes 4194336 | tf_op jit(solution)/shard_map/ppermute | solution.py:40
  33.5 3.2 broadcast_select_fusion.20
  39.4 3.0 collective-permute-start.1
  45.5 3.9 arrange.3
  49.5 12.4 %collective-permute-done.1 = bf16[544,384]{1,0:T(8,128)(2,1)S(1)} collective-permute-done((bf16[544,384]{1,0:T(8,128)(2,1)}, bf16[544,384]{1,0:T(8,128)(2,1)S(1)}, u32[]{:S(2)}, u32[]{:S(2)}) %collective-permute-start.1) | collective-permute-done | bytes 417824 | tf_op jit(solution)/shard_map/ppermute | solution.py:184
  82.3 2.9 multiply_convert_fusion.1
  87.2 3.5 fusion.qkv_ref
  90.7 7.6 %attend_first.1 = (bf16[1024,256]{1,0:T(8,128)(2,1)}, bf16[1024,128]{1,0:T(8,128)(2,1)}, bf16[512,256]{1,0:T(8,128)(2,1)}, f32[512,4]{1,0:T(8,128)}) custom-call(s32[2]{0:T(128)} %pad_add_fusion.at_ref, f32[1024,384]{1,0:T(8,128)} %fusion.qkv_ref, f32[1024,128]{1,0:T(8,128)} %get-tuple-element.357.cos_ref, f32[1024,128]{1,0:T(8,128)} %get-tuple-element.355.sin_ref, ...), custom_call_target="tpu_custom_call" | custom-call | flops 8000000000 | bytes 1572864 | tf_op jit(solution)/shard_map/attend_first/pallas_call | solution.py:396
  110.2 6.2 %collective-permute-done.16 = bf16[1024,256]{1,0:T(8,128)(2,1)S(1)} collective-permute-done((bf16[1024,256]{1,0:T(8,128)(2,1)S(1)}, bf16[1024,256]{1,0:T(8,128)(2,1)S(1)}, u32[]{:S(2)}, u32[]{:S(2)}) %collective-permute-start.16) | collective-permute-done | bytes 524320 | tf_op jit(solution)/shard_map/ppermute | solution.py:87
  117.2 5.8 attend_next.1
  124.7 2.8 broadcast_select_fusion.1
  139.8 3.1 fusion.79
  142.9 7.6 %collective-permute-done.14 = bf16[128,2048]{1,0:T(8,128)(2,1)S(1)} collective-permute-done((bf16[128,2048]{1,0:T(8,128)(2,1)S(1)}, bf16[128,2048]{1,0:T(8,128)(2,1)S(1)}, u32[]{:S(2)}, u32[]{:S(2)}) %collective-permute-start.14) | collective-permute-done | bytes 524320 | tf_op jit(solution)/shard_map/ppermute | solution.py:73
  151.7 15.2 %collective-permute-done.19 = bf16[128,2048]{1,0:T(8,128)(2,1)S(1)} collective-permute-done((bf16[128,2048]{1,0:T(8,128)(2,1)S(1)}, bf16[128,2048]{1,0:T(8,128)(2,1)S(1)}, u32[]{:S(2)}, u32[]{:S(2)}) %collective-permute-start.19) | collective-permute-done | bytes 524320 | tf_op jit(solution)/shard_map/ppermute | solution.py:73
  172.2 13.9 %collective-permute-done.21 = bf16[64,2048]{1,0:T(8,128)(2,1)S(1)} collective-permute-done((bf16[64,2048]{1,0:T(8,128)(2,1)S(1)}, bf16[64,2048]{1,0:T(8,128)(2,1)S(1)}, u32[]{:S(2)}, u32[]{:S(2)}) %collective-permute-start.21) | collective-permute-done | bytes 262176 | tf_op jit(solution)/shard_map/ppermute | solution.py:73
  188.2 3.5 collective-permute-done.20
  193.5 2.8 collective-permute-start.23
  197.9 11.1 %collective-permute-done.23 = bf16[64,2048]{1,0:T(8,128)(2,1)S(1)} collective-permute-done((bf16[64,2048]{1,0:T(8,128)(2,1)S(1)}, bf16[64,2048]{1,0:T(8,128)(2,1)S(1)}, u32[]{:S(2)}, u32[]{:S(2)}) %collective-permute-start.23) | collective-permute-done | bytes 262176 | tf_op jit(solution)/shard_map/ppermute | solution.py:646
  209.1 3.4 collective-permute-start.27
  216.3 7.7 %fusion.96 = f32[512,2048]{1,0:T(8,128)S(1)} fusion(bf16[512,2048]{1,0:T(8,128)(2,1)} %constant_dynamic-update-slice_fusion.5.refs_0_, bf16[2048,2048]{1,0:T(8,128)(2,1)} %all-gather.4.cloned.1.call-done), kind=kOutput, calls=%fused_computation.357 | convolution fusion | flops 4294967296 | bytes 14680064 | tf_op jit(solution)/shard_map/dot_general | solution.py:19
  224.2 4.7 multiply_convert_fusion.6
  228.9 4.5 fusion.72
  236.4 6.3 %fusion.97 = f32[512,2048]{1,0:T(8,128)} fusion(bf16[512,2048]{1,0:T(8,128)(2,1)S(1)} %constant_dynamic-update-slice_fusion.10.refs_1_, bf16[2048,2048]{1,0:T(8,128)(2,1)S(1)} %copy-done.58), kind=kOutput, calls=%fused_computation.358 | convolution fusion | flops 4294967296 | bytes 14680064 | tf_op jit(solution)/shard_map/dot_general | solution.py:19
  244.9 7.9 %multiply_convert_fusion.3 = (bf16[512,1024]{1,0:T(8,128)(2,1)S(1)}, bf16[512,1024]{1,0:T(8,128)(2,1)S(1)}, bf16[512,1024]{1,0:T(8,128)(2,1)}) fusion(f32[512,2048]{1,0:T(8,128)} %fusion.97, bf16[512,2048]{1,0:T(8,128)(2,1)S(1)} %copy-done.27, bf16[1024,2048]{1,0:T(8,128)(2,1)} %all-gather.6.cloned.1.call-done), kind=kOutput, calls=%fused_computation.41 | convolution fusion | flops 2155347968 | bytes 13631488 | tf_op jit(solution)/shard_map/dot_general | solution.py:23
  253.0 4.1 collective-permute-done.31
  257.2 4.5 fusion.98
  267.0 11.8 %collective-permute-done.32 = bf16[64,2048]{1,0:T(8,128)(2,1)S(1)} collective-permute-done((bf16[64,2048]{1,0:T(8,128)(2,1)S(1)}, bf16[64,2048]{1,0:T(8,128)(2,1)S(1)}, u32[]{:S(2)}, u32[]{:S(2)}) %collective-permute-start.32) | collective-permute-done | bytes 262176 | tf_op jit(solution)/shard_map/ppermute | solution.py:73
  281.0 6.0 %convolution_convert_fusion.2 = bf16[64,2048]{1,0:T(8,128)(2,1)S(1)} fusion(bf16[64,2048]{1,0:T(8,128)(2,1)S(1)} %get-tuple-element.229, bf16[2048,2048]{1,0:T(8,128)(2,1)} %all-gather.8.cloned.1.call-done), kind=kOutput, calls=%fused_computation.18 | convolution fusion | flops 537001984 | bytes 8912896 | tf_op jit(solution)/shard_map/dot_general | solution.py:23
  287.8 8.4 %grad.3 = bf16[2048,1024]{1,0:T(8,128)(2,1)} custom-call(bf16[512,2048]{1,0:T(8,128)(2,1)} %constant_dynamic-update-slice_fusion.5.refs_0_, bf16[512,2048]{1,0:T(8,128)(2,1)} %copy-done.52, bf16[512,2048]{1,0:T(8,128)(2,1)} %pad_maximum_fusion.7.refs_2_, bf16[512,2048]{1,0:T(8,128)(2,1)} %copy-done.28), custom_call_target="tpu_custom_call" | custom-call | flops 8589934592 | bytes 8388608 | tf_op jit(solution)/shard_map/grad/pallas_call | solution.py:236
  296.3 13.5 %collective-permute-done.37 = bf16[128,2048]{1,0:T(8,128)(2,1)S(1)} collective-permute-done((bf16[128,2048]{1,0:T(8,128)(2,1)S(1)}, bf16[128,2048]{1,0:T(8,128)(2,1)S(1)}, u32[]{:S(2)}, u32[]{:S(2)}) %collective-permute-start.37) | collective-permute-done | bytes 524320 | tf_op jit(solution)/shard_map/ppermute | solution.py:73
  317.0 8.4 %grad.4 = bf16[2048,1024]{1,0:T(8,128)(2,1)} custom-call(bf16[512,2048]{1,0:T(8,128)(2,1)} %constant_dynamic-update-slice_fusion.5.refs_0_, bf16[512,2048]{1,0:T(8,128)(2,1)} %copy-done.52, bf16[512,2048]{1,0:T(8,128)(2,1)} %pad_maximum_fusion.7.refs_2_, bf16[512,2048]{1,0:T(8,128)(2,1)} %copy-done.28), custom_call_target="tpu_custom_call" | custom-call | flops 8589934592 | bytes 8388608 | tf_op jit(solution)/shard_map/grad/pallas_call | solution.py:236
  325.9 2.8 collective-permute-done.38
  332.7 6.2 %convolution_convert_fusion.1 = bf16[64,2048]{1,0:T(8,128)(2,1)S(1)} fusion(bf16[64,2048]{1,0:T(8,128)(2,1)S(1)} %get-tuple-element.227, bf16[2048,2048]{1,0:T(8,128)(2,1)} %all-gather.8.cloned.1.call-done), kind=kOutput, calls=%fused_computation.17 | convolution fusion | flops 537001984 | bytes 8912896 | tf_op jit(solution)/shard_map/dot_general | solution.py:23
  339.6 2.7 collective-permute-start.41
  348.4 8.2 %attend_back.2 = (bf16[512,256]{1,0:T(8,128)(2,1)}, bf16[512,256]{1,0:T(8,128)(2,1)}, f32[2,1024,128]{2,1,0:T(8,128)}, f32[2,1024,128]{2,1,0:T(8,128)}) custom-call(s32[2]{0:T(128)} %pad_add_fusion.at_ref, bf16[1024,256]{1,0:T(8,128)(2,1)} %get-tuple-element.127.q_ref, bf16[1024,128]{1,0:T(8,128)(2,1)} %get-tuple-element.129.kv_ref, ...), custom_call_target="tpu_custom_call" | custom-call | flops 8000000000 | bytes 1048576 | tf_op jit(solution)/shard_map/attend_back/pallas_call | solution.py:510
  359.4 11.0 %attend_back.3 = (bf16[512,256]{1,0:T(8,128)(2,1)}, bf16[512,256]{1,0:T(8,128)(2,1)}, bf16[1024,128]{1,0:T(8,128)(2,1)}, bf16[1024,128]{1,0:T(8,128)(2,1)}) custom-call(s32[2]{0:T(128)} %pad_add_fusion.at_ref, bf16[1024,256]{1,0:T(8,128)(2,1)} %get-tuple-element.127.q_ref, bf16[1024,128]{1,0:T(8,128)(2,1)} %get-tuple-element.129.kv_ref, ...), custom_call_target="tpu_custom_call" | custom-call | flops 8000000000 | bytes 1048576 | tf_op jit(solution)/shard_map/attend_back/pallas_call | solution.py:510
  398.3 9.0 %collective-permute-done.48 = bf16[256,2048]{1,0:T(8,128)(2,1)} collective-permute-done((bf16[256,2048]{1,0:T(8,128)(2,1)}, bf16[256,2048]{1,0:T(8,128)(2,1)}, u32[]{:S(2)}, u32[]{:S(2)}) %collective-permute-start.48) | collective-permute-done | bytes 1048608 | tf_op jit(solution)/shard_map/ppermute | solution.py:736
  407.4 8.6 %grad.5 = bf16[1024,2048]{1,0:T(8,128)(2,1)} custom-call(bf16[512,1024]{1,0:T(8,128)(2,1)} %get-tuple-element.178.refs_0_, bf16[512,1024]{1,0:T(8,128)(2,1)} %get-tuple-element.179.refs_1_, bf16[512,2048]{1,0:T(8,128)(2,1)} %pad_maximum_fusion.5.refs_2_, bf16[512,2048]{1,0:T(8,128)(2,1)} %pad_maximum_fusion.6.refs_3_), custom_call_target="tpu_custom_call" | custom-call | flops 8589934592 | bytes 6291456 | tf_op jit(solution)/shard_map/grad/pallas_call | solution.py:236
  423.0 3.5 slice_add_fusion.1
  441.5 4.9 output_grad.1
  452.4 4.0 convolution_convert_fusion
  456.4 19.6 %collective-permute-done.59 = bf16[64,2048]{1,0:T(8,128)(2,1)S(1)} collective-permute-done((bf16[64,2048]{1,0:T(8,128)(2,1)S(1)}, bf16[64,2048]{1,0:T(8,128)(2,1)S(1)}, u32[]{:S(2)}, u32[]{:S(2)}) %collective-permute-start.59) | collective-permute-done | bytes 262176 | tf_op jit(solution)/shard_map/ppermute | solution.py:73
  482.3 12.2 %collective-permute-done.57 = bf16[2,256,640]{2,1,0:T(8,128)(2,1)S(1)} collective-permute-done((bf16[2,256,640]{2,1,0:T(8,128)(2,1)S(1)}, bf16[2,256,640]{2,1,0:T(8,128)(2,1)S(1)}, u32[]{:S(2)}, u32[]{:S(2)}) %collective-permute-start.57) | collective-permute-done | bytes 655392 | tf_op jit(solution)/shard_map/ppermute | solution.py:149
  501.5 16.6 %collective-permute-done.62 = bf16[128,2048]{1,0:T(8,128)(2,1)S(1)} collective-permute-done((bf16[128,2048]{1,0:T(8,128)(2,1)S(1)}, bf16[128,2048]{1,0:T(8,128)(2,1)S(1)}, u32[]{:S(2)}, u32[]{:S(2)}) %collective-permute-start.62) | collective-permute-done | bytes 524320 | tf_op jit(solution)/shard_map/ppermute | solution.py:796
  542.3 9.1 %collective-permute-done.63 = bf16[128,2048]{1,0:T(8,128)(2,1)} collective-permute-done((bf16[128,2048]{1,0:T(8,128)(2,1)}, bf16[128,2048]{1,0:T(8,128)(2,1)}, u32[]{:S(2)}, u32[]{:S(2)}) %collective-permute-start.63) | collective-permute-done | bytes 524320 | tf_op jit(solution)/shard_map/ppermute | solution.py:804
  555.8 4.2 arrange.4
  561.9 12.1 %collective-permute-done.73 = bf16[256,2048]{1,0:T(8,128)(2,1)} collective-permute-done((bf16[256,2048]{1,0:T(8,128)(2,1)S(1)}, bf16[256,2048]{1,0:T(8,128)(2,1)}, u32[]{:S(2)}, u32[]{:S(2)}) %collective-permute-start.73) | collective-permute-done | bytes 1048608 | tf_op jit(solution)/shard_map/ppermute | solution.py:824
  577.4 4.2 arrange.5
  (482 shorter events, 227.7 us)
Async XLA Ops:
  7.2 162.1 %all-gather.6.cloned.1.call-start = ((), (), s32[]{:S(2)}) async-start(), calls=%async_computation.4 | async-start | bytes 5242880 | tf_op jit(solution)/shard_map/all_gather | solution.py:591
  29.6 186.6 %all-gather.4.cloned.1.call-start = ((), (), s32[]{:S(2)}) async-start(), calls=%async_computation.3 | async-start | bytes 10485760 | tf_op jit(solution)/shard_map/all_gather | solution.py:590
  32.3 248.8 %all-gather.8.cloned.1.call-start = ((), (), s32[]{:S(2)}) async-start(), calls=%async_computation.5 | async-start | bytes 9437184 | tf_op jit(solution)/shard_map/all_gather | solution.py:613
  39.4 22.5 %collective-permute-start.1 = (bf16[544,384]{1,0:T(8,128)(2,1)}, bf16[544,384]{1,0:T(8,128)(2,1)S(1)}, u32[]{:S(2)}, u32[]{:S(2)}) collective-permute-start(bf16[544,384]{1,0:T(8,128)(2,1)} %pad_maximum_fusion.33), channel_id=1, source_target_pairs={{0,8},{8,0},{16,24},{24,16},{1,9},{9,1},{17,25},{25,17},{2,10},{10... | collective-permute-start | bytes 1253384 | tf_op jit(solution)/shard_map/ppermute | solution.py:184
  42.4 21.0 %collective-permute-start.2 = (bf16[544,384]{1,0:T(8,128)(2,1)}, bf16[544,384]{1,0:T(8,128)(2,1)S(1)}, u32[]{:S(2)}, u32[]{:S(2)}) collective-permute-start(bf16[544,384]{1,0:T(8,128)(2,1)} %pad_maximum_fusion.33), channel_id=1, source_target_pairs={{0,16},{8,24},{16,0},{24,8},{1,17},{9,25},{17,1},{25,9},{2,18},{10... | collective-permute-start | bytes 1253384 | tf_op jit(solution)/shard_map/ppermute | solution.py:185
  49.4 90.4 %collective-permute-start.24 = (bf16[512,2048]{1,0:T(8,128)(2,1)}, bf16[512,2048]{1,0:T(8,128)(2,1)}, u32[]{:S(2)}, u32[]{:S(2)}) collective-permute-start(bf16[512,2048]{1,0:T(8,128)(2,1)} %arrange.3), channel_id=1, source_target_pairs={{0,4},{4,0},{1,5},{5,1},{2,6},{6,2},{3,7},{7,3},{8,12},{12,8},{9,1... | collective-permute-start | bytes 6291464 | tf_op jit(solution)/shard_map/ppermute | solution.py:40
  77.5 20.8 %collective-permute-start.8 = (bf16[512,256]{1,0:T(8,128)(2,1)S(1)}, bf16[512,256]{1,0:T(8,128)(2,1)S(1)}, u32[]{:S(2)}, u32[]{:S(2)}) collective-permute-start(bf16[512,256]{1,0:T(8,128)(2,1)S(1)} %copy-done.22), channel_id=1, source_target_pairs={{0,8},{8,0},{16,24},{24,16},{1,9},{9,1},{17,25},{25,17},{2,10},{10... | collective-permute-start | bytes 786440 | tf_op jit(solution)/shard_map/ppermute | solution.py:184
  78.0 20.3 %collective-permute-start.9 = (bf16[512,256]{1,0:T(8,128)(2,1)S(1)}, bf16[512,256]{1,0:T(8,128)(2,1)S(1)}, u32[]{:S(2)}, u32[]{:S(2)}) collective-permute-start(bf16[512,256]{1,0:T(8,128)(2,1)S(1)} %copy-done.22), channel_id=1, source_target_pairs={{0,16},{8,24},{16,0},{24,8},{1,17},{9,25},{17,1},{25,9},{2,18},{10... | collective-permute-start | bytes 786440 | tf_op jit(solution)/shard_map/ppermute | solution.py:185
  80.0 22.2 %collective-permute-start.15 = (bf16[512,256]{1,0:T(8,128)(2,1)S(1)}, bf16[512,256]{1,0:T(8,128)(2,1)S(1)}, u32[]{:S(2)}, u32[]{:S(2)}) collective-permute-start(bf16[512,256]{1,0:T(8,128)(2,1)S(1)} %copy-done.22), channel_id=1, source_target_pairs={{0,2},{1,3},{2,0},{3,1},{4,6},{5,7},{6,4},{7,5},{8,10},{9,11},{10,... | collective-permute-start | bytes 786440 | tf_op jit(solution)/shard_map/ppermute | solution.py:86
  100.5 33.7 %collective-permute-start.13 = (bf16[256,256]{1,0:T(8,128)(2,1)}, bf16[256,256]{1,0:T(8,128)(2,1)}, u32[]{:S(2)}, u32[]{:S(2)}) collective-permute-start(bf16[256,256]{1,0:T(8,128)(2,1)} %get-tuple-element.309), channel_id=1, source_target_pairs={{0,4},{4,0},{1,5},{5,1},{2,6},{6,2},{3,7},{7,3},{8,12},{12,8},{9,1... | collective-permute-start | bytes 393224 | tf_op jit(solution)/shard_map/ppermute | solution.py:40
  139.3 27.7 %collective-permute-start.19 = (bf16[128,2048]{1,0:T(8,128)(2,1)S(1)}, bf16[128,2048]{1,0:T(8,128)(2,1)S(1)}, u32[]{:S(2)}, u32[]{:S(2)}) collective-permute-start(bf16[128,2048]{1,0:T(8,128)(2,1)S(1)} %slice.864), channel_id=1, source_target_pairs={{0,1},{1,0},{2,3},{3,2},{4,5},{5,4},{6,7},{7,6},{8,9},{9,8},{10,11... | collective-permute-start | bytes 1572872 | tf_op jit(solution)/shard_map/ppermute | solution.py:73
  150.7 17.3 %collective-permute-start.18 = (bf16[64,2048]{1,0:T(8,128)(2,1)S(1)}, bf16[64,2048]{1,0:T(8,128)(2,1)S(1)}, u32[]{:S(2)}, u32[]{:S(2)}) collective-permute-start(bf16[64,2048]{1,0:T(8,128)(2,1)S(1)} %slice.873), channel_id=1, source_target_pairs={{0,2},{1,3},{2,0},{3,1},{4,6},{5,7},{6,4},{7,5},{8,10},{9,11},{10,... | collective-permute-start | bytes 786440 | tf_op jit(solution)/shard_map/ppermute | solution.py:73
  167.1 19.1 %collective-permute-start.21 = (bf16[64,2048]{1,0:T(8,128)(2,1)S(1)}, bf16[64,2048]{1,0:T(8,128)(2,1)S(1)}, u32[]{:S(2)}, u32[]{:S(2)}) collective-permute-start(bf16[64,2048]{1,0:T(8,128)(2,1)S(1)} %slice.872), channel_id=1, source_target_pairs={{0,2},{1,3},{2,0},{3,1},{4,6},{5,7},{6,4},{7,5},{8,10},{9,11},{10,... | collective-permute-start | bytes 786440 | tf_op jit(solution)/shard_map/ppermute | solution.py:73
  169.3 252.5 %reduce-scatter.4.cloned.1.call-start = ((), (), s32[]{:S(2)}) async-start(), calls=%async_computation.6 | async-start | bytes 5242880 | tf_op jit(solution)/shard_map/reduce_scatter | solution.py:687
  170.2 21.5 %collective-permute-start.20 = (bf16[64,2048]{1,0:T(8,128)(2,1)S(1)}, bf16[64,2048]{1,0:T(8,128)(2,1)S(1)}, u32[]{:S(2)}, u32[]{:S(2)}) collective-permute-start(bf16[64,2048]{1,0:T(8,128)(2,1)S(1)} %get-tuple-element.234), channel_id=1, source_target_pairs={{0,2},{1,3},{2,0},{3,1},{4,6},{5,7},{6,4},{7,5},{8,10},{9,11},{10,... | collective-permute-start | bytes 786440 | tf_op jit(solution)/shard_map/ppermute | solution.py:644
  191.7 20.8 %collective-permute-start.22 = (bf16[128,2048]{1,0:T(8,128)(2,1)S(1)}, bf16[128,2048]{1,0:T(8,128)(2,1)S(1)}, u32[]{:S(2)}, u32[]{:S(2)}) collective-permute-start(bf16[128,2048]{1,0:T(8,128)(2,1)S(1)} %pad_maximum_fusion.26), channel_id=1, source_target_pairs={{0,1},{1,0},{2,3},{3,2},{4,5},{5,4},{6,7},{7,6},{8,9},{9,8},{10,11... | collective-permute-start | bytes 1572872 | tf_op jit(solution)/shard_map/ppermute | solution.py:648
  197.9 16.6 %collective-permute-start.25 = (bf16[128,2048]{1,0:T(8,128)(2,1)S(1)}, bf16[128,2048]{1,0:T(8,128)(2,1)S(1)}, u32[]{:S(2)}, u32[]{:S(2)}) collective-permute-start(bf16[128,2048]{1,0:T(8,128)(2,1)S(1)} %pad_maximum_fusion.26), channel_id=1, source_target_pairs={{0,4},{4,0},{1,5},{5,1},{2,6},{6,2},{3,7},{7,3},{8,12},{12,8},{9,1... | collective-permute-start | bytes 1572872 | tf_op jit(solution)/shard_map/ppermute | solution.py:40
  212.5 21.6 %collective-permute-start.28 = (bf16[128,2048]{1,0:T(8,128)(2,1)S(1)}, bf16[128,2048]{1,0:T(8,128)(2,1)}, u32[]{:S(2)}, u32[]{:S(2)}) collective-permute-start(bf16[128,2048]{1,0:T(8,128)(2,1)S(1)} %pad_maximum_fusion.27), channel_id=1, source_target_pairs={{0,4},{4,0},{1,5},{5,1},{2,6},{6,2},{3,7},{7,3},{8,12},{12,8},{9,1... | collective-permute-start | bytes 1572872 | tf_op jit(solution)/shard_map/ppermute | solution.py:40
  296.2 125.7 %reduce-scatter.6.cloned.1.call-start = ((), (), s32[]{:S(2)}) async-start(), calls=%async_computation.7 | async-start | bytes 5242880 | tf_op jit(solution)/shard_map/reduce_scatter | solution.py:687
  312.1 16.6 %collective-permute-start.38 = (bf16[64,2048]{1,0:T(8,128)(2,1)S(1)}, bf16[64,2048]{1,0:T(8,128)(2,1)S(1)}, u32[]{:S(2)}, u32[]{:S(2)}) collective-permute-start(bf16[64,2048]{1,0:T(8,128)(2,1)S(1)} %slice.870), channel_id=1, source_target_pairs={{0,2},{1,3},{2,0},{3,1},{4,6},{5,7},{6,4},{7,5},{8,10},{9,11},{10,... | collective-permute-start | bytes 786440 | tf_op jit(solution)/shard_map/ppermute | solution.py:73
  312.6 29.8 %collective-permute-start.34 = (bf16[64,512]{1,0:T(8,128)(2,1)}, bf16[64,512]{1,0:T(8,128)(2,1)S(1)}, u32[]{:S(2)}, u32[]{:S(2)}) collective-permute-start(bf16[64,512]{1,0:T(8,128)(2,1)} %get-tuple-element.332), channel_id=1, source_target_pairs={{0,2},{1,3},{2,0},{3,1},{4,6},{5,7},{6,4},{7,5},{8,10},{9,11},{10,... | collective-permute-start | bytes 196616 | tf_op jit(solution)/shard_map/ppermute | solution.py:706
  315.1 28.9 %collective-permute-start.35 = (bf16[64,512]{1,0:T(8,128)(2,1)}, bf16[64,512]{1,0:T(8,128)(2,1)}, u32[]{:S(2)}, u32[]{:S(2)}) collective-permute-start(bf16[64,512]{1,0:T(8,128)(2,1)} %get-tuple-element.331), channel_id=1, source_target_pairs={{0,1},{1,0},{2,3},{3,2},{4,5},{5,4},{6,7},{7,6},{8,9},{9,8},{10,11... | collective-permute-start | bytes 196616 | tf_op jit(solution)/shard_map/ppermute | solution.py:706
  315.4 28.6 %collective-permute-start.36 = (bf16[64,512]{1,0:T(8,128)(2,1)}, bf16[64,512]{1,0:T(8,128)(2,1)}, u32[]{:S(2)}, u32[]{:S(2)}) collective-permute-start(bf16[64,512]{1,0:T(8,128)(2,1)} %get-tuple-element.330), channel_id=1, source_target_pairs={{0,3},{1,2},{2,1},{3,0},{4,7},{5,6},{6,5},{7,4},{8,11},{9,10},{10,... | collective-permute-start | bytes 196616 | tf_op jit(solution)/shard_map/ppermute | solution.py:706
  325.4 208.5 %reduce-scatter.8.cloned.1.call-start = ((), (), s32[]{:S(2)}) async-start(), calls=%async_computation.8 | async-start | bytes 5242880 | tf_op jit(solution)/shard_map/reduce_scatter | solution.py:687
  339.6 17.0 %collective-permute-start.40 = (bf16[64,512]{1,0:T(8,128)(2,1)}, bf16[64,512]{1,0:T(8,128)(2,1)S(1)}, u32[]{:S(2)}, u32[]{:S(2)}) collective-permute-start(bf16[64,512]{1,0:T(8,128)(2,1)} %get-tuple-element.336), channel_id=1, source_target_pairs={{0,2},{1,3},{2,0},{3,1},{4,6},{5,7},{6,4},{7,5},{8,10},{9,11},{10,... | collective-permute-start | bytes 196616 | tf_op jit(solution)/shard_map/ppermute | solution.py:706
  339.6 17.0 %collective-permute-start.41 = (bf16[64,512]{1,0:T(8,128)(2,1)}, bf16[64,512]{1,0:T(8,128)(2,1)S(1)}, u32[]{:S(2)}, u32[]{:S(2)}) collective-permute-start(bf16[64,512]{1,0:T(8,128)(2,1)} %get-tuple-element.335), channel_id=1, source_target_pairs={{0,1},{1,0},{2,3},{3,2},{4,5},{5,4},{6,7},{7,6},{8,9},{9,8},{10,11... | collective-permute-start | bytes 196616 | tf_op jit(solution)/shard_map/ppermute | solution.py:706
  346.4 26.1 %collective-permute-start.44 = (bf16[128,2048]{1,0:T(8,128)(2,1)S(1)}, bf16[128,2048]{1,0:T(8,128)(2,1)}, u32[]{:S(2)}, u32[]{:S(2)}) collective-permute-start(bf16[128,2048]{1,0:T(8,128)(2,1)S(1)} %pad_maximum_fusion.28), channel_id=1, source_target_pairs={{0,2},{1,3},{2,0},{3,1},{4,6},{5,7},{6,4},{7,5},{8,10},{9,11},{10,... | collective-permute-start | bytes 1572872 | tf_op jit(solution)/shard_map/ppermute | solution.py:726
  381.0 26.3 %collective-permute-start.48 = (bf16[256,2048]{1,0:T(8,128)(2,1)}, bf16[256,2048]{1,0:T(8,128)(2,1)}, u32[]{:S(2)}, u32[]{:S(2)}) collective-permute-start(bf16[256,2048]{1,0:T(8,128)(2,1)} %constant_dynamic-update-slice_fusion.22), channel_id=1, source_target_pairs={{0,1},{1,0},{2,3},{3,2},{4,5},{5,4},{6,7},{7,6},{8,9},{9,8},{10,11... | collective-permute-start | bytes 3145736 | tf_op jit(solution)/shard_map/ppermute | solution.py:736
  396.2 25.6 %collective-permute-start.47 = (bf16[512,2048]{1,0:T(8,128)(2,1)}, bf16[512,2048]{1,0:T(8,128)(2,1)}, u32[]{:S(2)}, u32[]{:S(2)}) collective-permute-start(bf16[512,2048]{1,0:T(8,128)(2,1)} %pad_maximum_fusion.9), channel_id=1, source_target_pairs={{0,4},{4,0},{1,5},{5,1},{2,6},{6,2},{3,7},{7,3},{8,12},{12,8},{9,1... | collective-permute-start | bytes 6291464 | tf_op jit(solution)/shard_map/ppermute | solution.py:40
  396.3 22.2 %collective-permute-start.50 = (bf16[128,2048]{1,0:T(8,128)(2,1)}, bf16[128,2048]{1,0:T(8,128)(2,1)S(1)}, u32[]{:S(2)}, u32[]{:S(2)}) collective-permute-start(bf16[128,2048]{1,0:T(8,128)(2,1)} %slice.861), channel_id=1, source_target_pairs={{0,1},{1,0},{2,3},{3,2},{4,5},{5,4},{6,7},{7,6},{8,9},{9,8},{10,11... | collective-permute-start | bytes 1572872 | tf_op jit(solution)/shard_map/ppermute | solution.py:73
  397.4 38.1 %collective-permute-start.52 = (bf16[128,2048]{1,0:T(8,128)(2,1)}, bf16[128,2048]{1,0:T(8,128)(2,1)}, u32[]{:S(2)}, u32[]{:S(2)}) collective-permute-start(bf16[128,2048]{1,0:T(8,128)(2,1)} %slice.860), channel_id=1, source_target_pairs={{0,1},{1,0},{2,3},{3,2},{4,5},{5,4},{6,7},{7,6},{8,9},{9,8},{10,11... | collective-permute-start | bytes 1572872 | tf_op jit(solution)/shard_map/ppermute | solution.py:73
  420.6 25.9 %collective-permute-start.51 = (bf16[64,2048]{1,0:T(8,128)(2,1)}, bf16[64,2048]{1,0:T(8,128)(2,1)S(1)}, u32[]{:S(2)}, u32[]{:S(2)}) collective-permute-start(bf16[64,2048]{1,0:T(8,128)(2,1)} %slice.869), channel_id=1, source_target_pairs={{0,2},{1,3},{2,0},{3,1},{4,6},{5,7},{6,4},{7,5},{8,10},{9,11},{10,... | collective-permute-start | bytes 786440 | tf_op jit(solution)/shard_map/ppermute | solution.py:73
  429.1 68.1 %collective-permute-start.49 = (bf16[256,2048]{1,0:T(8,128)(2,1)}, bf16[256,2048]{1,0:T(8,128)(2,1)}, u32[]{:S(2)}, u32[]{:S(2)}) collective-permute-start(bf16[256,2048]{1,0:T(8,128)(2,1)} %pad_maximum_fusion.16), channel_id=1, source_target_pairs={{0,1},{1,0},{2,3},{3,2},{4,5},{5,4},{6,7},{7,6},{8,9},{9,8},{10,11... | collective-permute-start | bytes 3145736 | tf_op jit(solution)/shard_map/ppermute | solution.py:73
  446.5 30.9 %collective-permute-start.56 = (bf16[4,512,256]{2,1,0:T(8,128)(2,1)}, bf16[4,512,256]{2,1,0:T(8,128)(2,1)S(1)}, u32[]{:S(2)}, u32[]{:S(2)}) collective-permute-start(bf16[4,512,256]{2,1,0:T(8,128)(2,1)} %get-tuple-element.191), channel_id=1, source_target_pairs={{0,4},{4,0},{1,5},{5,1},{2,6},{6,2},{3,7},{7,3},{8,12},{12,8},{9,1... | collective-permute-start | bytes 3145736 | tf_op jit(solution)/shard_map/ppermute | solution.py:40
  449.4 47.6 %collective-permute-start.55 = (bf16[64,2048]{1,0:T(8,128)(2,1)S(1)}, bf16[64,2048]{1,0:T(8,128)(2,1)S(1)}, u32[]{:S(2)}, u32[]{:S(2)}) collective-permute-start(bf16[64,2048]{1,0:T(8,128)(2,1)S(1)} %fusion.31), channel_id=1, source_target_pairs={{0,2},{1,3},{2,0},{3,1},{4,6},{5,7},{6,4},{7,5},{8,10},{9,11},{10,... | collective-permute-start | bytes 786440 | tf_op jit(solution)/shard_map/ppermute | solution.py:779
  451.1 24.9 %collective-permute-start.59 = (bf16[64,2048]{1,0:T(8,128)(2,1)S(1)}, bf16[64,2048]{1,0:T(8,128)(2,1)S(1)}, u32[]{:S(2)}, u32[]{:S(2)}) collective-permute-start(bf16[64,2048]{1,0:T(8,128)(2,1)S(1)} %copy-done.50), channel_id=1, source_target_pairs={{0,2},{1,3},{2,0},{3,1},{4,6},{5,7},{6,4},{7,5},{8,10},{9,11},{10,... | collective-permute-start | bytes 786440 | tf_op jit(solution)/shard_map/ppermute | solution.py:73
  478.7 16.5 %collective-permute-start.58 = (bf16[2,256,640]{2,1,0:T(8,128)(2,1)S(1)}, bf16[2,256,640]{2,1,0:T(8,128)(2,1)S(1)}, u32[]{:S(2)}, u32[]{:S(2)}) collective-permute-start(bf16[2,256,640]{2,1,0:T(8,128)(2,1)S(1)} %pad_maximum_fusion.24), channel_id=1, source_target_pairs={{0,16},{8,24},{16,0},{24,8},{1,17},{9,25},{17,1},{25,9},{2,18},{10... | collective-permute-start | bytes 1966088 | tf_op jit(solution)/shard_map/ppermute | solution.py:150
  482.2 37.8 %collective-permute-start.61 = (bf16[64,2048]{1,0:T(8,128)(2,1)S(1)}, bf16[64,2048]{1,0:T(8,128)(2,1)S(1)}, u32[]{:S(2)}, u32[]{:S(2)}) collective-permute-start(bf16[64,2048]{1,0:T(8,128)(2,1)S(1)} %fusion.24), channel_id=1, source_target_pairs={{0,2},{1,3},{2,0},{3,1},{4,6},{5,7},{6,4},{7,5},{8,10},{9,11},{10,... | collective-permute-start | bytes 786440 | tf_op jit(solution)/shard_map/ppermute | solution.py:781
  495.3 36.1 %collective-permute-start.67 = (bf16[256,640]{1,0:T(8,128)(2,1)S(1)}, bf16[256,640]{1,0:T(8,128)(2,1)S(1)}, u32[]{:S(2)}, u32[]{:S(2)}) collective-permute-start(bf16[256,640]{1,0:T(8,128)(2,1)S(1)} %fusion.51), channel_id=1, source_target_pairs={{0,8},{8,0},{16,24},{24,16},{1,9},{9,1},{17,25},{25,17},{2,10},{10... | collective-permute-start | bytes 983048 | tf_op jit(solution)/shard_map/ppermute | solution.py:164
  497.1 21.0 %collective-permute-start.62 = (bf16[128,2048]{1,0:T(8,128)(2,1)S(1)}, bf16[128,2048]{1,0:T(8,128)(2,1)S(1)}, u32[]{:S(2)}, u32[]{:S(2)}) collective-permute-start(bf16[128,2048]{1,0:T(8,128)(2,1)S(1)} %pad_maximum_fusion.29), channel_id=1, source_target_pairs={{0,1},{1,0},{2,3},{3,2},{4,5},{5,4},{6,7},{7,6},{8,9},{9,8},{10,11... | collective-permute-start | bytes 1572872 | tf_op jit(solution)/shard_map/ppermute | solution.py:796
  498.8 24.8 %collective-permute-start.60 = (bf16[128,2048]{1,0:T(8,128)(2,1)S(1)}, bf16[128,2048]{1,0:T(8,128)(2,1)S(1)}, u32[]{:S(2)}, u32[]{:S(2)}) collective-permute-start(bf16[128,2048]{1,0:T(8,128)(2,1)S(1)} %pad_maximum_fusion.30), channel_id=1, source_target_pairs={{0,2},{1,3},{2,0},{3,1},{4,6},{5,7},{6,4},{7,5},{8,10},{9,11},{10,... | collective-permute-start | bytes 1572872 | tf_op jit(solution)/shard_map/ppermute | solution.py:73
  500.9 25.4 %collective-permute-start.70 = (f32[2,2048]{1,0:T(2,128)S(1)}, f32[2,2048]{1,0:T(2,128)S(1)}, u32[]{:S(2)}, u32[]{:S(2)}) collective-permute-start(f32[2,2048]{1,0:T(2,128)S(1)} %fusion.69), channel_id=1, source_target_pairs={{0,8},{8,0},{16,24},{24,16},{1,9},{9,1},{17,25},{25,17},{2,10},{10... | collective-permute-start | bytes 49160 | tf_op jit(solution)/shard_map/ppermute | solution.py:220
  526.3 25.0 %collective-permute-start.64 = (bf16[128,2048]{1,0:T(8,128)(2,1)}, bf16[128,2048]{1,0:T(8,128)(2,1)}, u32[]{:S(2)}, u32[]{:S(2)}) collective-permute-start(bf16[128,2048]{1,0:T(8,128)(2,1)} %pad_maximum_fusion.31), channel_id=1, source_target_pairs={{0,1},{1,0},{2,3},{3,2},{4,5},{5,4},{6,7},{7,6},{8,9},{9,8},{10,11... | collective-permute-start | bytes 1572872 | tf_op jit(solution)/shard_map/ppermute | solution.py:801
  526.4 25.0 %collective-permute-start.63 = (bf16[128,2048]{1,0:T(8,128)(2,1)}, bf16[128,2048]{1,0:T(8,128)(2,1)}, u32[]{:S(2)}, u32[]{:S(2)}) collective-permute-start(bf16[128,2048]{1,0:T(8,128)(2,1)} %pad_maximum_fusion.32), channel_id=1, source_target_pairs={{0,2},{1,3},{2,0},{3,1},{4,6},{5,7},{6,4},{7,5},{8,10},{9,11},{10,... | collective-permute-start | bytes 1572872 | tf_op jit(solution)/shard_map/ppermute | solution.py:804
  528.6 31.4 %collective-permute-start.74 = (f32[2,2048]{1,0:T(2,128)S(1)}, f32[2,2048]{1,0:T(2,128)}, u32[]{:S(2)}, u32[]{:S(2)}) collective-permute-start(f32[2,2048]{1,0:T(2,128)S(1)} %add_add_fusion.1), channel_id=1, source_target_pairs={{0,1},{1,0},{2,3},{3,2},{4,5},{5,4},{6,7},{7,6},{8,9},{9,8},{10,11... | collective-permute-start | bytes 49160 | tf_op jit(solution)/shard_map/ppermute | solution.py:220
  531.2 28.7 %collective-permute-start.75 = (f32[2,2048]{1,0:T(2,128)S(1)}, f32[2,2048]{1,0:T(2,128)}, u32[]{:S(2)}, u32[]{:S(2)}) collective-permute-start(f32[2,2048]{1,0:T(2,128)S(1)} %add_add_fusion.1), channel_id=1, source_target_pairs={{0,2},{1,3},{2,0},{3,1},{4,6},{5,7},{6,4},{7,5},{8,10},{9,11},{10,... | collective-permute-start | bytes 49160 | tf_op jit(solution)/shard_map/ppermute | solution.py:220
  538.9 21.0 %collective-permute-start.76 = (f32[2,2048]{1,0:T(2,128)S(1)}, f32[2,2048]{1,0:T(2,128)S(1)}, u32[]{:S(2)}, u32[]{:S(2)}) collective-permute-start(f32[2,2048]{1,0:T(2,128)S(1)} %add_add_fusion.1), channel_id=1, source_target_pairs={{0,3},{1,2},{2,1},{3,0},{4,7},{5,6},{6,5},{7,4},{8,11},{9,10},{10,... | collective-permute-start | bytes 49160 | tf_op jit(solution)/shard_map/ppermute | solution.py:220
  552.5 21.4 %collective-permute-start.73 = (bf16[256,2048]{1,0:T(8,128)(2,1)S(1)}, bf16[256,2048]{1,0:T(8,128)(2,1)}, u32[]{:S(2)}, u32[]{:S(2)}) collective-permute-start(bf16[256,2048]{1,0:T(8,128)(2,1)S(1)} %pad_maximum_fusion.17), channel_id=1, source_target_pairs={{0,1},{1,0},{2,3},{3,2},{4,5},{5,4},{6,7},{7,6},{8,9},{9,8},{10,11... | collective-permute-start | bytes 3145736 | tf_op jit(solution)/shard_map/ppermute | solution.py:824
  (100 other events, 657.7 us)
Sparse Core Ops, SparseCore 0:
  29.7 70.8 all-gather.5
  103.1 89.3 all-gather.3
  194.3 55.8 all-gather.7
  296.3 51.3 reduce-scatter.3
  350.5 52.5 reduce-scatter.5
  421.9 52.0 reduce-scatter.7
